TPU v7x, 32 devices: a whole 2x2x4 slice. The times are simulated.
32 devices in a mesh: gx: 2 (over core), gy: 4 (over y, x), gz: 4 (over z).
Axes of the slice: x: 2, y: 2, z: 4, core: 2. Of those that a mesh axis runs over, the one named last changes fastest.
Arguments:
- adj_prev: float32 [16, 32, 2048], P('gx', 'gz', 'gy'), may hold values from -6 to 6
- adj_cur: float32 [16, 32, 2048], P('gx', 'gz', 'gy'), may hold values from -6 to 6
- velocity: float32 [16, 32, 2048], P('gx', 'gz', 'gy'), may hold values from 1.5 to 4.4
- fwd_accel: float32 [2, 16, 32, 2048], P(None, 'gx', 'gz', 'gy'), may hold values from -6 to 6
- residuals: float32 [2, 8192], P(None, ('gx', 'gy', 'gz')), may hold values from -6 to 6
- recv_tile: int32 [8192, 1], P(('gx', 'gy', 'gz')), may hold values from 0 to 7; in each aligned block of 256 rows (0 to 255, 256 to 511, ...) at most 64 rows name the same one
- recv_cell: int32 [8192], P(('gx', 'gy', 'gz')), may hold values from 0 to 32767
Outputs:
- adj_prev_out: float32 [16, 32, 2048], P('gx', 'gz', 'gy')
- adj_cur_out: float32 [16, 32, 2048], P('gx', 'gz', 'gy')
- gradient: float32 [16, 32, 2048], P('gx', 'gz', 'gy')
Inputs may be any that keep to these rules, and one draw needn't show every extreme that they name: `recv_tile`: of the 256 receivers held by one device, at most 64 lie in one tile, and in every draw some tile takes exactly 64 of some device's receivers. `recv_cell`: cells are numbered first lateral slowest, then depth, then second lateral.
All inputs are finite; a program needn't handle non-finite values.
Results may differ from a plain program's by a relative error of at most 0.000026.
Values sent between devices are 32-bit elements; how exact they have to be, the bound alone decides.
No kernel may reach another device: no remote copies, remote signals or barrier semaphores. Data moves between devices by JAX's collectives and lax.ppermute only.
A program may use at most 64 MiB of HBM per device.

v0:
```python
import jax
import jax.numpy as jnp
from jax import lax
from jax.sharding import PartitionSpec as P

stencil_weights = (-205.0 / 72.0, 8.0 / 5.0, -1.0 / 5.0, 8.0 / 315.0, -1.0 / 560.0)
courant_scale = 0.1


def with_halo(value, sides, width):
    for axis, dim in sides:
        size, length = (lax.axis_size(axis), value.shape[dim])
        up = [(i, (i + 1) % size) for i in range(size - 1)]
        down = [(j, i) for i, j in up]
        last = lax.slice_in_dim(value, length - width, length, axis=dim)
        first = lax.slice_in_dim(value, 0, width, axis=dim)
        before = lax.ppermute(last, axis, up)
        after = lax.ppermute(first, axis, down)
        value = jnp.concatenate([before, value, after], axis=dim)
    return value


def laplace_axes(along_x, along_z, along_y):
    size_x = along_z.shape[0]
    size_z = along_x.shape[1]
    size_y = along_x.shape[2]
    centre = along_x[4 : 4 + size_x]
    total = 3.0 * stencil_weights[0] * centre
    for offset in range(1, 5):
        factor = stencil_weights[offset]
        total = total + factor * (
            along_x[4 + offset : 4 + offset + size_x]
            + along_x[4 - offset : 4 - offset + size_x]
            + along_z[:, 4 + offset : 4 + offset + size_z]
            + along_z[:, 4 - offset : 4 - offset + size_z]
            + along_y[:, :, 4 + offset : 4 + offset + size_y]
            + along_y[:, :, 4 - offset : 4 - offset + size_y]
        )
    return total


def shards(adj_prev, adj_cur, velocity, fwd_accel, residuals, recv_tile, recv_cell):
    tiles_x = lax.axis_size("gx")
    tiles_y = lax.axis_size("gy")
    tile_count = tiles_x * tiles_y
    held_count = residuals.shape[1]
    capacity = max(2, 2 * held_count // tile_count)
    target = recv_tile[:, 0]
    one_hot = (target[:, None] == jnp.arange(tile_count, dtype=jnp.int32)[None, :]).astype(
        jnp.int32
    )
    earlier = jnp.cumsum(one_hot, axis=0) - one_hot
    ranking = jnp.sum(one_hot * earlier, axis=1)
    slot_index = target * capacity + ranking
    payload = jnp.stack([residuals[0], residuals[1], recv_cell.astype(jnp.float32)])
    outgoing = jnp.zeros((3, tile_count * capacity), jnp.float32).at[:, slot_index].set(payload)
    incoming = lax.all_to_all(outgoing, ("gx", "gy"), split_axis=1, concat_axis=1, tiled=True)
    cell_index = incoming[2].astype(jnp.int32)
    field_shape = velocity.shape
    cell_total = field_shape[0] * field_shape[1] * field_shape[2]
    source_pair = jnp.zeros((2, cell_total), jnp.float32).at[:, cell_index].add(incoming[:2])
    source_pair = source_pair.reshape((2,) + field_shape)
    speed_sq = (velocity * courant_scale) ** 2
    weight = -2.0 / (velocity * velocity * velocity)
    gradient = jnp.zeros_like(velocity)
    previous = adj_prev
    current = adj_cur
    for moment in range(2):
        padded = with_halo(current, (("gx", 0), ("gy", 2), ("gz", 1)), 4)
        along_x = padded[:, 4:-4, 4:-4]
        along_z = padded[4:-4, :, 4:-4]
        along_y = padded[4:-4, 4:-4, :]
        laplacian = laplace_axes(along_x, along_z, along_y)
        advanced = 2.0 * current - previous + speed_sq * laplacian + source_pair[moment]
        gradient = gradient + weight * fwd_accel[moment] * advanced
        previous = current
        current = advanced
    return (previous, current, gradient)


def solution(mesh):
    placed = (
        P("gx", "gz", "gy"),
        P("gx", "gz", "gy"),
        P("gx", "gz", "gy"),
        P(None, "gx", "gz", "gy"),
        P(None, ("gx", "gy", "gz")),
        P(("gx", "gy", "gz"), None),
        P(("gx", "gy", "gz")),
    )
    return jax.shard_map(
        shards,
        mesh=mesh,
        in_specs=placed,
        out_specs=(P("gx", "gz", "gy"), P("gx", "gz", "gy"), P("gx", "gz", "gy")),
        check_vma=False,
    )
```

profile of v0, /device:TPU:20, one launch (start us, length us, event | category | flops | bytes accessed | tf_op | source)
XLA Modules:
  0.0 89.5 jit_solution(12856934389075197483)
XLA Ops:
  0.6 0.7 fusion.72
  1.3 0.6 reduce-window.6
  2.1 0.8 fusion.71
  2.9 0.7 compare_select_fusion.1
  3.6 0.7 convert_element_type.25
  4.3 0.7 maximum_bitcast_fusion
  5.1 1.2 %scatter_custom_fusion = f32[3,512]{0,1:T(8,128)S(1)} fusion(s32[256]{0:T(256)S(1)} %bitcast.42, f32[256,3]{1,0:T(8,128)S(1)} %copy.16, f32[]{:T(128)} %constant.6.clone.1), kind=kCustom, calls=%fused_computation.135 | custom fusion | bytes 6148 | tf_op jit(solution)/shard_map/scatter | solution.py:56
  6.5 0.7 reshape.84
  7.2 4.2 %all-to-all-start = ((f32[8,1,192]{2,1,0:T(1,128)}), f32[8,1,192]{2,1,0:T(1,128)S(1)}, u32[]{:S(2)}, u32[]{:S(2)}) async-start(f32[8,1,192]{2,1,0:T(1,128)} %reshape.84), calls=%async_computation | async-start | bytes 16384 | tf_op jit(solution)/shard_map/all_to_all | solution.py:57
  11.4 0.9 fusion.79
  12.3 2.1 %collective-permute-start.1 = (f32[4,8,512]{2,1,0:T(8,128)S(1)}, f32[4,8,512]{2,1,0:T(8,128)S(1)}, u32[]{:S(2)}, u32[]{:S(2)}) collective-permute-start(f32[4,8,512]{2,1,0:T(8,128)S(1)} %get-tuple-element.23), channel_id=1, source_target_pairs={{0,16},{1,17},{2,18},{3,19},{4,20},{5,21},{6,22},{7,23},{8,24},{9,... | collective-permute-start | bytes 196616 | tf_op jit(solution)/shard_map/ppermute | solution.py:17
  14.3 1.3 %collective-permute-start = (f32[4,8,512]{2,1,0:T(8,128)S(1)}, f32[4,8,512]{2,1,0:T(8,128)S(1)}, u32[]{:S(2)}, u32[]{:S(2)}) collective-permute-start(f32[4,8,512]{2,1,0:T(8,128)S(1)} %get-tuple-element.22), channel_id=1, source_target_pairs={{16,0},{17,1},{18,2},{19,3},{20,4},{21,5},{22,6},{23,7},{24,8},{25... | collective-permute-start | bytes 196616 | tf_op jit(solution)/shard_map/ppermute | solution.py:18
  16.2 0.7 reduce.10
  17.0 0.9 %constant_dynamic-update-slice_fusion.1 = (f32[12,8,512]{2,1,0:T(8,128)S(1)}, f32[12,8,512]{2,1,0:T(8,128)S(1)}, f32[16,8,512]{2,1,0:T(8,128)S(1)}) fusion(f32[8,8,512]{2,1,0:T(8,128)} %param.8, f32[12,8,512]{2,1,0:T(8,128)S(1)} %get-tuple-element.26, f32[16,8,512]{2,1,0:T(8,128)S(1)} %get-tuple-element.27), kind=kLoop, calls=%fused_computation.142 | loop fusion | bytes 524288
  18.1 3.4 %collective-permute-start.2 = (f32[16,8,4]{2,1,0:T(8,128)S(1)}, f32[16,8,4]{2,1,0:T(8,128)S(1)}, u32[]{:S(2)}, u32[]{:S(2)}) collective-permute-start(f32[16,8,4]{2,1,0:T(8,128)S(1)} %get-tuple-element.16), channel_id=1, source_target_pairs={{0,4},{4,8},{8,12},{1,5},{5,9},{9,13},{2,6},{6,10},{10,14},{3,7},{... | collective-permute-start | bytes 6152 | tf_op jit(solution)/shard_map/ppermute | solution.py:17
  21.5 3.4 %collective-permute-start.3 = (f32[16,8,4]{2,1,0:T(8,128)S(1)}, f32[16,8,4]{2,1,0:T(8,128)S(1)}, u32[]{:S(2)}, u32[]{:S(2)}) collective-permute-start(f32[16,8,4]{2,1,0:T(8,128)S(1)} %get-tuple-element.15), channel_id=1, source_target_pairs={{4,0},{8,4},{12,8},{5,1},{9,5},{13,9},{6,2},{10,6},{14,10},{7,3},{... | collective-permute-start | bytes 6152 | tf_op jit(solution)/shard_map/ppermute | solution.py:18
  25.1 10.3 %scatter_custom_fusion.1 = f32[2,32768]{0,1:T(8,128)} fusion(s32[512]{0:T(512)S(1)} %bitcast.41, f32[512,2]{1,0:T(8,128)S(1)} %copy.19, f32[]{:T(128)} %constant.6.clone.1), kind=kCustom, calls=%fused_computation.4 | custom fusion | flops 1024 | bytes 262148 | tf_op jit(solution)/shard_map/scatter-add | solution.py:61
  35.7 3.5 %collective-permute-start.5 = (f32[16,4,520]{2,1,0:T(4,128)S(1)}, f32[16,4,520]{2,1,0:T(4,128)S(1)}, u32[]{:S(2)}, u32[]{:S(2)}) collective-permute-start(f32[16,4,520]{2,1,0:T(4,128)S(1)} %get-tuple-element.10), channel_id=1, source_target_pairs={{0,1},{1,2},{2,3},{4,5},{5,6},{6,7},{8,9},{9,10},{10,11},{12,13},{... | collective-permute-start | bytes 399368 | tf_op jit(solution)/shard_map/ppermute | solution.py:17
  39.3 2.5 %collective-permute-start.4 = (f32[16,4,520]{2,1,0:T(4,128)S(1)}, f32[16,4,520]{2,1,0:T(4,128)S(1)}, u32[]{:S(2)}, u32[]{:S(2)}) collective-permute-start(f32[16,4,520]{2,1,0:T(4,128)S(1)} %get-tuple-element.9), channel_id=1, source_target_pairs={{1,0},{2,1},{3,2},{5,4},{6,5},{7,6},{9,8},{10,9},{11,10},{13,12},{... | collective-permute-start | bytes 399368 | tf_op jit(solution)/shard_map/ppermute | solution.py:18
  41.7 20.2 %slice_reduce_fusion = (f32[32768]{0:T(1024)S(1)}, f32[32768]{0:T(1024)S(1)}) fusion(f32[2,32768]{0,1:T(8,128)} %scatter_custom_fusion.1), kind=kLoop, calls=%fused_computation.2 | loop fusion | bytes 524288 | tf_op jit(solution)/shard_map/slice | solution.py:74
  62.0 0.8 fusion.41
  62.8 1.3 %collective-permute-start.6 = (f32[4,8,512]{2,1,0:T(8,128)S(1)}, f32[4,8,512]{2,1,0:T(8,128)S(1)}, u32[]{:S(2)}, u32[]{:S(2)}) collective-permute-start(f32[4,8,512]{2,1,0:T(8,128)S(1)} %get-tuple-element.18), channel_id=1, source_target_pairs={{16,0},{17,1},{18,2},{19,3},{20,4},{21,5},{22,6},{23,7},{24,8},{25... | collective-permute-start | bytes 196616 | tf_op jit(solution)/shard_map/ppermute | solution.py:18
  64.1 3.0 %collective-permute-start.7 = (f32[4,8,512]{2,1,0:T(8,128)S(1)}, f32[4,8,512]{2,1,0:T(8,128)S(1)}, u32[]{:S(2)}, u32[]{:S(2)}) collective-permute-start(f32[4,8,512]{2,1,0:T(8,128)S(1)} %get-tuple-element.17), channel_id=1, source_target_pairs={{0,16},{1,17},{2,18},{3,19},{4,20},{5,21},{6,22},{7,23},{8,24},{9,... | collective-permute-start | bytes 196616 | tf_op jit(solution)/shard_map/ppermute | solution.py:17
  67.1 0.9 collective-permute-done.7
  68.1 2.1 %collective-permute-start.9 = (f32[16,8,4]{2,1,0:T(8,128)S(1)}, f32[16,8,4]{2,1,0:T(8,128)S(1)}, u32[]{:S(2)}, u32[]{:S(2)}) collective-permute-start(f32[16,8,4]{2,1,0:T(8,128)S(1)} %get-tuple-element.13), channel_id=1, source_target_pairs={{4,0},{8,4},{12,8},{5,1},{9,5},{13,9},{6,2},{10,6},{14,10},{7,3},{... | collective-permute-start | bytes 6152 | tf_op jit(solution)/shard_map/ppermute | solution.py:18
  70.1 3.8 %collective-permute-start.8 = (f32[16,8,4]{2,1,0:T(8,128)S(1)}, f32[16,8,4]{2,1,0:T(8,128)S(1)}, u32[]{:S(2)}, u32[]{:S(2)}) collective-permute-start(f32[16,8,4]{2,1,0:T(8,128)S(1)} %get-tuple-element.14), channel_id=1, source_target_pairs={{0,4},{4,8},{8,12},{1,5},{5,9},{9,13},{2,6},{6,10},{10,14},{3,7},{... | collective-permute-start | bytes 6152 | tf_op jit(solution)/shard_map/ppermute | solution.py:17
  74.3 2.9 %collective-permute-done.8 = f32[16,8,4]{2,1,0:T(8,128)S(1)} collective-permute-done((f32[16,8,4]{2,1,0:T(8,128)S(1)}, f32[16,8,4]{2,1,0:T(8,128)S(1)}, u32[]{:S(2)}, u32[]{:S(2)}) %collective-permute-start.8) | collective-permute-done | bytes 2080 | tf_op jit(solution)/shard_map/ppermute | solution.py:17
  77.4 3.5 %collective-permute-start.11 = (f32[16,4,520]{2,1,0:T(4,128)S(1)}, f32[16,4,520]{2,1,0:T(4,128)S(1)}, u32[]{:S(2)}, u32[]{:S(2)}) collective-permute-start(f32[16,4,520]{2,1,0:T(4,128)S(1)} %get-tuple-element.8), channel_id=1, source_target_pairs={{0,1},{1,2},{2,3},{4,5},{5,6},{6,7},{8,9},{9,10},{10,11},{12,13},{... | collective-permute-start | bytes 399368 | tf_op jit(solution)/shard_map/ppermute | solution.py:17
  80.9 2.3 %collective-permute-start.10 = (f32[16,4,520]{2,1,0:T(4,128)S(1)}, f32[16,4,520]{2,1,0:T(4,128)S(1)}, u32[]{:S(2)}, u32[]{:S(2)}) collective-permute-start(f32[16,4,520]{2,1,0:T(4,128)S(1)} %get-tuple-element.7), channel_id=1, source_target_pairs={{1,0},{2,1},{3,2},{5,4},{6,5},{7,6},{9,8},{10,9},{11,10},{13,12},{... | collective-permute-start | bytes 399368 | tf_op jit(solution)/shard_map/ppermute | solution.py:18
  83.5 1.2 %collective-permute-done.11 = f32[16,4,520]{2,1,0:T(4,128)S(1)} collective-permute-done((f32[16,4,520]{2,1,0:T(4,128)S(1)}, f32[16,4,520]{2,1,0:T(4,128)S(1)}, u32[]{:S(2)}, u32[]{:S(2)}) %collective-permute-start.11) | collective-permute-done | bytes 133152 | tf_op jit(solution)/shard_map/ppermute | solution.py:17
  84.6 3.5 %collective-permute-done.10 = f32[16,4,520]{2,1,0:T(4,128)S(1)} collective-permute-done((f32[16,4,520]{2,1,0:T(4,128)S(1)}, f32[16,4,520]{2,1,0:T(4,128)S(1)}, u32[]{:S(2)}, u32[]{:S(2)}) %collective-permute-start.10) | collective-permute-done | bytes 133152 | tf_op jit(solution)/shard_map/ppermute | solution.py:18
  88.1 1.4 %fusion.66 = (f32[8,8,512]{2,1,0:T(8,128)}, f32[8,8,512]{2,1,0:T(8,128)}) fusion(f32[8,8,512]{2,1,0:T(8,128)S(1)} %fusion.41, f32[8,8,512]{2,1,0:T(8,128)S(1)} %copy-done.2, f32[2,8,8,512]{3,2,1,0:T(8,128)S(1)} %copy-done.3, f32[8,8,512]{2,1,0:T(8,128)S(1)} %squeeze.15, f32[16,8,516]{2,1,0:T(8,128)S(1)} %get-tuple-element.12, ...), kind=kLoop, calls=%fused_computation.132 | loop fusion | flops 3014656 | bytes 2498560 | tf_op jit(solution)/shard_map/add | solution.py:75
  (45 shorter events, 2.7 us)
Async XLA Ops:
  7.2 8.5 %all-to-all-start = ((f32[8,1,192]{2,1,0:T(1,128)}), f32[8,1,192]{2,1,0:T(1,128)S(1)}, u32[]{:S(2)}, u32[]{:S(2)}) async-start(f32[8,1,192]{2,1,0:T(1,128)} %reshape.84), calls=%async_computation | async-start | bytes 16384 | tf_op jit(solution)/shard_map/all_to_all | solution.py:57
  12.3 4.7 %collective-permute-start.1 = (f32[4,8,512]{2,1,0:T(8,128)S(1)}, f32[4,8,512]{2,1,0:T(8,128)S(1)}, u32[]{:S(2)}, u32[]{:S(2)}) collective-permute-start(f32[4,8,512]{2,1,0:T(8,128)S(1)} %get-tuple-element.23), channel_id=1, source_target_pairs={{0,16},{1,17},{2,18},{3,19},{4,20},{5,21},{6,22},{7,23},{8,24},{9,... | collective-permute-start | bytes 196616 | tf_op jit(solution)/shard_map/ppermute | solution.py:17
  14.3 3.6 %collective-permute-start = (f32[4,8,512]{2,1,0:T(8,128)S(1)}, f32[4,8,512]{2,1,0:T(8,128)S(1)}, u32[]{:S(2)}, u32[]{:S(2)}) collective-permute-start(f32[4,8,512]{2,1,0:T(8,128)S(1)} %get-tuple-element.22), channel_id=1, source_target_pairs={{16,0},{17,1},{18,2},{19,3},{20,4},{21,5},{22,6},{23,7},{24,8},{25... | collective-permute-start | bytes 196616 | tf_op jit(solution)/shard_map/ppermute | solution.py:18
  18.1 17.3 %collective-permute-start.2 = (f32[16,8,4]{2,1,0:T(8,128)S(1)}, f32[16,8,4]{2,1,0:T(8,128)S(1)}, u32[]{:S(2)}, u32[]{:S(2)}) collective-permute-start(f32[16,8,4]{2,1,0:T(8,128)S(1)} %get-tuple-element.16), channel_id=1, source_target_pairs={{0,4},{4,8},{8,12},{1,5},{5,9},{9,13},{2,6},{6,10},{10,14},{3,7},{... | collective-permute-start | bytes 6152 | tf_op jit(solution)/shard_map/ppermute | solution.py:17
  21.5 14.0 %collective-permute-start.3 = (f32[16,8,4]{2,1,0:T(8,128)S(1)}, f32[16,8,4]{2,1,0:T(8,128)S(1)}, u32[]{:S(2)}, u32[]{:S(2)}) collective-permute-start(f32[16,8,4]{2,1,0:T(8,128)S(1)} %get-tuple-element.15), channel_id=1, source_target_pairs={{4,0},{8,4},{12,8},{5,1},{9,5},{13,9},{6,2},{10,6},{14,10},{7,3},{... | collective-permute-start | bytes 6152 | tf_op jit(solution)/shard_map/ppermute | solution.py:18
  35.7 26.3 %collective-permute-start.5 = (f32[16,4,520]{2,1,0:T(4,128)S(1)}, f32[16,4,520]{2,1,0:T(4,128)S(1)}, u32[]{:S(2)}, u32[]{:S(2)}) collective-permute-start(f32[16,4,520]{2,1,0:T(4,128)S(1)} %get-tuple-element.10), channel_id=1, source_target_pairs={{0,1},{1,2},{2,3},{4,5},{5,6},{6,7},{8,9},{9,10},{10,11},{12,13},{... | collective-permute-start | bytes 399368 | tf_op jit(solution)/shard_map/ppermute | solution.py:17
  39.2 22.7 %copy-start.1 = (f32[8,8,512]{2,1,0:T(8,128)S(1)}, f32[8,8,512]{2,1,0:T(8,128)}, u32[]{:S(2)}) copy-start(f32[8,8,512]{2,1,0:T(8,128)} %param.8) | copy-start | bytes 393220
  39.2 22.7 %copy-start.2 = (f32[8,8,512]{2,1,0:T(8,128)S(1)}, f32[8,8,512]{2,1,0:T(8,128)}, u32[]{:S(2)}) copy-start(f32[8,8,512]{2,1,0:T(8,128)} %param.9) | copy-start | bytes 393220
  39.2 22.7 %copy-start.4 = (f32[8,8,512]{2,1,0:T(8,128)S(1)}, f32[8,8,512]{2,1,0:T(8,128)}, u32[]{:S(2)}) copy-start(f32[8,8,512]{2,1,0:T(8,128)} %param.7) | copy-start | bytes 393220
  39.2 48.9 %copy-start.3 = (f32[2,8,8,512]{3,2,1,0:T(8,128)S(1)}, f32[2,8,8,512]{3,2,1,0:T(8,128)}, u32[]{:S(2)}) copy-start(f32[2,8,8,512]{3,2,1,0:T(8,128)} %param.10) | copy-start | bytes 786436
  39.3 22.7 %collective-permute-start.4 = (f32[16,4,520]{2,1,0:T(4,128)S(1)}, f32[16,4,520]{2,1,0:T(4,128)S(1)}, u32[]{:S(2)}, u32[]{:S(2)}) collective-permute-start(f32[16,4,520]{2,1,0:T(4,128)S(1)} %get-tuple-element.9), channel_id=1, source_target_pairs={{1,0},{2,1},{3,2},{5,4},{6,5},{7,6},{9,8},{10,9},{11,10},{13,12},{... | collective-permute-start | bytes 399368 | tf_op jit(solution)/shard_map/ppermute | solution.py:18
  62.7 26.8 %copy-start = (f32[8,8,512]{2,1,0:T(8,128)}, f32[8,8,512]{2,1,0:T(8,128)S(1)}, u32[]{:S(2)}) copy-start(f32[8,8,512]{2,1,0:T(8,128)S(1)} %fusion.41) | copy-start | bytes 393220
  62.8 4.3 %collective-permute-start.6 = (f32[4,8,512]{2,1,0:T(8,128)S(1)}, f32[4,8,512]{2,1,0:T(8,128)S(1)}, u32[]{:S(2)}, u32[]{:S(2)}) collective-permute-start(f32[4,8,512]{2,1,0:T(8,128)S(1)} %get-tuple-element.18), channel_id=1, source_target_pairs={{16,0},{17,1},{18,2},{19,3},{20,4},{21,5},{22,6},{23,7},{24,8},{25... | collective-permute-start | bytes 196616 | tf_op jit(solution)/shard_map/ppermute | solution.py:18
  64.1 3.9 %collective-permute-start.7 = (f32[4,8,512]{2,1,0:T(8,128)S(1)}, f32[4,8,512]{2,1,0:T(8,128)S(1)}, u32[]{:S(2)}, u32[]{:S(2)}) collective-permute-start(f32[4,8,512]{2,1,0:T(8,128)S(1)} %get-tuple-element.17), channel_id=1, source_target_pairs={{0,16},{1,17},{2,18},{3,19},{4,20},{5,21},{6,22},{7,23},{8,24},{9,... | collective-permute-start | bytes 196616 | tf_op jit(solution)/shard_map/ppermute | solution.py:17
  68.1 6.2 %collective-permute-start.9 = (f32[16,8,4]{2,1,0:T(8,128)S(1)}, f32[16,8,4]{2,1,0:T(8,128)S(1)}, u32[]{:S(2)}, u32[]{:S(2)}) collective-permute-start(f32[16,8,4]{2,1,0:T(8,128)S(1)} %get-tuple-element.13), channel_id=1, source_target_pairs={{4,0},{8,4},{12,8},{5,1},{9,5},{13,9},{6,2},{10,6},{14,10},{7,3},{... | collective-permute-start | bytes 6152 | tf_op jit(solution)/shard_map/ppermute | solution.py:18
  70.1 7.1 %collective-permute-start.8 = (f32[16,8,4]{2,1,0:T(8,128)S(1)}, f32[16,8,4]{2,1,0:T(8,128)S(1)}, u32[]{:S(2)}, u32[]{:S(2)}) collective-permute-start(f32[16,8,4]{2,1,0:T(8,128)S(1)} %get-tuple-element.14), channel_id=1, source_target_pairs={{0,4},{4,8},{8,12},{1,5},{5,9},{9,13},{2,6},{6,10},{10,14},{3,7},{... | collective-permute-start | bytes 6152 | tf_op jit(solution)/shard_map/ppermute | solution.py:17
  77.4 7.2 %collective-permute-start.11 = (f32[16,4,520]{2,1,0:T(4,128)S(1)}, f32[16,4,520]{2,1,0:T(4,128)S(1)}, u32[]{:S(2)}, u32[]{:S(2)}) collective-permute-start(f32[16,4,520]{2,1,0:T(4,128)S(1)} %get-tuple-element.8), channel_id=1, source_target_pairs={{0,1},{1,2},{2,3},{4,5},{5,6},{6,7},{8,9},{9,10},{10,11},{12,13},{... | collective-permute-start | bytes 399368 | tf_op jit(solution)/shard_map/ppermute | solution.py:17
  80.9 7.2 %collective-permute-start.10 = (f32[16,4,520]{2,1,0:T(4,128)S(1)}, f32[16,4,520]{2,1,0:T(4,128)S(1)}, u32[]{:S(2)}, u32[]{:S(2)}) collective-permute-start(f32[16,4,520]{2,1,0:T(4,128)S(1)} %get-tuple-element.7), channel_id=1, source_target_pairs={{1,0},{2,1},{3,2},{5,4},{6,5},{7,6},{9,8},{10,9},{11,10},{13,12},{... | collective-permute-start | bytes 399368 | tf_op jit(solution)/shard_map/ppermute | solution.py:18
where the time goes:
time: 90.4 us; the launch traced here: 89.5 us
  starting transfers between devices  36.3 us (40%)
  local copies, waits for them, and re-layouts  25.6 us (28%)
  other arithmetic  17.8 us (20%)
  waiting for transfers between devices  8.85 us (10%)
  between operations  0.99 us (1%)
    slice x1, local copies, waits for them, and re-layouts, shards(): source_pair[moment]  20.2 us
    ppermute x6, starting transfers between devices, with_halo(): before = lax.ppermute(last, axis, up)  19.2 us
    ppermute x6, starting transfers between devices, with_halo(): after = lax.ppermute(first, axis, down)  12.8 us
    scatter-add x1, other arithmetic, shards(): jnp.zeros((2, cell_total), jnp.float32).at[:, cell_index].add(incoming[:2])  10.3 us
    ppermute x6, waiting for transfers between devices, with_halo(): before = lax.ppermute(last, axis, up)  4.94 us
    all_to_all x1, starting transfers between devices, shards(): lax.all_to_all(outgoing, ('gx', 'gy'), split_axis=1, concat_axis=1, tiled...  4.23 us
    ppermute x6, waiting for transfers between devices, with_halo(): after = lax.ppermute(first, axis, down)  3.9 us
  transfers between devices with their start and end apart: 13, of which 5 were waited for; matrix products, arithmetic and copies ran while one was open for 38% of the time, Pallas kernels for 0%

commit v1 on v0

v1 whole, which is shorter than its diff:
```python
import functools
import jax
import jax.numpy as jnp
from jax import lax
from jax.experimental import pallas as pl
from jax.experimental.pallas import tpu as pltpu
from jax.sharding import PartitionSpec as P

stencil_weights = (-205.0 / 72.0, 8.0 / 5.0, -1.0 / 5.0, 8.0 / 315.0, -1.0 / 560.0)
courant_scale = 0.1
LANES = 128
F32 = jnp.float32
BF16 = jnp.bfloat16
VMEM = pl.BlockSpec(memory_space=pltpu.VMEM)


def pair_swaps(size, offset):
    pairs = []
    for i in range(offset, size - 1, 2):
        pairs += [(i, i + 1), (i + 1, i)]
    return pairs


def xor_swaps(size, bits):
    return [(i, i ^ bits) for i in range(size)]


def pack_kernel(cur_ref, res_ref, tile_ref, cell_ref, even_ref, odd_ref, own_ref, sem):
    blocks = cur_ref.shape[2] // LANES
    is_odd = lax.rem(lax.axis_index("gy"), 2)
    last = (blocks - 1) * LANES
    start_even = pl.multiple_of((1 - is_odd) * last, LANES)
    start_odd = pl.multiple_of(is_odd * last, LANES)
    size_x = cur_ref.shape[0]
    copies = (
        pltpu.make_async_copy(cur_ref.at[:, :, pl.ds(start_even, LANES)], even_ref.at[0:size_x], sem.at[0]),
        pltpu.make_async_copy(cur_ref.at[:, :, pl.ds(start_odd, LANES)], odd_ref.at[0:size_x], sem.at[1]),
    )
    for copy in copies:
        copy.start()
    tile = tile_ref[...].astype(F32)
    cell = cell_ref[...].astype(F32)
    rows = (
        res_ref[0:1, 0:LANES], res_ref[0:1, LANES:],
        res_ref[1:2, 0:LANES], res_ref[1:2, LANES:],
        tile[0:1], tile[1:2], cell[0:1], cell[1:2],
    )
    payload = jnp.concatenate(rows, axis=0)
    even_ref[size_x] = payload
    odd_ref[size_x] = payload
    own_ref[0] = payload
    for copy in copies:
        copy.wait()


def pack(cur, residuals, tile, cell):
    size_x, size_z, _ = cur.shape
    message = jax.ShapeDtypeStruct((size_x + 1, size_z, LANES), F32)
    return pl.pallas_call(
        pack_kernel,
        out_shape=(message, message, jax.ShapeDtypeStruct((1, 8, LANES), F32)),
        in_specs=[pl.BlockSpec(memory_space=pl.ANY), VMEM, VMEM, VMEM],
        out_specs=(VMEM, VMEM, VMEM),
        scratch_shapes=[pltpu.SemaphoreType.DMA((2,))],
        name="pack",
    )(cur, residuals, tile, cell)


def scatter_kernel(picks, shape, *refs):
    blocks, (out_ref, left_ref, right_ref) = refs[: len(picks)], refs[len(picks) :]
    size_x, size_z, size_y = shape
    rows = size_x * size_z
    mine = (lax.axis_index("gx") * lax.axis_size("gy") + lax.axis_index("gy")).astype(F32)
    row_iota = lax.broadcasted_iota(jnp.int32, (rows, LANES), 0)
    column_iota = lax.broadcasted_iota(jnp.int32, (size_y, LANES), 0)
    place = 0
    for ref, pick in zip(blocks, picks):
        block = ref[pick]
        cell = block[6:8].astype(jnp.int32)
        column = lax.rem(cell, size_y)
        row = jnp.where(block[4:6] == mine, lax.div(cell, size_y), -1)
        high = block[0:4].astype(BF16).astype(F32)
        rest = block[0:4] - high
        middle = rest.astype(BF16).astype(F32)
        low = rest - middle
        for half in range(2):
            lanes = slice(place, place + LANES)
            hit = row_iota == row[half : half + 1]
            for moment in range(2):
                line = 2 * moment + half
                for piece, value in enumerate((high, middle, low)):
                    top = (3 * moment + piece) * rows
                    left_ref[top : top + rows, lanes] = jnp.where(hit, value[line : line + 1], 0.0).astype(BF16)
            right_ref[:, lanes] = jnp.where(column_iota == column[half : half + 1], 1.0, 0.0).astype(BF16)
            place += LANES
    total = lax.dot_general(
        left_ref[...], right_ref[...], (((1,), (1,)), ((), ())), preferred_element_type=F32
    )
    for moment in range(2):
        base = 3 * moment * rows
        field = total[base : base + rows] + (total[base + rows : base + 2 * rows] + total[base + 2 * rows : base + 3 * rows])
        out_ref[moment] = field.reshape(shape)


def scatter(blocks, picks, shape):
    count = 2 * LANES * len(picks)
    rows = shape[0] * shape[1]
    return pl.pallas_call(
        functools.partial(scatter_kernel, picks, shape),
        out_shape=jax.ShapeDtypeStruct((2,) + shape, F32),
        in_specs=[VMEM] * len(blocks),
        out_specs=VMEM,
        scratch_shapes=[pltpu.VMEM((6 * rows, count), BF16), pltpu.VMEM((shape[2], count), BF16)],
        name="scatter",
    )(*blocks)


def laplacian_blocks(sizes, cur_ref, x_refs, z_refs, y_refs):
    size_x, size_z, size_y = cur_ref.shape
    places = [lax.axis_index(name) for name in ("gx", "gz", "gy")]
    count_x, count_z, count_y = sizes
    odd = [lax.rem(place, 2) == 1 for place in places]
    shape = (size_x, size_z, LANES)
    layer = lax.broadcasted_iota(jnp.int32, shape, 1)
    lane = lax.broadcasted_iota(jnp.int32, shape, 2)

    def side(parts, is_odd, before):
        first, second = (parts[0], parts[1]) if before else (parts[1], parts[0])
        return jnp.where(is_odd, first, second)

    ends = []
    for before in (True, False):
        parts = [ref[0:size_x] for ref in y_refs]
        at_edge = places[2] == (0 if before else count_y - 1)
        ends.append(jnp.where(at_edge, 0.0, side(parts, odd[2], before)))
    columns = [cur_ref[:, :, j : j + LANES] for j in range(0, size_y, LANES)]
    columns = [ends[0]] + columns + [ends[1]]
    lower = layer < 4
    from_even = jnp.logical_xor(lower, odd[1])
    for j in range(size_y // LANES):
        where = slice(j * LANES, (j + 1) * LANES)
        centre, left, right = columns[j + 1], columns[j], columns[j + 2]
        halves = []
        for before in (True, False):
            layers = slice(size_x - 4, size_x) if before else slice(0, 4)
            parts = [ref[layers, :, where] for ref in x_refs]
            if len(parts) == 1:
                parts.append(jnp.zeros_like(parts[0]))
            halves.append(side(parts, odd[0], before))
        along_x = jnp.concatenate([halves[0], centre, halves[1]], axis=0)
        beyond = jnp.where(from_even, z_refs[0][:, :, where], z_refs[1][:, :, where])
        total = (3.0 * stencil_weights[0]) * centre
        for offset in range(1, 5):
            near = along_x[4 + offset : 4 + offset + size_x] + along_x[4 - offset : 4 - offset + size_x]
            near += pltpu.roll(jnp.where(layer >= offset, centre, beyond), size_z - offset, 1)
            near += pltpu.roll(jnp.where(layer < size_z - offset, centre, beyond), offset, 1)
            near += pltpu.roll(jnp.where(lane >= offset, centre, right), LANES - offset, 2)
            near += pltpu.roll(jnp.where(lane < LANES - offset, centre, left), offset, 2)
            total += stencil_weights[offset] * near
        yield where, centre, total


def first_kernel(sizes, count_x, cur_ref, prev_ref, vel_ref, src_ref, *refs):
    x_refs, refs = refs[:count_x], refs[count_x:]
    z_refs, y_refs, (next_ref, even_ref, odd_ref) = refs[:2], refs[2:4], refs[4:]
    for where, centre, laplacian in laplacian_blocks(sizes, cur_ref, x_refs, z_refs, y_refs):
        scaled = vel_ref[:, :, where] * courant_scale
        next_ref[:, :, where] = (
            2.0 * centre - prev_ref[:, :, where] + scaled * scaled * laplacian + src_ref[0, :, :, where]
        )
    is_odd = lax.rem(lax.axis_index("gy"), 2) == 1
    first, last = next_ref[:, :, 0:LANES], next_ref[:, :, next_ref.shape[2] - LANES :]
    even_ref[...] = jnp.where(is_odd, first, last)
    odd_ref[...] = jnp.where(is_odd, last, first)


def second_kernel(sizes, count_x, cur_ref, prev_ref, vel_ref, src_ref, accel_ref, *refs):
    x_refs, refs = refs[:count_x], refs[count_x:]
    z_refs, y_refs, (next_ref, gradient_ref) = refs[:2], refs[2:4], refs[4:]
    for where, centre, laplacian in laplacian_blocks(sizes, cur_ref, x_refs, z_refs, y_refs):
        velocity = vel_ref[:, :, where]
        scaled = velocity * courant_scale
        advanced = 2.0 * centre - prev_ref[:, :, where] + scaled * scaled * laplacian + src_ref[1, :, :, where]
        next_ref[:, :, where] = advanced
        weight = -2.0 / (velocity * velocity * velocity)
        gradient_ref[:, :, where] = weight * accel_ref[0, :, :, where] * centre + weight * accel_ref[1, :, :, where] * advanced


def bucketed(residuals, target, cell, tile_count):
    held_count = residuals.shape[1]
    capacity = max(2, 2 * held_count // tile_count)
    one_hot = (target[:, None] == jnp.arange(tile_count, dtype=jnp.int32)[None, :]).astype(jnp.int32)
    earlier = jnp.cumsum(one_hot, axis=0) - one_hot
    slot_index = target * capacity + jnp.sum(one_hot * earlier, axis=1)
    payload = jnp.stack([residuals[0], residuals[1], cell.astype(F32)])
    outgoing = jnp.zeros((3, tile_count * capacity), F32).at[:, slot_index].set(payload)
    incoming = lax.all_to_all(outgoing, ("gx", "gy"), split_axis=1, concat_axis=1, tiled=True)
    block = 2 * LANES
    count = -(-incoming.shape[1] // block)
    incoming = jnp.pad(incoming, ((0, 0), (0, count * block - incoming.shape[1])))
    mine = (lax.axis_index("gx") * lax.axis_size("gy") + lax.axis_index("gy")).astype(F32)
    parts = jnp.concatenate([incoming[:2], jnp.full((1, count * block), mine), incoming[2:]])
    return parts.reshape(4, count, 2, LANES).transpose(1, 0, 2, 3).reshape(count, 8, LANES)


def shards(adj_prev, adj_cur, velocity, fwd_accel, residuals, recv_tile, recv_cell):
    count_x, count_z, count_y = sizes = tuple(lax.axis_size(name) for name in ("gx", "gz", "gy"))
    shape = velocity.shape
    target = recv_tile[:, 0]

    def halos(value):
        along_x = [lax.ppermute(value, "gx", pair_swaps(count_x, 0))]
        if count_x > 2:
            along_x.append(lax.ppermute(value, "gx", pair_swaps(count_x, 1)))
        along_z = [lax.ppermute(value, "gz", pair_swaps(count_z, offset)) for offset in range(2)]
        return along_x + along_z

    even_face, odd_face, own = pack(
        adj_cur, residuals, target.reshape(2, LANES), recv_cell.reshape(2, LANES)
    )
    if count_x == 2 and count_y == 4:
        even = lax.ppermute(even_face, "gy", xor_swaps(4, 1))
        odd = lax.ppermute(odd_face, "gy", xor_swaps(4, 3))
        far = lax.ppermute(own, "gy", xor_swaps(4, 2))
        current, even_face, odd_face, own = lax.optimization_barrier((adj_cur, even_face, odd_face, own))
        around = halos(current)
        swap = functools.partial(lax.ppermute, axis_name="gx", perm=pair_swaps(2, 0))
        same = [own, far, even, odd]
        blocks = same + [swap(block) for block in same]
        source = scatter(blocks, (0, 0, shape[0], shape[0]) * 2, shape)
    else:
        even = lax.ppermute(even_face, "gy", pair_swaps(count_y, 0))
        odd = lax.ppermute(odd_face, "gy", pair_swaps(count_y, 1))
        around = halos(adj_cur)
        parts = bucketed(residuals, target, recv_cell, count_x * count_y)
        source = scatter([parts] * parts.shape[0], tuple(range(parts.shape[0])), shape)
    xs = len(around) - 2
    field = jax.ShapeDtypeStruct(shape, F32)
    face = jax.ShapeDtypeStruct(shape[:2] + (LANES,), F32)
    advanced, even_face, odd_face = pl.pallas_call(
        functools.partial(first_kernel, sizes, xs),
        out_shape=(field, face, face),
        in_specs=[VMEM] * (6 + len(around)),
        out_specs=(VMEM, VMEM, VMEM),
        name="first_step",
    )(adj_cur, adj_prev, velocity, source, *around, even, odd)
    even = lax.ppermute(even_face, "gy", pair_swaps(count_y, 0))
    odd = lax.ppermute(odd_face, "gy", pair_swaps(count_y, 1))
    around = halos(advanced)
    latest, gradient = pl.pallas_call(
        functools.partial(second_kernel, sizes, xs),
        out_shape=(field, field),
        in_specs=[VMEM] * (7 + len(around)),
        out_specs=(VMEM, VMEM),
        name="second_step",
    )(advanced, adj_cur, velocity, source, fwd_accel, *around, even, odd)
    return advanced, latest, gradient


def solution(mesh):
    placed = (
        P("gx", "gz", "gy"),
        P("gx", "gz", "gy"),
        P("gx", "gz", "gy"),
        P(None, "gx", "gz", "gy"),
        P(None, ("gx", "gy", "gz")),
        P(("gx", "gy", "gz"), None),
        P(("gx", "gy", "gz")),
    )
    return jax.shard_map(
        shards,
        mesh=mesh,
        in_specs=placed,
        out_specs=(P("gx", "gz", "gy"), P("gx", "gz", "gy"), P("gx", "gz", "gy")),
        check_vma=False,
    )
```

time: 90.4 us -> 41.5 us (0.46)
  the two profiles are of different devices: /device:TPU:20 before, /device:TPU:4 now
where the time goes in v1:
time: 41.5 us; the launch traced here: 41.1 us
  starting transfers between devices  14.9 us (36%)
  waiting for transfers between devices  12.2 us (29%)
  Pallas kernels  9.88 us (24%)
  local copies, waits for them, and re-layouts  3.3 us (8%)
  between operations  0.81 us (2%)
    ppermute x4, starting transfers between devices, halos(): lax.ppermute(value, 'gz', pair_swaps(count_z, offset))  7.7 us
    ppermute x1, waiting for transfers between devices, shards(): odd = lax.ppermute(odd_face, 'gy', pair_swaps(count_y, 1))  3.86 us
    unnamed x34, local copies, waits for them, and re-layouts  3.3 us
    pallas_call x1, Pallas kernels, scatter(): pl.pallas_call(functools.partial(scatter_kernel, picks, shape), out_shape...  3.03 us
    ppermute x1, waiting for transfers between devices, shards(): far = lax.ppermute(own, 'gy', xor_swaps(4, 2))  2.87 us
    ppermute x1, starting transfers between devices, shards(): odd = lax.ppermute(odd_face, 'gy', pair_swaps(count_y, 1))  2.79 us
    pallas_call x1, Pallas kernels, shards(): pl.pallas_call(functools.partial(second_kernel, sizes, xs), out_shape=(fi...  2.39 us
    ppermute x1, waiting for transfers between devices, shards(): odd = lax.ppermute(odd_face, 'gy', xor_swaps(4, 3))  2.39 us
  transfers between devices with their start and end apart: 15, of which 6 were waited for; matrix products, arithmetic and copies ran while one was open for 0% of the time, Pallas kernels for 7%

profile of v1, /device:TPU:4, one launch (start us, length us, event | category | flops | bytes accessed | tf_op | source)
XLA Modules:
  0.0 41.1 jit_solution(12043202449234201472)
XLA Ops:
  0.6 0.0 copy-start
  0.6 2.2 %pack.1 = (f32[9,8,128]{2,1,0:T(8,128)}, f32[9,8,128]{2,1,0:T(8,128)}, f32[1,8,128]{2,1,0:T(8,128)}) custom-call(f32[8,8,512]{2,1,0:T(8,128)} %prev_ref.3, f32[2,256]{1,0:T(2,128)} %res_ref.1, s32[2,128]{1,0:T(2,128)} %bitcast.2, s32[2,128]{1,0:T(2,128)} %bitcast.3), custom_call_target="tpu_custom_call" | custom-call | tf_op jit(solution)/shard_map/pack/pallas_call | solution.py:59
  2.8 0.0 copy-start.13
  2.8 0.7 %collective-permute-start.9 = (f32[8,8,512]{2,1,0:T(8,128)S(1)}, f32[8,8,512]{2,1,0:T(8,128)S(1)}, u32[]{:S(2)}, u32[]{:S(2)}) collective-permute-start(f32[8,8,512]{2,1,0:T(8,128)S(1)} %copy-done), channel_id=1, source_target_pairs={{1,2},{2,1},{5,6},{6,5},{9,10},{10,9},{13,14},{14,13},{17,18},{18,... | collective-permute-start | bytes 393224 | tf_op jit(solution)/shard_map/ppermute | solution.py:215
  3.5 4.5 %collective-permute-start.8 = (f32[8,8,512]{2,1,0:T(8,128)S(1)}, f32[8,8,512]{2,1,0:T(8,128)S(1)}, u32[]{:S(2)}, u32[]{:S(2)}) collective-permute-start(f32[8,8,512]{2,1,0:T(8,128)S(1)} %copy-done), channel_id=1, source_target_pairs={{0,1},{1,0},{2,3},{3,2},{4,5},{5,4},{6,7},{7,6},{8,9},{9,8},{10,11... | collective-permute-start | bytes 393224 | tf_op jit(solution)/shard_map/ppermute | solution.py:215
  8.0 0.5 %collective-permute-start = (f32[1,8,128]{2,1,0:T(8,128)S(1)}, f32[1,8,128]{2,1,0:T(8,128)S(1)}, u32[]{:S(2)}, u32[]{:S(2)}) collective-permute-start(f32[1,8,128]{2,1,0:T(8,128)S(1)} %copy-done.13), channel_id=1, source_target_pairs={{0,8},{4,12},{8,0},{12,4},{1,9},{5,13},{9,1},{13,5},{2,10},{6,14},... | collective-permute-start | bytes 12296 | tf_op jit(solution)/shard_map/ppermute | solution.py:224
  8.5 0.2 collective-permute-start.3
  8.7 2.9 %collective-permute-done.refs_1_ = f32[1,8,128]{2,1,0:T(8,128)S(1)} collective-permute-done((f32[1,8,128]{2,1,0:T(8,128)S(1)}, f32[1,8,128]{2,1,0:T(8,128)S(1)}, u32[]{:S(2)}, u32[]{:S(2)}) %collective-permute-start) | collective-permute-done | bytes 4128 | tf_op jit(solution)/shard_map/ppermute | solution.py:224
  11.6 1.6 %collective-permute-start.1 = (f32[9,8,128]{2,1,0:T(8,128)}, f32[9,8,128]{2,1,0:T(8,128)S(1)}, u32[]{:S(2)}, u32[]{:S(2)}) collective-permute-start(f32[9,8,128]{2,1,0:T(8,128)} %get-tuple-element.13), channel_id=1, source_target_pairs={{0,4},{4,0},{8,12},{12,8},{1,5},{5,1},{9,13},{13,9},{2,6},{6,2},{1... | collective-permute-start | bytes 110600 | tf_op jit(solution)/shard_map/ppermute | solution.py:222
  13.2 1.0 %collective-permute-start.2 = (f32[9,8,128]{2,1,0:T(8,128)}, f32[9,8,128]{2,1,0:T(8,128)S(1)}, u32[]{:S(2)}, u32[]{:S(2)}) collective-permute-start(f32[9,8,128]{2,1,0:T(8,128)} %get-tuple-element.14), channel_id=1, source_target_pairs={{0,12},{4,8},{8,4},{12,0},{1,13},{5,9},{9,5},{13,1},{2,14},{6,10},... | collective-permute-start | bytes 110600 | tf_op jit(solution)/shard_map/ppermute | solution.py:223
  14.2 1.6 %collective-permute-done.1.refs_2_.refs_3_ = f32[9,8,128]{2,1,0:T(8,128)S(1)} collective-permute-done((f32[9,8,128]{2,1,0:T(8,128)}, f32[9,8,128]{2,1,0:T(8,128)S(1)}, u32[]{:S(2)}, u32[]{:S(2)}) %collective-permute-start.1) | collective-permute-done | bytes 36896 | tf_op jit(solution)/shard_map/ppermute | solution.py:222
  15.9 2.4 %collective-permute-done.2.refs_3_.refs_4_ = f32[9,8,128]{2,1,0:T(8,128)S(1)} collective-permute-done((f32[9,8,128]{2,1,0:T(8,128)}, f32[9,8,128]{2,1,0:T(8,128)S(1)}, u32[]{:S(2)}, u32[]{:S(2)}) %collective-permute-start.2) | collective-permute-done | bytes 36896 | tf_op jit(solution)/shard_map/ppermute | solution.py:223
  18.3 0.0 copy-start.9
  18.3 1.2 %collective-permute-done.6.refs_7_ = f32[9,8,128]{2,1,0:T(8,128)S(1)} collective-permute-done((f32[9,8,128]{2,1,0:T(8,128)S(1)}, f32[9,8,128]{2,1,0:T(8,128)S(1)}, u32[]{:S(2)}, u32[]{:S(2)}) %collective-permute-start.6) | collective-permute-done | bytes 36896 | tf_op jit(solution)/shard_map/ppermute | solution.py:229
  19.5 0.0 copy-start.10
  19.5 0.6 %copy-done.10 = f32[9,8,128]{2,1,0:T(8,128)} copy-done((f32[9,8,128]{2,1,0:T(8,128)}, f32[9,8,128]{2,1,0:T(8,128)S(1)}, u32[]{:S(2)}) %copy-start.10) | copy-done | bytes 36888
  20.1 3.0 %scatter.1.src_ref = f32[2,8,8,512]{3,2,1,0:T(8,128)} custom-call(f32[1,8,128]{2,1,0:T(8,128)} %get-tuple-element.16.refs_0_, f32[1,8,128]{2,1,0:T(8,128)} %copy-done.14, f32[9,8,128]{2,1,0:T(8,128)} %copy-done.1, f32[9,8,128]{2,1,0:T(8,128)} %copy-done.2, f32[1,8,128]{2,1,0:T(8,128)} %copy-done.15, f32[1,8,128]{2,1,0:T(8,128)} %copy-done.16, ...), custom_call_target="tpu_custom_call" | custom-call | tf_op jit(solution)/shard_map/scatter/pallas_call | solution.py:108
  23.2 0.6 %copy-done.3 = f32[8,8,512]{2,1,0:T(8,128)} copy-done((f32[8,8,512]{2,1,0:T(8,128)}, f32[8,8,512]{2,1,0:T(8,128)S(1)}, u32[]{:S(2)}) %copy-start.3) | copy-done | bytes 131096
  23.8 0.1 copy-done.4
  23.9 0.7 %copy-done.5 = f32[8,8,512]{2,1,0:T(8,128)} copy-done((f32[8,8,512]{2,1,0:T(8,128)}, f32[8,8,512]{2,1,0:T(8,128)S(1)}, u32[]{:S(2)}) %copy-start.5) | copy-done | bytes 131096
  24.5 2.3 %first_step.1 = (f32[8,8,512]{2,1,0:T(8,128)}, f32[8,8,128]{2,1,0:T(8,128)}, f32[8,8,128]{2,1,0:T(8,128)}) custom-call(f32[8,8,512]{2,1,0:T(8,128)} %prev_ref.3, f32[8,8,512]{2,1,0:T(8,128)} %prev_ref.2, f32[8,8,512]{2,1,0:T(8,128)} %vel_ref.3, f32[2,8,8,512]{3,2,1,0:T(8,128)} %scatter.1.src_ref, f32[8,8,512]{2,1,0:T(8,128)} %copy-done.5, ...), custom_call_target="tpu_custom_call" | custom-call | tf_op jit(solution)/shard_map/first_step/pallas_call | solution.py:240
  26.8 0.7 %collective-permute-start.12 = (f32[8,8,512]{2,1,0:T(8,128)}, f32[8,8,512]{2,1,0:T(8,128)S(1)}, u32[]{:S(2)}, u32[]{:S(2)}) collective-permute-start(f32[8,8,512]{2,1,0:T(8,128)} %get-tuple-element.10.cur_ref), channel_id=1, source_target_pairs={{1,2},{2,1},{5,6},{6,5},{9,10},{10,9},{13,14},{14,13},{17,18},{18,... | collective-permute-start | bytes 393224 | tf_op jit(solution)/shard_map/ppermute | solution.py:215
  27.5 1.9 %collective-permute-start.11 = (f32[8,8,512]{2,1,0:T(8,128)}, f32[8,8,512]{2,1,0:T(8,128)S(1)}, u32[]{:S(2)}, u32[]{:S(2)}) collective-permute-start(f32[8,8,512]{2,1,0:T(8,128)} %get-tuple-element.10.cur_ref), channel_id=1, source_target_pairs={{0,1},{1,0},{2,3},{3,2},{4,5},{5,4},{6,7},{7,6},{8,9},{9,8},{10,11... | collective-permute-start | bytes 393224 | tf_op jit(solution)/shard_map/ppermute | solution.py:215
  29.4 1.1 %collective-permute-start.13 = (f32[8,8,128]{2,1,0:T(8,128)}, f32[8,8,128]{2,1,0:T(8,128)S(1)}, u32[]{:S(2)}, u32[]{:S(2)}) collective-permute-start(f32[8,8,128]{2,1,0:T(8,128)} %get-tuple-element.19), channel_id=1, source_target_pairs={{0,4},{4,0},{8,12},{12,8},{1,5},{5,1},{9,13},{13,9},{2,6},{6,2},{1... | collective-permute-start | bytes 98312 | tf_op jit(solution)/shard_map/ppermute | solution.py:247
  30.5 2.8 %collective-permute-start.14 = (f32[8,8,128]{2,1,0:T(8,128)}, f32[8,8,128]{2,1,0:T(8,128)S(1)}, u32[]{:S(2)}, u32[]{:S(2)}) collective-permute-start(f32[8,8,128]{2,1,0:T(8,128)} %get-tuple-element.20), channel_id=1, source_target_pairs={{4,8},{8,4},{5,9},{9,5},{6,10},{10,6},{7,11},{11,7},{20,24},{24,20... | collective-permute-start | bytes 98312 | tf_op jit(solution)/shard_map/ppermute | solution.py:248
  33.3 0.3 collective-permute-done.13.refs_3_
  33.5 3.9 %collective-permute-done.14.refs_4_ = f32[8,8,128]{2,1,0:T(8,128)S(1)} collective-permute-done((f32[8,8,128]{2,1,0:T(8,128)}, f32[8,8,128]{2,1,0:T(8,128)S(1)}, u32[]{:S(2)}, u32[]{:S(2)}) %collective-permute-start.14) | collective-permute-done | bytes 32800 | tf_op jit(solution)/shard_map/ppermute | solution.py:248
  37.4 0.6 %copy-done.12 = f32[8,8,128]{2,1,0:T(8,128)} copy-done((f32[8,8,128]{2,1,0:T(8,128)}, f32[8,8,128]{2,1,0:T(8,128)S(1)}, u32[]{:S(2)}) %copy-start.12) | copy-done | bytes 32792
  38.0 0.0 copy-done.6
  38.0 0.1 copy-done.7
  38.1 0.6 %copy-done.8 = f32[8,8,512]{2,1,0:T(8,128)} copy-done((f32[8,8,512]{2,1,0:T(8,128)}, f32[8,8,512]{2,1,0:T(8,128)S(1)}, u32[]{:S(2)}) %copy-start.8) | copy-done | bytes 131096
  38.7 2.4 %second_step.1 = (f32[8,8,512]{2,1,0:T(8,128)}, f32[8,8,512]{2,1,0:T(8,128)}) custom-call(f32[8,8,512]{2,1,0:T(8,128)} %get-tuple-element.10.cur_ref, f32[8,8,512]{2,1,0:T(8,128)} %prev_ref.3, f32[8,8,512]{2,1,0:T(8,128)} %vel_ref.3, f32[2,8,8,512]{3,2,1,0:T(8,128)} %scatter.1.src_ref, f32[2,8,8,512]{3,2,1,0:T(8,128)} %accel_ref.1, f32[8,8,512]{2,1,0:T(8,128)} %copy-done.8, ...), custom_call_target="tpu_custom_call" | custom-call | tf_op jit(solution)/shard_map/second_step/pallas_call | solution.py:250
  (36 shorter events, 0.1 us)
Async XLA Ops:
  0.6 2.2 %copy-start = (f32[8,8,512]{2,1,0:T(8,128)S(1)}, f32[8,8,512]{2,1,0:T(8,128)}, u32[]{:S(2)}) copy-start(f32[8,8,512]{2,1,0:T(8,128)} %prev_ref.3) | copy-start | bytes 393220
  2.8 5.2 %copy-start.13 = (f32[1,8,128]{2,1,0:T(8,128)S(1)}, f32[1,8,128]{2,1,0:T(8,128)}, u32[]{:S(2)}) copy-start(f32[1,8,128]{2,1,0:T(8,128)} %get-tuple-element.16.refs_0_) | copy-start | bytes 12292
  2.8 20.3 %collective-permute-start.9 = (f32[8,8,512]{2,1,0:T(8,128)S(1)}, f32[8,8,512]{2,1,0:T(8,128)S(1)}, u32[]{:S(2)}, u32[]{:S(2)}) collective-permute-start(f32[8,8,512]{2,1,0:T(8,128)S(1)} %copy-done), channel_id=1, source_target_pairs={{1,2},{2,1},{5,6},{6,5},{9,10},{10,9},{13,14},{14,13},{17,18},{18,... | collective-permute-start | bytes 393224 | tf_op jit(solution)/shard_map/ppermute | solution.py:215
  3.5 19.6 %collective-permute-start.8 = (f32[8,8,512]{2,1,0:T(8,128)S(1)}, f32[8,8,512]{2,1,0:T(8,128)S(1)}, u32[]{:S(2)}, u32[]{:S(2)}) collective-permute-start(f32[8,8,512]{2,1,0:T(8,128)S(1)} %copy-done), channel_id=1, source_target_pairs={{0,1},{1,0},{2,3},{3,2},{4,5},{5,4},{6,7},{7,6},{8,9},{9,8},{10,11... | collective-permute-start | bytes 393224 | tf_op jit(solution)/shard_map/ppermute | solution.py:215
  8.0 15.2 %collective-permute-start.7 = (f32[8,8,512]{2,1,0:T(8,128)S(1)}, f32[8,8,512]{2,1,0:T(8,128)S(1)}, u32[]{:S(2)}, u32[]{:S(2)}) collective-permute-start(f32[8,8,512]{2,1,0:T(8,128)S(1)} %copy-done), channel_id=1, source_target_pairs={{0,16},{16,0},{1,17},{17,1},{2,18},{18,2},{3,19},{19,3},{4,20},{20... | collective-permute-start | bytes 393224 | tf_op jit(solution)/shard_map/ppermute | solution.py:212
  8.0 3.6 %collective-permute-start = (f32[1,8,128]{2,1,0:T(8,128)S(1)}, f32[1,8,128]{2,1,0:T(8,128)S(1)}, u32[]{:S(2)}, u32[]{:S(2)}) collective-permute-start(f32[1,8,128]{2,1,0:T(8,128)S(1)} %copy-done.13), channel_id=1, source_target_pairs={{0,8},{4,12},{8,0},{12,4},{1,9},{5,13},{9,1},{13,5},{2,10},{6,14},... | collective-permute-start | bytes 12296 | tf_op jit(solution)/shard_map/ppermute | solution.py:224
  8.5 3.1 %collective-permute-start.3 = (f32[1,8,128]{2,1,0:T(8,128)S(1)}, f32[1,8,128]{2,1,0:T(8,128)S(1)}, u32[]{:S(2)}, u32[]{:S(2)}) collective-permute-start(f32[1,8,128]{2,1,0:T(8,128)S(1)} %copy-done.13), channel_id=1, source_target_pairs={{0,16},{16,0},{1,17},{17,1},{2,18},{18,2},{3,19},{19,3},{4,20},{20... | collective-permute-start | bytes 12296 | tf_op jit(solution)/shard_map/ppermute | solution.py:229
  11.6 7.9 %copy-start.14 = (f32[1,8,128]{2,1,0:T(8,128)}, f32[1,8,128]{2,1,0:T(8,128)S(1)}, u32[]{:S(2)}) copy-start(f32[1,8,128]{2,1,0:T(8,128)S(1)} %collective-permute-done.refs_1_) | copy-start | bytes 12292
  11.6 1.6 %collective-permute-start.4 = (f32[1,8,128]{2,1,0:T(8,128)S(1)}, f32[1,8,128]{2,1,0:T(8,128)S(1)}, u32[]{:S(2)}, u32[]{:S(2)}) collective-permute-start(f32[1,8,128]{2,1,0:T(8,128)S(1)} %collective-permute-done.refs_1_), channel_id=1, source_target_pairs={{0,16},{16,0},{1,17},{17,1},{2,18},{18,2},{3,19},{19,3},{4,20},{20... | collective-permute-start | bytes 12296 | tf_op jit(solution)/shard_map/ppermute | solution.py:229
  11.6 7.9 %copy-start.15 = (f32[1,8,128]{2,1,0:T(8,128)}, f32[1,8,128]{2,1,0:T(8,128)S(1)}, u32[]{:S(2)}) copy-start(f32[1,8,128]{2,1,0:T(8,128)S(1)} %collective-permute-done.3.refs_4_) | copy-start | bytes 12292
  11.6 4.2 %collective-permute-start.1 = (f32[9,8,128]{2,1,0:T(8,128)}, f32[9,8,128]{2,1,0:T(8,128)S(1)}, u32[]{:S(2)}, u32[]{:S(2)}) collective-permute-start(f32[9,8,128]{2,1,0:T(8,128)} %get-tuple-element.13), channel_id=1, source_target_pairs={{0,4},{4,0},{8,12},{12,8},{1,5},{5,1},{9,13},{13,9},{2,6},{6,2},{1... | collective-permute-start | bytes 110600 | tf_op jit(solution)/shard_map/ppermute | solution.py:222
  13.2 6.3 %copy-start.16 = (f32[1,8,128]{2,1,0:T(8,128)}, f32[1,8,128]{2,1,0:T(8,128)S(1)}, u32[]{:S(2)}) copy-start(f32[1,8,128]{2,1,0:T(8,128)S(1)} %collective-permute-done.4.refs_5_) | copy-start | bytes 12292
  13.2 5.1 %collective-permute-start.2 = (f32[9,8,128]{2,1,0:T(8,128)}, f32[9,8,128]{2,1,0:T(8,128)S(1)}, u32[]{:S(2)}, u32[]{:S(2)}) collective-permute-start(f32[9,8,128]{2,1,0:T(8,128)} %get-tuple-element.14), channel_id=1, source_target_pairs={{0,12},{4,8},{8,4},{12,0},{1,13},{5,9},{9,5},{13,1},{2,14},{6,10},... | collective-permute-start | bytes 110600 | tf_op jit(solution)/shard_map/ppermute | solution.py:223
  15.8 3.6 %copy-start.1 = (f32[9,8,128]{2,1,0:T(8,128)}, f32[9,8,128]{2,1,0:T(8,128)S(1)}, u32[]{:S(2)}) copy-start(f32[9,8,128]{2,1,0:T(8,128)S(1)} %collective-permute-done.1.refs_2_.refs_3_) | copy-start | bytes 110596
  15.9 2.4 %collective-permute-start.5 = (f32[9,8,128]{2,1,0:T(8,128)S(1)}, f32[9,8,128]{2,1,0:T(8,128)S(1)}, u32[]{:S(2)}, u32[]{:S(2)}) collective-permute-start(f32[9,8,128]{2,1,0:T(8,128)S(1)} %collective-permute-done.1.refs_2_.refs_3_), channel_id=1, source_target_pairs={{0,16},{16,0},{1,17},{17,1},{2,18},{18,2},{3,19},{19,3},{4,20},{20... | collective-permute-start | bytes 110600 | tf_op jit(solution)/shard_map/ppermute | solution.py:229
  18.2 1.2 %copy-start.2 = (f32[9,8,128]{2,1,0:T(8,128)}, f32[9,8,128]{2,1,0:T(8,128)S(1)}, u32[]{:S(2)}) copy-start(f32[9,8,128]{2,1,0:T(8,128)S(1)} %collective-permute-done.2.refs_3_.refs_4_) | copy-start | bytes 110596
  18.2 1.2 %collective-permute-start.6 = (f32[9,8,128]{2,1,0:T(8,128)S(1)}, f32[9,8,128]{2,1,0:T(8,128)S(1)}, u32[]{:S(2)}, u32[]{:S(2)}) collective-permute-start(f32[9,8,128]{2,1,0:T(8,128)S(1)} %collective-permute-done.2.refs_3_.refs_4_), channel_id=1, source_target_pairs={{0,16},{16,0},{1,17},{17,1},{2,18},{18,2},{3,19},{19,3},{4,20},{20... | collective-permute-start | bytes 110600 | tf_op jit(solution)/shard_map/ppermute | solution.py:229
  18.3 1.2 %copy-start.9 = (f32[9,8,128]{2,1,0:T(8,128)}, f32[9,8,128]{2,1,0:T(8,128)S(1)}, u32[]{:S(2)}) copy-start(f32[9,8,128]{2,1,0:T(8,128)S(1)} %collective-permute-done.5.refs_6_) | copy-start | bytes 110596
  19.5 0.6 %copy-start.10 = (f32[9,8,128]{2,1,0:T(8,128)}, f32[9,8,128]{2,1,0:T(8,128)S(1)}, u32[]{:S(2)}) copy-start(f32[9,8,128]{2,1,0:T(8,128)S(1)} %collective-permute-done.6.refs_7_) | copy-start | bytes 110596
  23.2 0.6 %copy-start.3 = (f32[8,8,512]{2,1,0:T(8,128)}, f32[8,8,512]{2,1,0:T(8,128)S(1)}, u32[]{:S(2)}) copy-start(f32[8,8,512]{2,1,0:T(8,128)S(1)} %collective-permute-done.9.refs_2_) | copy-start | bytes 393220
  23.2 0.7 %copy-start.4 = (f32[8,8,512]{2,1,0:T(8,128)}, f32[8,8,512]{2,1,0:T(8,128)S(1)}, u32[]{:S(2)}) copy-start(f32[8,8,512]{2,1,0:T(8,128)S(1)} %collective-permute-done.8.refs_1_) | copy-start | bytes 393220
  23.9 0.7 %copy-start.5 = (f32[8,8,512]{2,1,0:T(8,128)}, f32[8,8,512]{2,1,0:T(8,128)S(1)}, u32[]{:S(2)}) copy-start(f32[8,8,512]{2,1,0:T(8,128)S(1)} %collective-permute-done.7.refs_0_) | copy-start | bytes 393220
  26.8 10.6 %collective-permute-start.12 = (f32[8,8,512]{2,1,0:T(8,128)}, f32[8,8,512]{2,1,0:T(8,128)S(1)}, u32[]{:S(2)}, u32[]{:S(2)}) collective-permute-start(f32[8,8,512]{2,1,0:T(8,128)} %get-tuple-element.10.cur_ref), channel_id=1, source_target_pairs={{1,2},{2,1},{5,6},{6,5},{9,10},{10,9},{13,14},{14,13},{17,18},{18,... | collective-permute-start | bytes 393224 | tf_op jit(solution)/shard_map/ppermute | solution.py:215
  27.5 9.9 %collective-permute-start.11 = (f32[8,8,512]{2,1,0:T(8,128)}, f32[8,8,512]{2,1,0:T(8,128)S(1)}, u32[]{:S(2)}, u32[]{:S(2)}) collective-permute-start(f32[8,8,512]{2,1,0:T(8,128)} %get-tuple-element.10.cur_ref), channel_id=1, source_target_pairs={{0,1},{1,0},{2,3},{3,2},{4,5},{5,4},{6,7},{7,6},{8,9},{9,8},{10,11... | collective-permute-start | bytes 393224 | tf_op jit(solution)/shard_map/ppermute | solution.py:215
  29.4 8.0 %collective-permute-start.10 = (f32[8,8,512]{2,1,0:T(8,128)}, f32[8,8,512]{2,1,0:T(8,128)S(1)}, u32[]{:S(2)}, u32[]{:S(2)}) collective-permute-start(f32[8,8,512]{2,1,0:T(8,128)} %get-tuple-element.10.cur_ref), channel_id=1, source_target_pairs={{0,16},{16,0},{1,17},{17,1},{2,18},{18,2},{3,19},{19,3},{4,20},{20... | collective-permute-start | bytes 393224 | tf_op jit(solution)/shard_map/ppermute | solution.py:212
  29.4 4.1 %collective-permute-start.13 = (f32[8,8,128]{2,1,0:T(8,128)}, f32[8,8,128]{2,1,0:T(8,128)S(1)}, u32[]{:S(2)}, u32[]{:S(2)}) collective-permute-start(f32[8,8,128]{2,1,0:T(8,128)} %get-tuple-element.19), channel_id=1, source_target_pairs={{0,4},{4,0},{8,12},{12,8},{1,5},{5,1},{9,13},{13,9},{2,6},{6,2},{1... | collective-permute-start | bytes 98312 | tf_op jit(solution)/shard_map/ppermute | solution.py:247
  30.5 6.9 %collective-permute-start.14 = (f32[8,8,128]{2,1,0:T(8,128)}, f32[8,8,128]{2,1,0:T(8,128)S(1)}, u32[]{:S(2)}, u32[]{:S(2)}) collective-permute-start(f32[8,8,128]{2,1,0:T(8,128)} %get-tuple-element.20), channel_id=1, source_target_pairs={{4,8},{8,4},{5,9},{9,5},{6,10},{10,6},{7,11},{11,7},{20,24},{24,20... | collective-permute-start | bytes 98312 | tf_op jit(solution)/shard_map/ppermute | solution.py:248
  33.5 3.9 %copy-start.11 = (f32[8,8,128]{2,1,0:T(8,128)}, f32[8,8,128]{2,1,0:T(8,128)S(1)}, u32[]{:S(2)}) copy-start(f32[8,8,128]{2,1,0:T(8,128)S(1)} %collective-permute-done.13.refs_3_) | copy-start | bytes 98308
  37.4 0.6 %copy-start.12 = (f32[8,8,128]{2,1,0:T(8,128)}, f32[8,8,128]{2,1,0:T(8,128)S(1)}, u32[]{:S(2)}) copy-start(f32[8,8,128]{2,1,0:T(8,128)S(1)} %collective-permute-done.14.refs_4_) | copy-start | bytes 98308
  37.4 0.7 %copy-start.6 = (f32[8,8,512]{2,1,0:T(8,128)}, f32[8,8,512]{2,1,0:T(8,128)S(1)}, u32[]{:S(2)}) copy-start(f32[8,8,512]{2,1,0:T(8,128)S(1)} %collective-permute-done.12.refs_2_) | copy-start | bytes 393220
  37.4 0.7 %copy-start.7 = (f32[8,8,512]{2,1,0:T(8,128)}, f32[8,8,512]{2,1,0:T(8,128)S(1)}, u32[]{:S(2)}) copy-start(f32[8,8,512]{2,1,0:T(8,128)S(1)} %collective-permute-done.11.refs_1_) | copy-start | bytes 393220
  38.1 0.6 %copy-start.8 = (f32[8,8,512]{2,1,0:T(8,128)}, f32[8,8,512]{2,1,0:T(8,128)S(1)}, u32[]{:S(2)}) copy-start(f32[8,8,512]{2,1,0:T(8,128)S(1)} %collective-permute-done.10.refs_0_) | copy-start | bytes 393220

commit v2 on v1

v2 whole, which is shorter than its diff:
```python
import functools
import jax
import jax.numpy as jnp
from jax import lax
from jax.experimental import pallas as pl
from jax.experimental.pallas import tpu as pltpu
from jax.sharding import PartitionSpec as P

stencil_weights = (-205.0 / 72.0, 8.0 / 5.0, -1.0 / 5.0, 8.0 / 315.0, -1.0 / 560.0)
courant_scale = 0.1
LANES = 128
F32 = jnp.float32
BF16 = jnp.bfloat16
VMEM = pl.BlockSpec(memory_space=pltpu.VMEM)
HBM = pl.BlockSpec(memory_space=pltpu.HBM)


def near(values):
    return [pltpu.with_memory_space_constraint(value, pltpu.VMEM) for value in values]


def pair_swaps(size, offset):
    pairs = []
    for i in range(offset, size - 1, 2):
        pairs += [(i, i + 1), (i + 1, i)]
    return pairs


def full_swaps(count_x, size, offset):
    pairs = pair_swaps(size, offset)
    partner = dict(pairs)
    places = [(x, i) for x in range(count_x) for i in range(size)]
    return [
        (x * size + i, x * size + partner[i] if i in partner else (x ^ 1) * size + i) for x, i in places
    ]


def xor_swaps(size, bits):
    return [(i, i ^ bits) for i in range(size)]


def pack_kernel(cur_ref, res_ref, tile_ref, cell_ref, even_ref, odd_ref, own_ref, copy_ref, res, tile, cell, sem):
    is_odd = lax.rem(lax.axis_index("gy"), 2)
    last = cur_ref.shape[2] - LANES
    start_even = pl.multiple_of((1 - is_odd) * last, LANES)
    start_odd = pl.multiple_of(is_odd * last, LANES)
    size_x = cur_ref.shape[0]
    pairs = (
        (res_ref, res),
        (tile_ref, tile),
        (cell_ref, cell),
        (cur_ref.at[:, :, pl.ds(start_even, LANES)], even_ref.at[0:size_x]),
        (cur_ref.at[:, :, pl.ds(start_odd, LANES)], odd_ref.at[0:size_x]),
        (cur_ref, copy_ref),
    )
    copies = [pltpu.make_async_copy(*pair, sem.at[i]) for i, pair in enumerate(pairs)]
    for copy in copies:
        copy.start()
    for copy in copies[:3]:
        copy.wait()
    rows = (
        res[0:1, 0:LANES], res[0:1, LANES:], res[1:2, 0:LANES], res[1:2, LANES:],
        tile[...].astype(F32), cell[...].astype(F32),
    )
    payload = jnp.concatenate(rows, axis=0)
    even_ref[size_x] = payload
    odd_ref[size_x] = payload
    own_ref[0] = payload
    for copy in copies[3:]:
        copy.wait()


def pack(cur, residuals, tile, cell):
    size_x, size_z, _ = cur.shape
    message = pltpu.VMEM((size_x + 1, size_z, LANES), F32)
    return pl.pallas_call(
        pack_kernel,
        out_shape=(message, message, pltpu.VMEM((1, 8, LANES), F32), pltpu.VMEM(cur.shape, F32)),
        in_specs=[pl.BlockSpec(memory_space=pl.ANY)] * 4,
        out_specs=(VMEM,) * 4,
        scratch_shapes=[
            pltpu.VMEM(residuals.shape, F32),
            pltpu.VMEM(tile.shape, jnp.int32),
            pltpu.VMEM(cell.shape, jnp.int32),
            pltpu.SemaphoreType.DMA((6,)),
        ],
        name="pack",
    )(cur, residuals, tile, cell)


def scattered(blocks, shape, left_ref, right_ref):
    size_x, size_z, size_y = shape
    rows = size_x * size_z
    mine = (lax.axis_index("gx") * lax.axis_size("gy") + lax.axis_index("gy")).astype(F32)
    row_iota = lax.broadcasted_iota(jnp.int32, (rows, LANES), 0)
    column_iota = lax.broadcasted_iota(jnp.int32, (size_y, LANES), 0)
    place = 0
    for block in blocks:
        cell = block[6:8].astype(jnp.int32)
        column = lax.rem(cell, size_y)
        row = jnp.where(block[4:6] == mine, lax.div(cell, size_y), -1)
        high = block[0:4].astype(BF16).astype(F32)
        rest = block[0:4] - high
        middle = rest.astype(BF16).astype(F32)
        low = rest - middle
        for half in range(2):
            lanes = slice(place, place + LANES)
            hit = row_iota == row[half : half + 1]
            for moment in range(2):
                line = 2 * moment + half
                for piece, value in enumerate((high, middle, low)):
                    top = (3 * moment + piece) * rows
                    left_ref[top : top + rows, lanes] = jnp.where(hit, value[line : line + 1], 0.0).astype(BF16)
            right_ref[:, lanes] = jnp.where(column_iota == column[half : half + 1], 1.0, 0.0).astype(BF16)
            place += LANES
    total = lax.dot_general(
        left_ref[...], right_ref[...], (((1,), (1,)), ((), ())), preferred_element_type=F32
    )
    parts = [total[i * rows : (i + 1) * rows].reshape(shape) for i in range(6)]
    return [parts[3 * moment] + (parts[3 * moment + 1] + parts[3 * moment + 2]) for moment in range(2)]


def one_hot_scratch(shape, blocks):
    count = 2 * LANES * blocks
    return [pltpu.VMEM((6 * shape[0] * shape[1], count), BF16), pltpu.VMEM((shape[2], count), BF16)]


def scatter_kernel(picks, based, *refs):
    blocks, refs = refs[: len(picks)], refs[len(picks) :]
    base_ref, refs = (refs[0], refs[1:]) if based else (None, refs)
    out_ref, left_ref, right_ref = refs
    values = [ref[pick] for ref, pick in zip(blocks, picks)]
    for moment, field in enumerate(scattered(values, out_ref.shape[1:], left_ref, right_ref)):
        out_ref[moment] = base_ref[moment] + field if based else field


def scatter(blocks, picks, shape, base=()):
    operands = near([*blocks, *base])
    return pl.pallas_call(
        functools.partial(scatter_kernel, picks, len(base)),
        out_shape=pltpu.VMEM((2,) + shape, F32),
        in_specs=[VMEM] * len(operands),
        out_specs=VMEM,
        scratch_shapes=one_hot_scratch(shape, len(picks)),
        name="scatter",
    )(*operands)


def faces_kernel(cur_ref, even_ref, odd_ref):
    half = cur_ref.shape[0] // 2
    is_odd = lax.rem(lax.axis_index("gz"), 2) == 1
    for where in column_blocks(cur_ref.shape[2]):
        low, high = cur_ref[0:half, :, where], cur_ref[half:, :, where]
        upper = lax.broadcasted_iota(jnp.int32, low.shape, 1) < 4
        first = jnp.where(upper, low, pltpu.roll(high, 4, 1))
        last = jnp.where(upper, pltpu.roll(low, 4, 1), high)
        even_ref[:, :, where] = jnp.where(is_odd, first, last)
        odd_ref[:, :, where] = jnp.where(is_odd, last, first)


def faces_z(cur):
    face = pltpu.VMEM((cur.shape[0] // 2,) + cur.shape[1:], F32)
    return call(faces_kernel, "faces_z", [cur], [face, face], (), 40000000)


def gather_kernel(picks, *refs):
    for place, pick in enumerate(picks):
        refs[-1][place] = refs[place][pick]


def gather_blocks(blocks, picks):
    return pl.pallas_call(
        functools.partial(gather_kernel, picks),
        out_shape=pltpu.VMEM((len(blocks), 8, LANES), F32),
        in_specs=[VMEM] * len(blocks),
        out_specs=VMEM,
        name="gather_blocks",
    )(*near(blocks))


def column_blocks(size_y):
    return [slice(start, start + LANES) for start in range(0, size_y, LANES)]


def pick_side(parts, is_odd, before):
    first, second = (parts[0], parts[1]) if before else (parts[1], parts[0])
    return jnp.where(is_odd, first, second)


def along_columns(count_y, cur_ref, y_refs):
    size_x, size_z, size_y = cur_ref.shape
    place = lax.axis_index("gy")
    is_odd = lax.rem(place, 2) == 1
    lane = lax.broadcasted_iota(jnp.int32, (size_x, size_z, LANES), 2)
    ends = []
    for before in (True, False):
        face = pick_side([ref[0:size_x] for ref in y_refs], is_odd, before)
        ends.append(jnp.where(place == (0 if before else count_y - 1), 0.0, face))
    wheres = column_blocks(size_y)
    columns = [ends[0]] + [cur_ref[:, :, where] for where in wheres] + [ends[1]]
    for j, where in enumerate(wheres):
        left, centre, right = columns[j : j + 3]
        total = (3.0 * stencil_weights[0]) * centre
        for offset in range(1, 5):
            pair = pltpu.roll(jnp.where(lane >= offset, centre, right), LANES - offset, 2)
            pair += pltpu.roll(jnp.where(lane < LANES - offset, centre, left), offset, 2)
            total += stencil_weights[offset] * pair
        yield where, centre, total


def across_columns(count_z, cur_ref, x_refs, z_refs):
    size_x, size_z, size_y = cur_ref.shape
    odd_x, odd_z = [lax.rem(lax.axis_index(name), 2) == 1 for name in ("gx", "gz")]
    layer = lax.broadcasted_iota(jnp.int32, (size_x, size_z, LANES), 1)
    upper = layer[0 : size_x // 2] < 4
    place_z = lax.axis_index("gz")
    for where in column_blocks(size_y):
        centre = cur_ref[:, :, where]
        halves = []
        for before in (True, False):
            layers = slice(size_x - 4, size_x) if before else slice(0, 4)
            parts = [ref[layers, :, where] for ref in x_refs]
            if len(parts) == 1:
                parts.append(jnp.zeros_like(parts[0]))
            halves.append(pick_side(parts, odd_x, before))
        along_x = jnp.concatenate([halves[0], centre, halves[1]], axis=0)
        parts = [ref[:, :, where] for ref in z_refs]
        after = jnp.where(place_z == count_z - 1, 0.0, pick_side(parts, odd_z, False))
        before = jnp.where(place_z == 0, 0.0, pick_side(parts, odd_z, True))
        low = jnp.where(upper, after, pltpu.roll(before, 4, 1))
        high = jnp.where(upper, pltpu.roll(after, 4, 1), before)
        beyond = jnp.concatenate([low, high], axis=0)
        total = jnp.zeros_like(centre)
        for offset in range(1, 5):
            pair = along_x[4 + offset : 4 + offset + size_x] + along_x[4 - offset : 4 - offset + size_x]
            pair += pltpu.roll(jnp.where(layer >= offset, centre, beyond), size_z - offset, 1)
            pair += pltpu.roll(jnp.where(layer < size_z - offset, centre, beyond), offset, 1)
            total += stencil_weights[offset] * pair
        yield where, centre, total


def first_kernel(counts, cur_ref, prev_ref, vel_ref, src_ref, even_ref, odd_ref, *refs):
    count_x, count_z, count_y = counts
    x_refs, z_refs, (next_ref, even_out, odd_out) = refs[:count_x], refs[count_x : count_x + 2], refs[count_x + 2 :]
    along = along_columns(count_y, cur_ref, (even_ref, odd_ref))
    across = across_columns(count_z, cur_ref, x_refs, z_refs)
    for (where, centre, total), (_, _, more) in zip(along, across):
        scaled = vel_ref[:, :, where] * courant_scale
        next_ref[:, :, where] = (
            2.0 * centre - prev_ref[:, :, where] + scaled * scaled * (total + more) + src_ref[0, :, :, where]
        )
    is_odd = lax.rem(lax.axis_index("gy"), 2) == 1
    first, last = next_ref[:, :, 0:LANES], next_ref[:, :, next_ref.shape[2] - LANES :]
    even_out[...] = jnp.where(is_odd, first, last)
    odd_out[...] = jnp.where(is_odd, last, first)


def second_start_kernel(counts, cur_ref, prev_ref, vel_ref, src_ref, accel_ref, *refs):
    count_x, count_z, _ = counts
    x_refs, z_refs, refs = refs[:count_x], refs[count_x : count_x + 2], refs[count_x + 2 :]
    out_ref, part_ref, speed_ref, sum_ref, factor_ref, sem = refs
    copy = pltpu.make_async_copy(cur_ref, out_ref, sem)
    copy.start()
    for where, centre, laplacian in across_columns(count_z, cur_ref, x_refs, z_refs):
        velocity = vel_ref[:, :, where]
        scaled = velocity * courant_scale
        speed_sq = scaled * scaled
        part_ref[:, :, where] = 2.0 * centre - prev_ref[:, :, where] + speed_sq * laplacian + src_ref[1, :, :, where]
        speed_ref[:, :, where] = speed_sq
        weight = -2.0 / (velocity * velocity * velocity)
        sum_ref[:, :, where] = weight * accel_ref[0, :, :, where] * centre
        factor_ref[:, :, where] = weight * accel_ref[1, :, :, where]
    copy.wait()


def second_end_kernel(
    counts, cur_ref, part_ref, speed_ref, sum_ref, factor_ref, even_ref, odd_ref,
    next_out, gradient_out, next_ref, gradient_ref, sem,
):
    copies = []
    for place, (where, _, laplacian) in enumerate(along_columns(counts[2], cur_ref, (even_ref, odd_ref))):
        advanced = part_ref[:, :, where] + speed_ref[:, :, where] * laplacian
        next_ref[place] = advanced
        gradient_ref[place] = sum_ref[:, :, where] + factor_ref[:, :, where] * advanced
        for ref, out_ref, i in ((next_ref, next_out, 0), (gradient_ref, gradient_out, 1)):
            copies.append(pltpu.make_async_copy(ref.at[place], out_ref.at[:, :, where], sem.at[2 * place + i]))
            copies[-1].start()
    for copy in copies:
        copy.wait()


def call(kernel, name, operands, outputs, scratch=(), cost=0):
    estimate = pl.CostEstimate(flops=0, bytes_accessed=cost, transcendentals=0) if cost else None
    return pl.pallas_call(
        kernel,
        out_shape=tuple(outputs),
        in_specs=[VMEM] * len(operands),
        out_specs=tuple(HBM if isinstance(output, jax.ShapeDtypeStruct) else VMEM for output in outputs),
        scratch_shapes=list(scratch),
        cost_estimate=estimate,
        name=name,
    )(*near(operands))


def bucketed(residuals, target, cell, tile_count):
    held_count = residuals.shape[1]
    capacity = max(2, 2 * held_count // tile_count)
    one_hot = (target[:, None] == jnp.arange(tile_count, dtype=jnp.int32)[None, :]).astype(jnp.int32)
    earlier = jnp.cumsum(one_hot, axis=0) - one_hot
    slot_index = target * capacity + jnp.sum(one_hot * earlier, axis=1)
    payload = jnp.stack([residuals[0], residuals[1], cell.astype(F32)])
    outgoing = jnp.zeros((3, tile_count * capacity), F32).at[:, slot_index].set(payload)
    incoming = lax.all_to_all(outgoing, ("gx", "gy"), split_axis=1, concat_axis=1, tiled=True)
    block = 2 * LANES
    count = -(-incoming.shape[1] // block)
    incoming = jnp.pad(incoming, ((0, 0), (0, count * block - incoming.shape[1])))
    mine = (lax.axis_index("gx") * lax.axis_size("gy") + lax.axis_index("gy")).astype(F32)
    parts = jnp.concatenate([incoming[:2], jnp.full((1, count * block), mine), incoming[2:]])
    return parts.reshape(4, count, 2, LANES).transpose(1, 0, 2, 3).reshape(count, 8, LANES)


def shards(adj_prev, adj_cur, velocity, fwd_accel, residuals, recv_tile, recv_cell):
    count_x, count_z, count_y = sizes = tuple(lax.axis_size(name) for name in ("gx", "gz", "gy"))
    shape = velocity.shape
    target = recv_tile[:, 0]

    def swap_faces(face, axis, size, offset):
        if count_x % 2 or (offset == 0 and size % 2 == 0):
            return lax.ppermute(face, axis, pair_swaps(size, offset))
        return lax.ppermute(face, ("gx", axis), full_swaps(count_x, size, offset))

    def halos_x(value):
        return [lax.ppermute(value, "gx", pair_swaps(count_x, offset)) for offset in range(min(2, count_x - 1))]

    def halos_z(value):
        return [swap_faces(face, "gz", count_z, offset) for offset, face in enumerate(faces_z(value))]

    even_face, odd_face, own, current = pack(
        adj_cur, residuals, target.reshape(2, LANES), recv_cell.reshape(2, LANES)
    )
    if count_x == 2 and count_y == 4:
        even = lax.ppermute(even_face, "gy", xor_swaps(4, 1))
        odd = lax.ppermute(odd_face, "gy", xor_swaps(4, 3))
        far = lax.ppermute(own, "gy", xor_swaps(4, 2))
        along_z = halos_z(current)
        same, picks = [own, far, even, odd], (0, 0, shape[0], shape[0])
        packed = gather_blocks(same, picks)
        packed, late = lax.optimization_barrier((packed, current))
        along_x = halos_x(late)
        swapped = lax.ppermute(packed, "gx", pair_swaps(2, 0))
        source = scatter(same, picks, shape)
        source = scatter([swapped] * len(same), tuple(range(len(same))), shape, [source])
    else:
        along_x, along_z = halos_x(current), halos_z(current)
        even = lax.ppermute(even_face, "gy", pair_swaps(count_y, 0))
        odd = lax.ppermute(odd_face, "gy", pair_swaps(count_y, 1))
        parts = bucketed(residuals, target, recv_cell, count_x * count_y)
        source = scatter([parts] * parts.shape[0], tuple(range(parts.shape[0])), shape)
    counts = (len(along_x), count_z, count_y)
    field, face = pltpu.VMEM(shape, F32), pltpu.VMEM(shape[:2] + (LANES,), F32)
    whole = jax.ShapeDtypeStruct(shape, F32)
    advanced, even_face, odd_face = call(
        functools.partial(first_kernel, counts),
        "first_step",
        [current, adj_prev, velocity, source, even, odd, *along_x, *along_z],
        [field, face, face],
    )
    along_x, along_z = halos_x(advanced), halos_z(advanced)
    odd = swap_faces(odd_face, "gy", count_y, 1)
    even = swap_faces(even_face, "gy", count_y, 0)
    first, *parts = call(
        functools.partial(second_start_kernel, counts),
        "second_start",
        [advanced, current, velocity, source, fwd_accel, *along_x, *along_z],
        [whole, field, field, field, field],
        [pltpu.SemaphoreType.DMA],
    )
    blocks = shape[2] // LANES
    tiles = pltpu.VMEM((blocks,) + shape[:2] + (LANES,), F32)
    latest, gradient = call(
        functools.partial(second_end_kernel, counts),
        "second_end",
        [advanced, *parts, even, odd],
        [whole, whole],
        [tiles, tiles, pltpu.SemaphoreType.DMA((2 * blocks,))],
    )
    return first, latest, gradient


def solution(mesh):
    placed = (
        P("gx", "gz", "gy"),
        P("gx", "gz", "gy"),
        P("gx", "gz", "gy"),
        P(None, "gx", "gz", "gy"),
        P(None, ("gx", "gy", "gz")),
        P(("gx", "gy", "gz"), None),
        P(("gx", "gy", "gz")),
    )
    return jax.shard_map(
        shards,
        mesh=mesh,
        in_specs=placed,
        out_specs=(P("gx", "gz", "gy"), P("gx", "gz", "gy"), P("gx", "gz", "gy")),
        check_vma=False,
    )
```

time: 41.5 us -> 23.4 us (0.56)
  the two profiles are of different devices: /device:TPU:4 before, /device:TPU:10 now
where the time goes in v2:
time: 23.4 us; the launch traced here: 23.2 us
  starting transfers between devices  11 us (47%)
  waiting for transfers between devices  6.58 us (28%)
  Pallas kernels  4.84 us (21%)
  between operations  0.76 us (3%)
    ppermute x3, starting transfers between devices, swap_faces(): return lax.ppermute(face, ('gx', axis), full_swaps(count_x, size, offset))  6.16 us
    ppermute x1, waiting for transfers between devices, shards(): far = lax.ppermute(own, 'gy', xor_swaps(4, 2))  3.1 us
    ppermute x1, starting transfers between devices, shards(): odd = lax.ppermute(odd_face, 'gy', xor_swaps(4, 3))  2.45 us
    pallas_call x5, Pallas kernels, call(): pl.pallas_call(kernel, out_shape=tuple(outputs), in_specs=[VMEM] * len(op...  2.14 us
    ppermute x3, waiting for transfers between devices, swap_faces(): return lax.ppermute(face, ('gx', axis), full_swaps(count_x, size, offset))  2.01 us
    pallas_call x2, Pallas kernels, scatter(): pl.pallas_call(functools.partial(scatter_kernel, picks, len(base)), out_s...  1.64 us
    ppermute x3, waiting for transfers between devices, swap_faces(): return lax.ppermute(face, axis, pair_swaps(size, offset))  1.13 us
    ppermute x3, starting transfers between devices, swap_faces(): return lax.ppermute(face, axis, pair_swaps(size, offset))  1.12 us
  transfers between devices with their start and end apart: 12, of which 7 were waited for; matrix products, arithmetic and copies ran while one was open for 0% of the time, Pallas kernels for 10%

profile of v2, /device:TPU:10, one launch (start us, length us, event | category | flops | bytes accessed | tf_op | source)
XLA Modules:
  0.0 23.2 jit_solution(17080108571906629882)
XLA Ops:
  0.6 1.1 %pack.1 = (f32[9,8,128]{2,1,0:T(8,128)S(1)}, f32[9,8,128]{2,1,0:T(8,128)S(1)}, f32[1,8,128]{2,1,0:T(8,128)S(1)}, f32[8,8,512]{2,1,0:T(8,128)S(1)}) custom-call(f32[8,8,512]{2,1,0:T(8,128)} %cur_ref.1, f32[2,256]{1,0:T(2,128)} %res_ref.1, s32[2,128]{1,0:T(2,128)} %bitcast.2, s32[2,128]{1,0:T(2,128)} %bitcast.3), custom_call_target="tpu_custom_call" | custom-call | tf_op jit(solution)/shard_map/pack/pallas_call | solution.py:76
  1.7 0.6 %collective-permute-start.1 = (f32[9,8,128]{2,1,0:T(8,128)S(1)}, f32[9,8,128]{2,1,0:T(8,128)S(1)}, u32[]{:S(2)}, u32[]{:S(2)}) collective-permute-start(f32[9,8,128]{2,1,0:T(8,128)S(1)} %get-tuple-element.25), channel_id=1, source_target_pairs={{0,4},{4,0},{8,12},{12,8},{1,5},{5,1},{9,13},{13,9},{2,6},{6,2},{1... | collective-permute-start | bytes 110600 | tf_op jit(solution)/shard_map/ppermute | solution.py:342
  2.3 2.4 %collective-permute-start.2 = (f32[9,8,128]{2,1,0:T(8,128)S(1)}, f32[9,8,128]{2,1,0:T(8,128)S(1)}, u32[]{:S(2)}, u32[]{:S(2)}) collective-permute-start(f32[9,8,128]{2,1,0:T(8,128)S(1)} %get-tuple-element.26), channel_id=1, source_target_pairs={{0,12},{4,8},{8,4},{12,0},{1,13},{5,9},{9,5},{13,1},{2,14},{6,10},... | collective-permute-start | bytes 110600 | tf_op jit(solution)/shard_map/ppermute | solution.py:343
  4.7 0.5 %collective-permute-start = (f32[1,8,128]{2,1,0:T(8,128)S(1)}, f32[1,8,128]{2,1,0:T(8,128)S(1)}, u32[]{:S(2)}, u32[]{:S(2)}) collective-permute-start(f32[1,8,128]{2,1,0:T(8,128)S(1)} %get-tuple-element.24.refs_0_), channel_id=1, source_target_pairs={{0,8},{4,12},{8,0},{12,4},{1,9},{5,13},{9,1},{13,5},{2,10},{6,14},... | collective-permute-start | bytes 12296 | tf_op jit(solution)/shard_map/ppermute | solution.py:344
  5.3 3.1 %collective-permute-done.refs_1_ = f32[1,8,128]{2,1,0:T(8,128)S(1)} collective-permute-done((f32[1,8,128]{2,1,0:T(8,128)S(1)}, f32[1,8,128]{2,1,0:T(8,128)S(1)}, u32[]{:S(2)}, u32[]{:S(2)}) %collective-permute-start) | collective-permute-done | bytes 4128 | tf_op jit(solution)/shard_map/ppermute | solution.py:344
  8.4 0.0 collective-permute-done.1.refs_2_.even_ref
  8.4 0.0 collective-permute-done.2.refs_3_.odd_ref
  8.4 0.1 collective-permute-start.4
  8.5 0.5 %collective-permute-start.5 = (f32[4,8,512]{2,1,0:T(8,128)S(1)}, f32[4,8,512]{2,1,0:T(8,128)S(1)}, u32[]{:S(2)}, u32[]{:S(2)}) collective-permute-start(f32[4,8,512]{2,1,0:T(8,128)S(1)} %get-tuple-element.29), channel_id=1, source_target_pairs={{0,1},{1,0},{2,3},{3,2},{4,5},{5,4},{6,7},{7,6},{8,9},{9,8},{10,11... | collective-permute-start | bytes 196616 | tf_op jit(solution)/shard_map/ppermute | solution.py:329
  9.0 2.7 %collective-permute-start.6 = (f32[4,8,512]{2,1,0:T(8,128)S(1)}, f32[4,8,512]{2,1,0:T(8,128)S(1)}, u32[]{:S(2)}, u32[]{:S(2)}) collective-permute-start(f32[4,8,512]{2,1,0:T(8,128)S(1)} %get-tuple-element.30), channel_id=1, source_target_pairs={{0,16},{1,2},{2,1},{3,19},{16,0},{17,18},{18,17},{19,3},{4,20},{5,... | collective-permute-start | bytes 196616 | tf_op jit(solution)/shard_map/ppermute | solution.py:330
  11.7 0.0 collective-permute-start.3
  11.7 0.8 %scatter.2.refs_4_ = f32[2,8,8,512]{3,2,1,0:T(8,128)S(1)} custom-call(f32[1,8,128]{2,1,0:T(8,128)S(1)} %get-tuple-element.24.refs_0_, f32[1,8,128]{2,1,0:T(8,128)S(1)} %collective-permute-done.refs_1_, f32[9,8,128]{2,1,0:T(8,128)S(1)} %collective-permute-done.1.refs_2_.even_ref, f32[9,8,128]{2,1,0:T(8,128)S(1)} %collective-permute-done.2.refs_3_.odd_ref), custom_call_target="tpu_custom_call" | custom-call | tf_op jit(solution)/shard_map/scatter/pallas_call | solution.py:139
  12.5 0.0 copy-start
  12.5 0.0 copy-start.2
  12.5 0.3 %collective-permute-done.3.refs_0_.refs_1_.refs_2_.refs_3_ = f32[4,8,128]{2,1,0:T(8,128)S(1)} collective-permute-done((f32[4,8,128]{2,1,0:T(8,128)S(1)}, f32[4,8,128]{2,1,0:T(8,128)S(1)}, u32[]{:S(2)}, u32[]{:S(2)}) %collective-permute-start.3) | collective-permute-done | bytes 16416 | tf_op jit(solution)/shard_map/ppermute | solution.py:350
  12.9 0.8 %scatter.3.src_ref = f32[2,8,8,512]{3,2,1,0:T(8,128)S(1)} custom-call(f32[4,8,128]{2,1,0:T(8,128)S(1)} %collective-permute-done.3.refs_0_.refs_1_.refs_2_.refs_3_, f32[4,8,128]{2,1,0:T(8,128)S(1)} %collective-permute-done.3.refs_0_.refs_1_.refs_2_.refs_3_, f32[4,8,128]{2,1,0:T(8,128)S(1)} %collective-permute-done.3.refs_0_.refs_1_.refs_2_.refs_3_, ...), custom_call_target="tpu_custom_call" | custom-call | tf_op jit(solution)/shard_map/scatter/pallas_call | solution.py:139
  13.7 0.4 %collective-permute-done.6.refs_2_ = f32[4,8,512]{2,1,0:T(8,128)S(1)} collective-permute-done((f32[4,8,512]{2,1,0:T(8,128)S(1)}, f32[4,8,512]{2,1,0:T(8,128)S(1)}, u32[]{:S(2)}, u32[]{:S(2)}) %collective-permute-start.6) | collective-permute-done | bytes 65568 | tf_op jit(solution)/shard_map/ppermute | solution.py:330
  14.2 0.0 collective-permute-done.4.refs_0_
  14.2 0.0 copy-start.1
  14.2 0.4 %first_step.1 = (f32[8,8,512]{2,1,0:T(8,128)S(1)}, f32[8,8,128]{2,1,0:T(8,128)S(1)}, f32[8,8,128]{2,1,0:T(8,128)S(1)}) custom-call(f32[8,8,512]{2,1,0:T(8,128)S(1)} %get-tuple-element.28.cur_ref.prev_ref, f32[8,8,512]{2,1,0:T(8,128)S(1)} %copy-done.2, f32[8,8,512]{2,1,0:T(8,128)S(1)} %copy-done, f32[2,8,8,512]{3,2,1,0:T(8,128)S(1)} %scatter.3.src_ref, ...), custom_call_target="tpu_custom_call" | custom-call | tf_op jit(solution)/shard_map/first_step/pallas_call | solution.py:294
  14.6 0.1 collective-permute-start.7
  14.7 0.1 collective-permute-start.8
  14.8 2.0 %collective-permute-start.9 = (f32[4,8,512]{2,1,0:T(8,128)S(1)}, f32[4,8,512]{2,1,0:T(8,128)S(1)}, u32[]{:S(2)}, u32[]{:S(2)}) collective-permute-start(f32[4,8,512]{2,1,0:T(8,128)S(1)} %get-tuple-element.33), channel_id=1, source_target_pairs={{0,16},{1,2},{2,1},{3,19},{16,0},{17,18},{18,17},{19,3},{4,20},{5,... | collective-permute-start | bytes 196616 | tf_op jit(solution)/shard_map/ppermute | solution.py:330
  16.8 0.5 %collective-permute-start.10 = (f32[8,8,128]{2,1,0:T(8,128)S(1)}, f32[8,8,128]{2,1,0:T(8,128)S(1)}, u32[]{:S(2)}, u32[]{:S(2)}) collective-permute-start(f32[8,8,128]{2,1,0:T(8,128)S(1)} %get-tuple-element.39), channel_id=1, source_target_pairs={{0,4},{4,0},{8,12},{12,8},{1,5},{5,1},{9,13},{13,9},{2,6},{6,2},{1... | collective-permute-start | bytes 98312 | tf_op jit(solution)/shard_map/ppermute | solution.py:329
  17.3 1.4 %collective-permute-start.11 = (f32[8,8,128]{2,1,0:T(8,128)S(1)}, f32[8,8,128]{2,1,0:T(8,128)S(1)}, u32[]{:S(2)}, u32[]{:S(2)}) collective-permute-start(f32[8,8,128]{2,1,0:T(8,128)S(1)} %get-tuple-element.40), channel_id=1, source_target_pairs={{0,16},{4,8},{8,4},{12,28},{16,0},{20,24},{24,20},{28,12},{1,17},{... | collective-permute-start | bytes 98312 | tf_op jit(solution)/shard_map/ppermute | solution.py:330
  18.7 0.5 %collective-permute-done.8.refs_1_ = f32[4,8,512]{2,1,0:T(8,128)S(1)} collective-permute-done((f32[4,8,512]{2,1,0:T(8,128)S(1)}, f32[4,8,512]{2,1,0:T(8,128)S(1)}, u32[]{:S(2)}, u32[]{:S(2)}) %collective-permute-start.8) | collective-permute-done | bytes 65568 | tf_op jit(solution)/shard_map/ppermute | solution.py:329
  19.2 0.1 collective-permute-done.9.refs_2_
  19.4 0.0 collective-permute-done.7.refs_0_
  19.4 0.7 %second_start.1 = (f32[8,8,512]{2,1,0:T(8,128)}, f32[8,8,512]{2,1,0:T(8,128)S(1)}, f32[8,8,512]{2,1,0:T(8,128)S(1)}, f32[8,8,512]{2,1,0:T(8,128)S(1)}, f32[8,8,512]{2,1,0:T(8,128)S(1)}) custom-call(f32[8,8,512]{2,1,0:T(8,128)S(1)} %get-tuple-element.31.cur_ref, f32[8,8,512]{2,1,0:T(8,128)S(1)} %get-tuple-element.28.cur_ref.prev_ref, ...), custom_call_target="tpu_custom_call" | custom-call | tf_op jit(solution)/shard_map/second_start/pallas_call | solution.py:294
  20.1 0.6 %collective-permute-done.10.even_ref = f32[8,8,128]{2,1,0:T(8,128)S(1)} collective-permute-done((f32[8,8,128]{2,1,0:T(8,128)S(1)}, f32[8,8,128]{2,1,0:T(8,128)S(1)}, u32[]{:S(2)}, u32[]{:S(2)}) %collective-permute-start.10) | collective-permute-done | bytes 32800 | tf_op jit(solution)/shard_map/ppermute | solution.py:329
  20.7 1.4 %collective-permute-done.11.odd_ref = f32[8,8,128]{2,1,0:T(8,128)S(1)} collective-permute-done((f32[8,8,128]{2,1,0:T(8,128)S(1)}, f32[8,8,128]{2,1,0:T(8,128)S(1)}, u32[]{:S(2)}, u32[]{:S(2)}) %collective-permute-start.11) | collective-permute-done | bytes 32800 | tf_op jit(solution)/shard_map/ppermute | solution.py:330
  22.1 1.0 %second_end.1 = (f32[8,8,512]{2,1,0:T(8,128)}, f32[8,8,512]{2,1,0:T(8,128)}) custom-call(f32[8,8,512]{2,1,0:T(8,128)S(1)} %get-tuple-element.31.cur_ref, f32[8,8,512]{2,1,0:T(8,128)S(1)} %get-tuple-element.35.part_ref, f32[8,8,512]{2,1,0:T(8,128)S(1)} %get-tuple-element.36.speed_ref, f32[8,8,512]{2,1,0:T(8,128)S(1)} %get-tuple-element.37.sum_ref, ...), custom_call_target="tpu_custom_call" | custom-call | tf_op jit(solution)/shard_map/second_end/pallas_call | solution.py:294
  (7 shorter events, 0.1 us)
Async XLA Ops:
  1.7 6.7 %collective-permute-start.1 = (f32[9,8,128]{2,1,0:T(8,128)S(1)}, f32[9,8,128]{2,1,0:T(8,128)S(1)}, u32[]{:S(2)}, u32[]{:S(2)}) collective-permute-start(f32[9,8,128]{2,1,0:T(8,128)S(1)} %get-tuple-element.25), channel_id=1, source_target_pairs={{0,4},{4,0},{8,12},{12,8},{1,5},{5,1},{9,13},{13,9},{2,6},{6,2},{1... | collective-permute-start | bytes 110600 | tf_op jit(solution)/shard_map/ppermute | solution.py:342
  2.3 6.1 %collective-permute-start.2 = (f32[9,8,128]{2,1,0:T(8,128)S(1)}, f32[9,8,128]{2,1,0:T(8,128)S(1)}, u32[]{:S(2)}, u32[]{:S(2)}) collective-permute-start(f32[9,8,128]{2,1,0:T(8,128)S(1)} %get-tuple-element.26), channel_id=1, source_target_pairs={{0,12},{4,8},{8,4},{12,0},{1,13},{5,9},{9,5},{13,1},{2,14},{6,10},... | collective-permute-start | bytes 110600 | tf_op jit(solution)/shard_map/ppermute | solution.py:343
  4.7 3.6 %collective-permute-start = (f32[1,8,128]{2,1,0:T(8,128)S(1)}, f32[1,8,128]{2,1,0:T(8,128)S(1)}, u32[]{:S(2)}, u32[]{:S(2)}) collective-permute-start(f32[1,8,128]{2,1,0:T(8,128)S(1)} %get-tuple-element.24.refs_0_), channel_id=1, source_target_pairs={{0,8},{4,12},{8,0},{12,4},{1,9},{5,13},{9,1},{13,5},{2,10},{6,14},... | collective-permute-start | bytes 12296 | tf_op jit(solution)/shard_map/ppermute | solution.py:344
  8.4 5.8 %collective-permute-start.4 = (f32[8,8,512]{2,1,0:T(8,128)S(1)}, f32[8,8,512]{2,1,0:T(8,128)S(1)}, u32[]{:S(2)}, u32[]{:S(2)}) collective-permute-start(f32[8,8,512]{2,1,0:T(8,128)S(1)} %get-tuple-element.28.cur_ref.prev_ref), channel_id=1, source_target_pairs={{0,16},{16,0},{1,17},{17,1},{2,18},{18,2},{3,19},{19,3},{4,20},{20... | collective-permute-start | bytes 393224 | tf_op jit(solution)/shard_map/ppermute | solution.py:333
  8.5 5.2 %collective-permute-start.5 = (f32[4,8,512]{2,1,0:T(8,128)S(1)}, f32[4,8,512]{2,1,0:T(8,128)S(1)}, u32[]{:S(2)}, u32[]{:S(2)}) collective-permute-start(f32[4,8,512]{2,1,0:T(8,128)S(1)} %get-tuple-element.29), channel_id=1, source_target_pairs={{0,1},{1,0},{2,3},{3,2},{4,5},{5,4},{6,7},{7,6},{8,9},{9,8},{10,11... | collective-permute-start | bytes 196616 | tf_op jit(solution)/shard_map/ppermute | solution.py:329
  9.0 5.2 %collective-permute-start.6 = (f32[4,8,512]{2,1,0:T(8,128)S(1)}, f32[4,8,512]{2,1,0:T(8,128)S(1)}, u32[]{:S(2)}, u32[]{:S(2)}) collective-permute-start(f32[4,8,512]{2,1,0:T(8,128)S(1)} %get-tuple-element.30), channel_id=1, source_target_pairs={{0,16},{1,2},{2,1},{3,19},{16,0},{17,18},{18,17},{19,3},{4,20},{5,... | collective-permute-start | bytes 196616 | tf_op jit(solution)/shard_map/ppermute | solution.py:330
  11.7 1.2 %collective-permute-start.3 = (f32[4,8,128]{2,1,0:T(8,128)S(1)}, f32[4,8,128]{2,1,0:T(8,128)S(1)}, u32[]{:S(2)}, u32[]{:S(2)}) collective-permute-start(f32[4,8,128]{2,1,0:T(8,128)S(1)} %gather_blocks.1), channel_id=1, source_target_pairs={{0,16},{16,0},{1,17},{17,1},{2,18},{18,2},{3,19},{19,3},{4,20},{20... | collective-permute-start | bytes 49160 | tf_op jit(solution)/shard_map/ppermute | solution.py:350
  12.5 1.6 %copy-start = (f32[8,8,512]{2,1,0:T(8,128)S(1)}, f32[8,8,512]{2,1,0:T(8,128)}, u32[]{:S(2)}) copy-start(f32[8,8,512]{2,1,0:T(8,128)} %vel_ref.3) | copy-start | bytes 393220
  12.5 1.6 %copy-start.2 = (f32[8,8,512]{2,1,0:T(8,128)S(1)}, f32[8,8,512]{2,1,0:T(8,128)}, u32[]{:S(2)}) copy-start(f32[8,8,512]{2,1,0:T(8,128)} %prev_ref.1) | copy-start | bytes 393220
  14.2 5.2 %copy-start.1 = (f32[2,8,8,512]{3,2,1,0:T(8,128)S(1)}, f32[2,8,8,512]{3,2,1,0:T(8,128)}, u32[]{:S(2)}) copy-start(f32[2,8,8,512]{3,2,1,0:T(8,128)} %accel_ref.1) | copy-start | bytes 786436
  14.6 4.8 %collective-permute-start.7 = (f32[8,8,512]{2,1,0:T(8,128)S(1)}, f32[8,8,512]{2,1,0:T(8,128)S(1)}, u32[]{:S(2)}, u32[]{:S(2)}) collective-permute-start(f32[8,8,512]{2,1,0:T(8,128)S(1)} %get-tuple-element.31.cur_ref), channel_id=1, source_target_pairs={{0,16},{16,0},{1,17},{17,1},{2,18},{18,2},{3,19},{19,3},{4,20},{20... | collective-permute-start | bytes 393224 | tf_op jit(solution)/shard_map/ppermute | solution.py:333
  14.7 4.6 %collective-permute-start.8 = (f32[4,8,512]{2,1,0:T(8,128)S(1)}, f32[4,8,512]{2,1,0:T(8,128)S(1)}, u32[]{:S(2)}, u32[]{:S(2)}) collective-permute-start(f32[4,8,512]{2,1,0:T(8,128)S(1)} %get-tuple-element.32), channel_id=1, source_target_pairs={{0,1},{1,0},{2,3},{3,2},{4,5},{5,4},{6,7},{7,6},{8,9},{9,8},{10,11... | collective-permute-start | bytes 196616 | tf_op jit(solution)/shard_map/ppermute | solution.py:329
  14.8 4.6 %collective-permute-start.9 = (f32[4,8,512]{2,1,0:T(8,128)S(1)}, f32[4,8,512]{2,1,0:T(8,128)S(1)}, u32[]{:S(2)}, u32[]{:S(2)}) collective-permute-start(f32[4,8,512]{2,1,0:T(8,128)S(1)} %get-tuple-element.33), channel_id=1, source_target_pairs={{0,16},{1,2},{2,1},{3,19},{16,0},{17,18},{18,17},{19,3},{4,20},{5,... | collective-permute-start | bytes 196616 | tf_op jit(solution)/shard_map/ppermute | solution.py:330
  16.8 3.9 %collective-permute-start.10 = (f32[8,8,128]{2,1,0:T(8,128)S(1)}, f32[8,8,128]{2,1,0:T(8,128)S(1)}, u32[]{:S(2)}, u32[]{:S(2)}) collective-permute-start(f32[8,8,128]{2,1,0:T(8,128)S(1)} %get-tuple-element.39), channel_id=1, source_target_pairs={{0,4},{4,0},{8,12},{12,8},{1,5},{5,1},{9,13},{13,9},{2,6},{6,2},{1... | collective-permute-start | bytes 98312 | tf_op jit(solution)/shard_map/ppermute | solution.py:329
  17.3 4.8 %collective-permute-start.11 = (f32[8,8,128]{2,1,0:T(8,128)S(1)}, f32[8,8,128]{2,1,0:T(8,128)S(1)}, u32[]{:S(2)}, u32[]{:S(2)}) collective-permute-start(f32[8,8,128]{2,1,0:T(8,128)S(1)} %get-tuple-element.40), channel_id=1, source_target_pairs={{0,16},{4,8},{8,4},{12,28},{16,0},{20,24},{24,20},{28,12},{1,17},{... | collective-permute-start | bytes 98312 | tf_op jit(solution)/shard_map/ppermute | solution.py:330

commit v3 on v2

--- a/solution.py
+++ b/solution.py
@@ -146,9 +146,10 @@
     )(*operands)
 
 
-def faces_kernel(cur_ref, even_ref, odd_ref):
+def faces_kernel(cur_ref, even_ref, odd_ref, *x_refs):
     half = cur_ref.shape[0] // 2
     is_odd = lax.rem(lax.axis_index("gz"), 2) == 1
+    at_odd_x = lax.rem(lax.axis_index("gx"), 2) == 1
     for where in column_blocks(cur_ref.shape[2]):
         low, high = cur_ref[0:half, :, where], cur_ref[half:, :, where]
         upper = lax.broadcasted_iota(jnp.int32, low.shape, 1) < 4
@@ -156,11 +157,15 @@
         last = jnp.where(upper, pltpu.roll(low, 4, 1), high)
         even_ref[:, :, where] = jnp.where(is_odd, first, last)
         odd_ref[:, :, where] = jnp.where(is_odd, last, first)
-
-
-def faces_z(cur):
-    face = pltpu.VMEM((cur.shape[0] // 2,) + cur.shape[1:], F32)
-    return call(faces_kernel, "faces_z", [cur], [face, face], (), 40000000)
+        first, last = cur_ref[0:4, :, where], cur_ref[cur_ref.shape[0] - 4 :, :, where]
+        for ref, mine, other in zip(x_refs, (last, first), (first, last)):
+            ref[:, :, where] = jnp.where(at_odd_x, other, mine)
+
+
+def faces_xz(cur, count_x):
+    face_z = pltpu.VMEM((cur.shape[0] // 2,) + cur.shape[1:], F32)
+    face_x = pltpu.VMEM((4,) + cur.shape[1:], F32)
+    return call(faces_kernel, "faces", [cur], [face_z, face_z] + [face_x] * count_x)
 
 
 def gather_kernel(picks, *refs):
@@ -218,8 +223,7 @@
         centre = cur_ref[:, :, where]
         halves = []
         for before in (True, False):
-            layers = slice(size_x - 4, size_x) if before else slice(0, 4)
-            parts = [ref[layers, :, where] for ref in x_refs]
+            parts = [ref[:, :, where] for ref in x_refs]
             if len(parts) == 1:
                 parts.append(jnp.zeros_like(parts[0]))
             halves.append(pick_side(parts, odd_x, before))
@@ -329,11 +333,13 @@
             return lax.ppermute(face, axis, pair_swaps(size, offset))
         return lax.ppermute(face, ("gx", axis), full_swaps(count_x, size, offset))
 
-    def halos_x(value):
-        return [lax.ppermute(value, "gx", pair_swaps(count_x, offset)) for offset in range(min(2, count_x - 1))]
-
-    def halos_z(value):
-        return [swap_faces(face, "gz", count_z, offset) for offset, face in enumerate(faces_z(value))]
+    messages_x = min(2, count_x - 1)
+
+    def halos_x(faces):
+        return [lax.ppermute(face, "gx", pair_swaps(count_x, offset)) for offset, face in enumerate(faces)]
+
+    def halos_z(faces):
+        return [swap_faces(face, "gz", count_z, offset) for offset, face in enumerate(faces)]
 
     even_face, odd_face, own, current = pack(
         adj_cur, residuals, target.reshape(2, LANES), recv_cell.reshape(2, LANES)
@@ -342,21 +348,23 @@
         even = lax.ppermute(even_face, "gy", xor_swaps(4, 1))
         odd = lax.ppermute(odd_face, "gy", xor_swaps(4, 3))
         far = lax.ppermute(own, "gy", xor_swaps(4, 2))
-        along_z = halos_z(current)
+        *faces_z, face_x = faces_xz(current, messages_x)
+        along_z = halos_z(faces_z)
         same, picks = [own, far, even, odd], (0, 0, shape[0], shape[0])
         packed = gather_blocks(same, picks)
-        packed, late = lax.optimization_barrier((packed, current))
-        along_x = halos_x(late)
+        packed, face_x = lax.optimization_barrier((packed, face_x))
+        along_x = halos_x([face_x])
         swapped = lax.ppermute(packed, "gx", pair_swaps(2, 0))
         source = scatter(same, picks, shape)
         source = scatter([swapped] * len(same), tuple(range(len(same))), shape, [source])
     else:
-        along_x, along_z = halos_x(current), halos_z(current)
+        faces = faces_xz(current, messages_x)
+        along_x, along_z = halos_x(faces[2:]), halos_z(faces[:2])
         even = lax.ppermute(even_face, "gy", pair_swaps(count_y, 0))
         odd = lax.ppermute(odd_face, "gy", pair_swaps(count_y, 1))
         parts = bucketed(residuals, target, recv_cell, count_x * count_y)
         source = scatter([parts] * parts.shape[0], tuple(range(parts.shape[0])), shape)
-    counts = (len(along_x), count_z, count_y)
+    counts = (messages_x, count_z, count_y)
     field, face = pltpu.VMEM(shape, F32), pltpu.VMEM(shape[:2] + (LANES,), F32)
     whole = jax.ShapeDtypeStruct(shape, F32)
     advanced, even_face, odd_face = call(
@@ -365,7 +373,8 @@
         [current, adj_prev, velocity, source, even, odd, *along_x, *along_z],
         [field, face, face],
     )
-    along_x, along_z = halos_x(advanced), halos_z(advanced)
+    faces = faces_xz(advanced, messages_x)
+    along_x, along_z = halos_x(faces[2:]), halos_z(faces[:2])
     odd = swap_faces(odd_face, "gy", count_y, 1)
     even = swap_faces(even_face, "gy", count_y, 0)
     first, *parts = call(

time: 23.4 us -> 21.2 us (0.906)
  waiting for transfers between devices: 6.58 us -> 2.72 us
  starting transfers between devices: 11 us -> 12.6 us
    ppermute x1, waiting for transfers between devices: 3.1 us -> 0.01 us  [shards(): far = lax.ppermute(own, 'gy', xor_swaps(4, 2))]
    ppermute x3, starting transfers between devices: 6.16 us -> 6.85 us  [swap_faces(): return lax.ppermute(face, ('gx', axis), full_swaps(count_x, size, offset))]
    ppermute x1, starting transfers between devices: 0.01 us -> 0.5 us  [shards(): swapped = lax.ppermute(packed, 'gx', pair_swaps(2, 0))]
    ppermute x1, waiting for transfers between devices: 0.33 us -> 0.01 us  [shards(): swapped = lax.ppermute(packed, 'gx', pair_swaps(2, 0))]
    ppermute x3, waiting for transfers between devices: 2.01 us -> 1.7 us  [swap_faces(): return lax.ppermute(face, ('gx', axis), full_swaps(count_x, size, offset))]
    ppermute x2, starting transfers between devices: 0.14 us -> 0.42 us  [halos_x(): lax.ppermute(face, 'gx', pair_swaps(count_x, offset))]
  transfers between devices with their start and end apart: 12 -> 12, of which waited for: 7 -> 3; matrix products, arithmetic and copies ran while one was open for 0% -> 0% of each run, Pallas kernels for 10% -> 11%
where the time goes in v3:
time: 21.2 us; the launch traced here: 21.1 us
  starting transfers between devices  12.6 us (59%)
  Pallas kernels  4.86 us (23%)
  waiting for transfers between devices  2.72 us (13%)
  between operations  0.76 us (4%)
    ppermute x3, starting transfers between devices, swap_faces(): return lax.ppermute(face, ('gx', axis), full_swaps(count_x, size, offset))  6.85 us
    ppermute x1, starting transfers between devices, shards(): odd = lax.ppermute(odd_face, 'gy', xor_swaps(4, 3))  2.45 us
    pallas_call x5, Pallas kernels, call(): pl.pallas_call(kernel, out_shape=tuple(outputs), in_specs=[VMEM] * len(op...  2.15 us
    ppermute x3, waiting for transfers between devices, swap_faces(): return lax.ppermute(face, ('gx', axis), full_swaps(count_x, size, offset))  1.7 us
    pallas_call x2, Pallas kernels, scatter(): pl.pallas_call(functools.partial(scatter_kernel, picks, len(base)), out_s...  1.65 us
    ppermute x3, starting transfers between devices, swap_faces(): return lax.ppermute(face, axis, pair_swaps(size, offset))  1.33 us
    pallas_call x1, Pallas kernels, pack(): pl.pallas_call(pack_kernel, out_shape=(message, message, pltpu.VMEM((1, 8...  1.06 us
    ppermute x3, waiting for transfers between devices, swap_faces(): return lax.ppermute(face, axis, pair_swaps(size, offset))  1 us
  transfers between devices with their start and end apart: 12, of which 3 were waited for; matrix products, arithmetic and copies ran while one was open for 0% of the time, Pallas kernels for 11%

profile of v3, /device:TPU:10, one launch (start us, length us, event | category | flops | bytes accessed | tf_op | source)
XLA Modules:
  0.0 21.1 jit_solution(2945460703992778497)
XLA Ops:
  0.6 1.1 %pack.1 = (f32[9,8,128]{2,1,0:T(8,128)S(1)}, f32[9,8,128]{2,1,0:T(8,128)S(1)}, f32[1,8,128]{2,1,0:T(8,128)S(1)}, f32[8,8,512]{2,1,0:T(8,128)S(1)}) custom-call(f32[8,8,512]{2,1,0:T(8,128)} %cur_ref.1, f32[2,256]{1,0:T(2,128)} %res_ref.1, s32[2,128]{1,0:T(2,128)} %bitcast.2, s32[2,128]{1,0:T(2,128)} %bitcast.3), custom_call_target="tpu_custom_call" | custom-call | tf_op jit(solution)/shard_map/pack/pallas_call | solution.py:76
  1.7 0.6 %collective-permute-start.1 = (f32[9,8,128]{2,1,0:T(8,128)S(1)}, f32[9,8,128]{2,1,0:T(8,128)S(1)}, u32[]{:S(2)}, u32[]{:S(2)}) collective-permute-start(f32[9,8,128]{2,1,0:T(8,128)S(1)} %get-tuple-element.27), channel_id=1, source_target_pairs={{0,4},{4,0},{8,12},{12,8},{1,5},{5,1},{9,13},{13,9},{2,6},{6,2},{1... | collective-permute-start | bytes 110600 | tf_op jit(solution)/shard_map/ppermute | solution.py:348
  2.3 2.4 %collective-permute-start.2 = (f32[9,8,128]{2,1,0:T(8,128)S(1)}, f32[9,8,128]{2,1,0:T(8,128)S(1)}, u32[]{:S(2)}, u32[]{:S(2)}) collective-permute-start(f32[9,8,128]{2,1,0:T(8,128)S(1)} %get-tuple-element.28), channel_id=1, source_target_pairs={{0,12},{4,8},{8,4},{12,0},{1,13},{5,9},{9,5},{13,1},{2,14},{6,10},... | collective-permute-start | bytes 110600 | tf_op jit(solution)/shard_map/ppermute | solution.py:349
  4.7 0.5 %collective-permute-start = (f32[1,8,128]{2,1,0:T(8,128)S(1)}, f32[1,8,128]{2,1,0:T(8,128)S(1)}, u32[]{:S(2)}, u32[]{:S(2)}) collective-permute-start(f32[1,8,128]{2,1,0:T(8,128)S(1)} %get-tuple-element.26.refs_0_), channel_id=1, source_target_pairs={{0,8},{4,12},{8,0},{12,4},{1,9},{5,13},{9,1},{13,5},{2,10},{6,14},... | collective-permute-start | bytes 12296 | tf_op jit(solution)/shard_map/ppermute | solution.py:350
  5.3 0.5 %collective-permute-start.5 = (f32[4,8,512]{2,1,0:T(8,128)S(1)}, f32[4,8,512]{2,1,0:T(8,128)S(1)}, u32[]{:S(2)}, u32[]{:S(2)}) collective-permute-start(f32[4,8,512]{2,1,0:T(8,128)S(1)} %get-tuple-element.32), channel_id=1, source_target_pairs={{0,1},{1,0},{2,3},{3,2},{4,5},{5,4},{6,7},{7,6},{8,9},{9,8},{10,11... | collective-permute-start | bytes 196616 | tf_op jit(solution)/shard_map/ppermute | solution.py:333
  5.8 2.7 %collective-permute-start.6 = (f32[4,8,512]{2,1,0:T(8,128)S(1)}, f32[4,8,512]{2,1,0:T(8,128)S(1)}, u32[]{:S(2)}, u32[]{:S(2)}) collective-permute-start(f32[4,8,512]{2,1,0:T(8,128)S(1)} %get-tuple-element.33), channel_id=1, source_target_pairs={{0,16},{1,2},{2,1},{3,19},{16,0},{17,18},{18,17},{19,3},{4,20},{5,... | collective-permute-start | bytes 196616 | tf_op jit(solution)/shard_map/ppermute | solution.py:334
  8.5 0.0 collective-permute-done.refs_1_
  8.5 0.0 collective-permute-done.1.refs_2_.even_ref
  8.5 0.0 collective-permute-done.2.refs_3_.odd_ref
  8.5 0.1 collective-permute-start.4
  8.6 0.5 %collective-permute-start.3 = (f32[4,8,128]{2,1,0:T(8,128)S(1)}, f32[4,8,128]{2,1,0:T(8,128)S(1)}, u32[]{:S(2)}, u32[]{:S(2)}) collective-permute-start(f32[4,8,128]{2,1,0:T(8,128)S(1)} %gather_blocks.1), channel_id=1, source_target_pairs={{0,16},{16,0},{1,17},{17,1},{2,18},{18,2},{3,19},{19,3},{4,20},{20... | collective-permute-start | bytes 49160 | tf_op jit(solution)/shard_map/ppermute | solution.py:357
  9.1 0.8 %scatter.2.refs_4_ = f32[2,8,8,512]{3,2,1,0:T(8,128)S(1)} custom-call(f32[1,8,128]{2,1,0:T(8,128)S(1)} %get-tuple-element.26.refs_0_, f32[1,8,128]{2,1,0:T(8,128)S(1)} %collective-permute-done.refs_1_, f32[9,8,128]{2,1,0:T(8,128)S(1)} %collective-permute-done.1.refs_2_.even_ref, f32[9,8,128]{2,1,0:T(8,128)S(1)} %collective-permute-done.2.refs_3_.odd_ref), custom_call_target="tpu_custom_call" | custom-call | tf_op jit(solution)/shard_map/scatter/pallas_call | solution.py:139
  9.9 0.0 copy-start
  9.9 0.0 copy-start.2
  10.0 0.0 collective-permute-done.3.refs_0_.refs_1_.refs_2_.refs_3_
  10.0 0.8 %scatter.3.src_ref = f32[2,8,8,512]{3,2,1,0:T(8,128)S(1)} custom-call(f32[4,8,128]{2,1,0:T(8,128)S(1)} %collective-permute-done.3.refs_0_.refs_1_.refs_2_.refs_3_, f32[4,8,128]{2,1,0:T(8,128)S(1)} %collective-permute-done.3.refs_0_.refs_1_.refs_2_.refs_3_, f32[4,8,128]{2,1,0:T(8,128)S(1)} %collective-permute-done.3.refs_0_.refs_1_.refs_2_.refs_3_, ...), custom_call_target="tpu_custom_call" | custom-call | tf_op jit(solution)/shard_map/scatter/pallas_call | solution.py:139
  10.8 0.0 collective-permute-done.5.refs_1_
  10.8 0.0 collective-permute-done.6.refs_2_
  10.8 0.0 collective-permute-done.4.refs_0_
  10.8 0.0 copy-done
  10.8 0.1 copy-done.2
  10.9 0.4 %first_step.1 = (f32[8,8,512]{2,1,0:T(8,128)S(1)}, f32[8,8,128]{2,1,0:T(8,128)S(1)}, f32[8,8,128]{2,1,0:T(8,128)S(1)}) custom-call(f32[8,8,512]{2,1,0:T(8,128)S(1)} %get-tuple-element.25.cur_ref.prev_ref, f32[8,8,512]{2,1,0:T(8,128)S(1)} %copy-done.2, f32[8,8,512]{2,1,0:T(8,128)S(1)} %copy-done, f32[2,8,8,512]{3,2,1,0:T(8,128)S(1)} %scatter.3.src_ref, ...), custom_call_target="tpu_custom_call" | custom-call | tf_op jit(solution)/shard_map/first_step/pallas_call | solution.py:298
  11.3 0.3 %collective-permute-start.7 = (f32[4,8,512]{2,1,0:T(8,128)S(1)}, f32[4,8,512]{2,1,0:T(8,128)S(1)}, u32[]{:S(2)}, u32[]{:S(2)}) collective-permute-start(f32[4,8,512]{2,1,0:T(8,128)S(1)} %get-tuple-element.35), channel_id=1, source_target_pairs={{0,16},{16,0},{1,17},{17,1},{2,18},{18,2},{3,19},{19,3},{4,20},{20... | collective-permute-start | bytes 196616 | tf_op jit(solution)/shard_map/ppermute | solution.py:339
  11.7 0.3 %collective-permute-start.8 = (f32[4,8,512]{2,1,0:T(8,128)S(1)}, f32[4,8,512]{2,1,0:T(8,128)S(1)}, u32[]{:S(2)}, u32[]{:S(2)}) collective-permute-start(f32[4,8,512]{2,1,0:T(8,128)S(1)} %get-tuple-element.36), channel_id=1, source_target_pairs={{0,1},{1,0},{2,3},{3,2},{4,5},{5,4},{6,7},{7,6},{8,9},{9,8},{10,11... | collective-permute-start | bytes 196616 | tf_op jit(solution)/shard_map/ppermute | solution.py:333
  12.0 2.7 %collective-permute-start.9 = (f32[4,8,512]{2,1,0:T(8,128)S(1)}, f32[4,8,512]{2,1,0:T(8,128)S(1)}, u32[]{:S(2)}, u32[]{:S(2)}) collective-permute-start(f32[4,8,512]{2,1,0:T(8,128)S(1)} %get-tuple-element.37), channel_id=1, source_target_pairs={{0,16},{1,2},{2,1},{3,19},{16,0},{17,18},{18,17},{19,3},{4,20},{5,... | collective-permute-start | bytes 196616 | tf_op jit(solution)/shard_map/ppermute | solution.py:334
  14.7 0.5 %collective-permute-start.10 = (f32[8,8,128]{2,1,0:T(8,128)S(1)}, f32[8,8,128]{2,1,0:T(8,128)S(1)}, u32[]{:S(2)}, u32[]{:S(2)}) collective-permute-start(f32[8,8,128]{2,1,0:T(8,128)S(1)} %get-tuple-element.43), channel_id=1, source_target_pairs={{0,4},{4,0},{8,12},{12,8},{1,5},{5,1},{9,13},{13,9},{2,6},{6,2},{1... | collective-permute-start | bytes 98312 | tf_op jit(solution)/shard_map/ppermute | solution.py:333
  15.2 1.4 %collective-permute-start.11 = (f32[8,8,128]{2,1,0:T(8,128)S(1)}, f32[8,8,128]{2,1,0:T(8,128)S(1)}, u32[]{:S(2)}, u32[]{:S(2)}) collective-permute-start(f32[8,8,128]{2,1,0:T(8,128)S(1)} %get-tuple-element.44), channel_id=1, source_target_pairs={{0,16},{4,8},{8,4},{12,28},{16,0},{20,24},{24,20},{28,12},{1,17},{... | collective-permute-start | bytes 98312 | tf_op jit(solution)/shard_map/ppermute | solution.py:334
  16.6 0.3 %collective-permute-done.9.refs_2_ = f32[4,8,512]{2,1,0:T(8,128)S(1)} collective-permute-done((f32[4,8,512]{2,1,0:T(8,128)S(1)}, f32[4,8,512]{2,1,0:T(8,128)S(1)}, u32[]{:S(2)}, u32[]{:S(2)}) %collective-permute-start.9) | collective-permute-done | bytes 65568 | tf_op jit(solution)/shard_map/ppermute | solution.py:334
  16.9 0.7 %second_start.1 = (f32[8,8,512]{2,1,0:T(8,128)}, f32[8,8,512]{2,1,0:T(8,128)S(1)}, f32[8,8,512]{2,1,0:T(8,128)S(1)}, f32[8,8,512]{2,1,0:T(8,128)S(1)}, f32[8,8,512]{2,1,0:T(8,128)S(1)}) custom-call(f32[8,8,512]{2,1,0:T(8,128)S(1)} %get-tuple-element.34.cur_ref, f32[8,8,512]{2,1,0:T(8,128)S(1)} %get-tuple-element.25.cur_ref.prev_ref, ...), custom_call_target="tpu_custom_call" | custom-call | tf_op jit(solution)/shard_map/second_start/pallas_call | solution.py:298
  17.6 1.0 %collective-permute-done.10.even_ref = f32[8,8,128]{2,1,0:T(8,128)S(1)} collective-permute-done((f32[8,8,128]{2,1,0:T(8,128)S(1)}, f32[8,8,128]{2,1,0:T(8,128)S(1)}, u32[]{:S(2)}, u32[]{:S(2)}) %collective-permute-start.10) | collective-permute-done | bytes 32800 | tf_op jit(solution)/shard_map/ppermute | solution.py:333
  18.6 1.4 %collective-permute-done.11.odd_ref = f32[8,8,128]{2,1,0:T(8,128)S(1)} collective-permute-done((f32[8,8,128]{2,1,0:T(8,128)S(1)}, f32[8,8,128]{2,1,0:T(8,128)S(1)}, u32[]{:S(2)}, u32[]{:S(2)}) %collective-permute-start.11) | collective-permute-done | bytes 32800 | tf_op jit(solution)/shard_map/ppermute | solution.py:334
  20.0 1.0 %second_end.1 = (f32[8,8,512]{2,1,0:T(8,128)}, f32[8,8,512]{2,1,0:T(8,128)}) custom-call(f32[8,8,512]{2,1,0:T(8,128)S(1)} %get-tuple-element.34.cur_ref, f32[8,8,512]{2,1,0:T(8,128)S(1)} %get-tuple-element.39.part_ref, f32[8,8,512]{2,1,0:T(8,128)S(1)} %get-tuple-element.40.speed_ref, f32[8,8,512]{2,1,0:T(8,128)S(1)} %get-tuple-element.41.sum_ref, ...), custom_call_target="tpu_custom_call" | custom-call | tf_op jit(solution)/shard_map/second_end/pallas_call | solution.py:298
  (7 shorter events, 0.1 us)
Async XLA Ops:
  1.7 6.8 %collective-permute-start.1 = (f32[9,8,128]{2,1,0:T(8,128)S(1)}, f32[9,8,128]{2,1,0:T(8,128)S(1)}, u32[]{:S(2)}, u32[]{:S(2)}) collective-permute-start(f32[9,8,128]{2,1,0:T(8,128)S(1)} %get-tuple-element.27), channel_id=1, source_target_pairs={{0,4},{4,0},{8,12},{12,8},{1,5},{5,1},{9,13},{13,9},{2,6},{6,2},{1... | collective-permute-start | bytes 110600 | tf_op jit(solution)/shard_map/ppermute | solution.py:348
  2.3 6.2 %collective-permute-start.2 = (f32[9,8,128]{2,1,0:T(8,128)S(1)}, f32[9,8,128]{2,1,0:T(8,128)S(1)}, u32[]{:S(2)}, u32[]{:S(2)}) collective-permute-start(f32[9,8,128]{2,1,0:T(8,128)S(1)} %get-tuple-element.28), channel_id=1, source_target_pairs={{0,12},{4,8},{8,4},{12,0},{1,13},{5,9},{9,5},{13,1},{2,14},{6,10},... | collective-permute-start | bytes 110600 | tf_op jit(solution)/shard_map/ppermute | solution.py:349
  4.7 3.8 %collective-permute-start = (f32[1,8,128]{2,1,0:T(8,128)S(1)}, f32[1,8,128]{2,1,0:T(8,128)S(1)}, u32[]{:S(2)}, u32[]{:S(2)}) collective-permute-start(f32[1,8,128]{2,1,0:T(8,128)S(1)} %get-tuple-element.26.refs_0_), channel_id=1, source_target_pairs={{0,8},{4,12},{8,0},{12,4},{1,9},{5,13},{9,1},{13,5},{2,10},{6,14},... | collective-permute-start | bytes 12296 | tf_op jit(solution)/shard_map/ppermute | solution.py:350
  5.3 5.5 %collective-permute-start.5 = (f32[4,8,512]{2,1,0:T(8,128)S(1)}, f32[4,8,512]{2,1,0:T(8,128)S(1)}, u32[]{:S(2)}, u32[]{:S(2)}) collective-permute-start(f32[4,8,512]{2,1,0:T(8,128)S(1)} %get-tuple-element.32), channel_id=1, source_target_pairs={{0,1},{1,0},{2,3},{3,2},{4,5},{5,4},{6,7},{7,6},{8,9},{9,8},{10,11... | collective-permute-start | bytes 196616 | tf_op jit(solution)/shard_map/ppermute | solution.py:333
  5.8 5.0 %collective-permute-start.6 = (f32[4,8,512]{2,1,0:T(8,128)S(1)}, f32[4,8,512]{2,1,0:T(8,128)S(1)}, u32[]{:S(2)}, u32[]{:S(2)}) collective-permute-start(f32[4,8,512]{2,1,0:T(8,128)S(1)} %get-tuple-element.33), channel_id=1, source_target_pairs={{0,16},{1,2},{2,1},{3,19},{16,0},{17,18},{18,17},{19,3},{4,20},{5,... | collective-permute-start | bytes 196616 | tf_op jit(solution)/shard_map/ppermute | solution.py:334
  8.5 2.3 %collective-permute-start.4 = (f32[4,8,512]{2,1,0:T(8,128)S(1)}, f32[4,8,512]{2,1,0:T(8,128)S(1)}, u32[]{:S(2)}, u32[]{:S(2)}) collective-permute-start(f32[4,8,512]{2,1,0:T(8,128)S(1)} %get-tuple-element.31), channel_id=1, source_target_pairs={{0,16},{16,0},{1,17},{17,1},{2,18},{18,2},{3,19},{19,3},{4,20},{20... | collective-permute-start | bytes 196616 | tf_op jit(solution)/shard_map/ppermute | solution.py:339
  8.6 1.4 %collective-permute-start.3 = (f32[4,8,128]{2,1,0:T(8,128)S(1)}, f32[4,8,128]{2,1,0:T(8,128)S(1)}, u32[]{:S(2)}, u32[]{:S(2)}) collective-permute-start(f32[4,8,128]{2,1,0:T(8,128)S(1)} %gather_blocks.1), channel_id=1, source_target_pairs={{0,16},{16,0},{1,17},{17,1},{2,18},{18,2},{3,19},{19,3},{4,20},{20... | collective-permute-start | bytes 49160 | tf_op jit(solution)/shard_map/ppermute | solution.py:357
  9.9 0.9 %copy-start = (f32[8,8,512]{2,1,0:T(8,128)S(1)}, f32[8,8,512]{2,1,0:T(8,128)}, u32[]{:S(2)}) copy-start(f32[8,8,512]{2,1,0:T(8,128)} %vel_ref.3) | copy-start | bytes 393220
  9.9 1.0 %copy-start.2 = (f32[8,8,512]{2,1,0:T(8,128)S(1)}, f32[8,8,512]{2,1,0:T(8,128)}, u32[]{:S(2)}) copy-start(f32[8,8,512]{2,1,0:T(8,128)} %prev_ref.1) | copy-start | bytes 393220
  10.9 6.0 %copy-start.1 = (f32[2,8,8,512]{3,2,1,0:T(8,128)S(1)}, f32[2,8,8,512]{3,2,1,0:T(8,128)}, u32[]{:S(2)}) copy-start(f32[2,8,8,512]{3,2,1,0:T(8,128)} %accel_ref.1) | copy-start | bytes 786436
  11.3 5.3 %collective-permute-start.7 = (f32[4,8,512]{2,1,0:T(8,128)S(1)}, f32[4,8,512]{2,1,0:T(8,128)S(1)}, u32[]{:S(2)}, u32[]{:S(2)}) collective-permute-start(f32[4,8,512]{2,1,0:T(8,128)S(1)} %get-tuple-element.35), channel_id=1, source_target_pairs={{0,16},{16,0},{1,17},{17,1},{2,18},{18,2},{3,19},{19,3},{4,20},{20... | collective-permute-start | bytes 196616 | tf_op jit(solution)/shard_map/ppermute | solution.py:339
  11.7 5.0 %collective-permute-start.8 = (f32[4,8,512]{2,1,0:T(8,128)S(1)}, f32[4,8,512]{2,1,0:T(8,128)S(1)}, u32[]{:S(2)}, u32[]{:S(2)}) collective-permute-start(f32[4,8,512]{2,1,0:T(8,128)S(1)} %get-tuple-element.36), channel_id=1, source_target_pairs={{0,1},{1,0},{2,3},{3,2},{4,5},{5,4},{6,7},{7,6},{8,9},{9,8},{10,11... | collective-permute-start | bytes 196616 | tf_op jit(solution)/shard_map/ppermute | solution.py:333
  12.0 5.0 %collective-permute-start.9 = (f32[4,8,512]{2,1,0:T(8,128)S(1)}, f32[4,8,512]{2,1,0:T(8,128)S(1)}, u32[]{:S(2)}, u32[]{:S(2)}) collective-permute-start(f32[4,8,512]{2,1,0:T(8,128)S(1)} %get-tuple-element.37), channel_id=1, source_target_pairs={{0,16},{1,2},{2,1},{3,19},{16,0},{17,18},{18,17},{19,3},{4,20},{5,... | collective-permute-start | bytes 196616 | tf_op jit(solution)/shard_map/ppermute | solution.py:334
  14.7 3.9 %collective-permute-start.10 = (f32[8,8,128]{2,1,0:T(8,128)S(1)}, f32[8,8,128]{2,1,0:T(8,128)S(1)}, u32[]{:S(2)}, u32[]{:S(2)}) collective-permute-start(f32[8,8,128]{2,1,0:T(8,128)S(1)} %get-tuple-element.43), channel_id=1, source_target_pairs={{0,4},{4,0},{8,12},{12,8},{1,5},{5,1},{9,13},{13,9},{2,6},{6,2},{1... | collective-permute-start | bytes 98312 | tf_op jit(solution)/shard_map/ppermute | solution.py:333
  15.2 4.8 %collective-permute-start.11 = (f32[8,8,128]{2,1,0:T(8,128)S(1)}, f32[8,8,128]{2,1,0:T(8,128)S(1)}, u32[]{:S(2)}, u32[]{:S(2)}) collective-permute-start(f32[8,8,128]{2,1,0:T(8,128)S(1)} %get-tuple-element.44), channel_id=1, source_target_pairs={{0,16},{4,8},{8,4},{12,28},{16,0},{20,24},{24,20},{28,12},{1,17},{... | collective-permute-start | bytes 98312 | tf_op jit(solution)/shard_map/ppermute | solution.py:334

commit v4 on v3

--- a/solution.py
+++ b/solution.py
@@ -39,7 +39,7 @@
     return [(i, i ^ bits) for i in range(size)]
 
 
-def pack_kernel(cur_ref, res_ref, tile_ref, cell_ref, even_ref, odd_ref, own_ref, copy_ref, res, tile, cell, sem):
+def pack_kernel(cur_ref, res_ref, tile_ref, cell_ref, even_ref, odd_ref, own_ref, res, tile, cell, sem):
     is_odd = lax.rem(lax.axis_index("gy"), 2)
     last = cur_ref.shape[2] - LANES
     start_even = pl.multiple_of((1 - is_odd) * last, LANES)
@@ -51,7 +51,6 @@
         (cell_ref, cell),
         (cur_ref.at[:, :, pl.ds(start_even, LANES)], even_ref.at[0:size_x]),
         (cur_ref.at[:, :, pl.ds(start_odd, LANES)], odd_ref.at[0:size_x]),
-        (cur_ref, copy_ref),
     )
     copies = [pltpu.make_async_copy(*pair, sem.at[i]) for i, pair in enumerate(pairs)]
     for copy in copies:
@@ -75,14 +74,14 @@
     message = pltpu.VMEM((size_x + 1, size_z, LANES), F32)
     return pl.pallas_call(
         pack_kernel,
-        out_shape=(message, message, pltpu.VMEM((1, 8, LANES), F32), pltpu.VMEM(cur.shape, F32)),
+        out_shape=(message, message, pltpu.VMEM((1, 8, LANES), F32)),
         in_specs=[pl.BlockSpec(memory_space=pl.ANY)] * 4,
-        out_specs=(VMEM,) * 4,
+        out_specs=(VMEM,) * 3,
         scratch_shapes=[
             pltpu.VMEM(residuals.shape, F32),
             pltpu.VMEM(tile.shape, jnp.int32),
             pltpu.VMEM(cell.shape, jnp.int32),
-            pltpu.SemaphoreType.DMA((6,)),
+            pltpu.SemaphoreType.DMA((5,)),
         ],
         name="pack",
     )(cur, residuals, tile, cell)
@@ -92,17 +91,20 @@
     size_x, size_z, size_y = shape
     rows = size_x * size_z
     mine = (lax.axis_index("gx") * lax.axis_size("gy") + lax.axis_index("gy")).astype(F32)
-    row_iota = lax.broadcasted_iota(jnp.int32, (rows, LANES), 0)
-    column_iota = lax.broadcasted_iota(jnp.int32, (size_y, LANES), 0)
+    row_iota = lax.broadcasted_iota(jnp.int32, (rows, LANES), 0).astype(BF16)
+    group = min(size_y, 256)
+    column_iota = lax.broadcasted_iota(jnp.int32, (group, LANES), 0).astype(BF16)
+    one, zero = jnp.ones((), BF16), jnp.zeros((), BF16)
     place = 0
     for block in blocks:
         cell = block[6:8].astype(jnp.int32)
         column = lax.rem(cell, size_y)
         row = jnp.where(block[4:6] == mine, lax.div(cell, size_y), -1)
-        high = block[0:4].astype(BF16).astype(F32)
-        rest = block[0:4] - high
-        middle = rest.astype(BF16).astype(F32)
-        low = rest - middle
+        row = row.astype(BF16)
+        high = block[0:4].astype(BF16)
+        rest = block[0:4] - high.astype(F32)
+        middle = rest.astype(BF16)
+        low = (rest - middle.astype(F32)).astype(BF16)
         for half in range(2):
             lanes = slice(place, place + LANES)
             hit = row_iota == row[half : half + 1]
@@ -110,8 +112,10 @@
                 line = 2 * moment + half
                 for piece, value in enumerate((high, middle, low)):
                     top = (3 * moment + piece) * rows
-                    left_ref[top : top + rows, lanes] = jnp.where(hit, value[line : line + 1], 0.0).astype(BF16)
-            right_ref[:, lanes] = jnp.where(column_iota == column[half : half + 1], 1.0, 0.0).astype(BF16)
+                    left_ref[top : top + rows, lanes] = jnp.where(hit, value[line : line + 1], zero)
+            for start in range(0, size_y, group):
+                there = column_iota == (column[half : half + 1] - start).astype(BF16)
+                right_ref[start : start + group, lanes] = jnp.where(there, one, zero)
             place += LANES
     total = lax.dot_general(
         left_ref[...], right_ref[...], (((1,), (1,)), ((), ())), preferred_element_type=F32
@@ -199,7 +203,9 @@
     lane = lax.broadcasted_iota(jnp.int32, (size_x, size_z, LANES), 2)
     ends = []
     for before in (True, False):
-        face = pick_side([ref[0:size_x] for ref in y_refs], is_odd, before)
+        width = y_refs[0].shape[2]
+        nearest = slice(width - LANES, width) if before else slice(0, LANES)
+        face = pick_side([ref[0:size_x, :, nearest] for ref in y_refs], is_odd, before)
         ends.append(jnp.where(place == (0 if before else count_y - 1), 0.0, face))
     wheres = column_blocks(size_y)
     columns = [ends[0]] + [cur_ref[:, :, where] for where in wheres] + [ends[1]]
@@ -254,18 +260,17 @@
             2.0 * centre - prev_ref[:, :, where] + scaled * scaled * (total + more) + src_ref[0, :, :, where]
         )
     is_odd = lax.rem(lax.axis_index("gy"), 2) == 1
-    first, last = next_ref[:, :, 0:LANES], next_ref[:, :, next_ref.shape[2] - LANES :]
+    width = even_out.shape[2]
+    first, last = next_ref[:, :, 0:width], next_ref[:, :, next_ref.shape[2] - width :]
     even_out[...] = jnp.where(is_odd, first, last)
     odd_out[...] = jnp.where(is_odd, last, first)
 
 
-def second_start_kernel(counts, cur_ref, prev_ref, vel_ref, src_ref, accel_ref, *refs):
-    count_x, count_z, _ = counts
-    x_refs, z_refs, refs = refs[:count_x], refs[count_x : count_x + 2], refs[count_x + 2 :]
+def second_start_kernel(counts, cur_ref, prev_ref, vel_ref, src_ref, accel_ref, even_ref, odd_ref, *refs):
     out_ref, part_ref, speed_ref, sum_ref, factor_ref, sem = refs
     copy = pltpu.make_async_copy(cur_ref, out_ref, sem)
     copy.start()
-    for where, centre, laplacian in across_columns(count_z, cur_ref, x_refs, z_refs):
+    for where, centre, laplacian in along_columns(counts[2], cur_ref, (even_ref, odd_ref)):
         velocity = vel_ref[:, :, where]
         scaled = velocity * courant_scale
         speed_sq = scaled * scaled
@@ -278,11 +283,13 @@
 
 
 def second_end_kernel(
-    counts, cur_ref, part_ref, speed_ref, sum_ref, factor_ref, even_ref, odd_ref,
-    next_out, gradient_out, next_ref, gradient_ref, sem,
+    counts, cur_ref, part_ref, speed_ref, sum_ref, factor_ref, *refs
 ):
+    count_x, count_z, _ = counts
+    x_refs, z_refs, refs = refs[:count_x], refs[count_x : count_x + 2], refs[count_x + 2 :]
+    next_out, gradient_out, next_ref, gradient_ref, sem = refs
     copies = []
-    for place, (where, _, laplacian) in enumerate(along_columns(counts[2], cur_ref, (even_ref, odd_ref))):
+    for place, (where, _, laplacian) in enumerate(across_columns(count_z, cur_ref, x_refs, z_refs)):
         advanced = part_ref[:, :, where] + speed_ref[:, :, where] * laplacian
         next_ref[place] = advanced
         gradient_ref[place] = sum_ref[:, :, where] + factor_ref[:, :, where] * advanced
@@ -341,7 +348,8 @@
     def halos_z(faces):
         return [swap_faces(face, "gz", count_z, offset) for offset, face in enumerate(faces)]
 
-    even_face, odd_face, own, current = pack(
+    current = adj_cur
+    even_face, odd_face, own = pack(
         adj_cur, residuals, target.reshape(2, LANES), recv_cell.reshape(2, LANES)
     )
     if count_x == 2 and count_y == 4:
@@ -365,7 +373,7 @@
         parts = bucketed(residuals, target, recv_cell, count_x * count_y)
         source = scatter([parts] * parts.shape[0], tuple(range(parts.shape[0])), shape)
     counts = (messages_x, count_z, count_y)
-    field, face = pltpu.VMEM(shape, F32), pltpu.VMEM(shape[:2] + (LANES,), F32)
+    field, face = pltpu.VMEM(shape, F32), pltpu.VMEM(shape[:2] + (2 * LANES,), F32)
     whole = jax.ShapeDtypeStruct(shape, F32)
     advanced, even_face, odd_face = call(
         functools.partial(first_kernel, counts),
@@ -380,7 +388,7 @@
     first, *parts = call(
         functools.partial(second_start_kernel, counts),
         "second_start",
-        [advanced, current, velocity, source, fwd_accel, *along_x, *along_z],
+        [advanced, current, velocity, source, fwd_accel, even, odd],
         [whole, field, field, field, field],
         [pltpu.SemaphoreType.DMA],
     )
@@ -389,7 +397,7 @@
     latest, gradient = call(
         functools.partial(second_end_kernel, counts),
         "second_end",
-        [advanced, *parts, even, odd],
+        [advanced, *parts, *along_x, *along_z],
         [whole, whole],
         [tiles, tiles, pltpu.SemaphoreType.DMA((2 * blocks,))],
     )

time: 21.2 us -> 20.2 us (0.953); the launches traced: 21.1 us -> 19.9 us
  Pallas kernels: 4.86 us -> 4.23 us
  waiting for transfers between devices: 2.72 us -> 2.2 us
    ppermute x3, waiting for transfers between devices: 1 us -> 0.3 us  [swap_faces(): return lax.ppermute(face, axis, pair_swaps(size, offset))]
    ppermute x3, starting transfers between devices: 6.85 us -> 7.24 us  [swap_faces(): return lax.ppermute(face, ('gx', axis), full_swaps(count_x, size, offset))]
    pallas_call x2, Pallas kernels: 1.65 us -> 1.31 us  [scatter(): pl.pallas_call(functools.partial(scatter_kernel, picks, len(base)), out_s...]
    ppermute x2, starting transfers between devices: 0.42 us -> 0.14 us  [halos_x(): lax.ppermute(face, 'gx', pair_swaps(count_x, offset))]
  transfers between devices with their start and end apart: 12 -> 12, of which waited for: 3 -> 5; matrix products, arithmetic and copies ran while one was open for 0% -> 0% of each run, Pallas kernels for 11% -> 10%
where the time goes in v4:
time: 20.2 us; the launch traced here: 19.9 us
  starting transfers between devices  12.6 us (62%)
  Pallas kernels  4.23 us (21%)
  waiting for transfers between devices  2.2 us (11%)
  between operations  0.77 us (4%)
    ppermute x3, starting transfers between devices, swap_faces(): return lax.ppermute(face, ('gx', axis), full_swaps(count_x, size, offset))  7.24 us
    ppermute x1, starting transfers between devices, shards(): odd = lax.ppermute(odd_face, 'gy', xor_swaps(4, 3))  2.45 us
    pallas_call x5, Pallas kernels, call(): pl.pallas_call(kernel, out_shape=tuple(outputs), in_specs=[VMEM] * len(op...  2.01 us
    ppermute x3, waiting for transfers between devices, swap_faces(): return lax.ppermute(face, ('gx', axis), full_swaps(count_x, size, offset))  1.74 us
    pallas_call x2, Pallas kernels, scatter(): pl.pallas_call(functools.partial(scatter_kernel, picks, len(base)), out_s...  1.31 us
    ppermute x3, starting transfers between devices, swap_faces(): return lax.ppermute(face, axis, pair_swaps(size, offset))  1.19 us
    pallas_call x1, Pallas kernels, pack(): pl.pallas_call(pack_kernel, out_shape=(message, message, pltpu.VMEM((1, 8...  0.9 us
    ppermute x1, starting transfers between devices, shards(): even = lax.ppermute(even_face, 'gy', xor_swaps(4, 1))  0.6 us
  transfers between devices with their start and end apart: 12, of which 5 were waited for; matrix products, arithmetic and copies ran while one was open for 0% of the time, Pallas kernels for 10%

profile of v4, /device:TPU:10, one launch (start us, length us, event | category | flops | bytes accessed | tf_op | source)
XLA Modules:
  0.0 19.9 jit_solution(5931843264655966202)
XLA Ops:
  0.6 0.9 %pack.1 = (f32[9,8,128]{2,1,0:T(8,128)S(1)}, f32[9,8,128]{2,1,0:T(8,128)S(1)}, f32[1,8,128]{2,1,0:T(8,128)S(1)}) custom-call(f32[8,8,512]{2,1,0:T(8,128)} %prev_ref.3, f32[2,256]{1,0:T(2,128)} %res_ref.1, s32[2,128]{1,0:T(2,128)} %bitcast.2, s32[2,128]{1,0:T(2,128)} %bitcast.3), custom_call_target="tpu_custom_call" | custom-call | tf_op jit(solution)/shard_map/pack/pallas_call | solution.py:75
  1.6 0.6 %collective-permute-start.1 = (f32[9,8,128]{2,1,0:T(8,128)S(1)}, f32[9,8,128]{2,1,0:T(8,128)S(1)}, u32[]{:S(2)}, u32[]{:S(2)}) collective-permute-start(f32[9,8,128]{2,1,0:T(8,128)S(1)} %get-tuple-element.25), channel_id=1, source_target_pairs={{0,4},{4,0},{8,12},{12,8},{1,5},{5,1},{9,13},{13,9},{2,6},{6,2},{1... | collective-permute-start | bytes 110600 | tf_op jit(solution)/shard_map/ppermute | solution.py:356
  2.2 2.4 %collective-permute-start.2 = (f32[9,8,128]{2,1,0:T(8,128)S(1)}, f32[9,8,128]{2,1,0:T(8,128)S(1)}, u32[]{:S(2)}, u32[]{:S(2)}) collective-permute-start(f32[9,8,128]{2,1,0:T(8,128)S(1)} %get-tuple-element.26), channel_id=1, source_target_pairs={{0,12},{4,8},{8,4},{12,0},{1,13},{5,9},{9,5},{13,1},{2,14},{6,10},... | collective-permute-start | bytes 110600 | tf_op jit(solution)/shard_map/ppermute | solution.py:357
  4.6 0.5 %collective-permute-start = (f32[1,8,128]{2,1,0:T(8,128)S(1)}, f32[1,8,128]{2,1,0:T(8,128)S(1)}, u32[]{:S(2)}, u32[]{:S(2)}) collective-permute-start(f32[1,8,128]{2,1,0:T(8,128)S(1)} %get-tuple-element.24.refs_0_), channel_id=1, source_target_pairs={{0,8},{4,12},{8,0},{12,4},{1,9},{5,13},{9,1},{13,5},{2,10},{6,14},... | collective-permute-start | bytes 12296 | tf_op jit(solution)/shard_map/ppermute | solution.py:358
  5.1 0.5 %collective-permute-start.5 = (f32[4,8,512]{2,1,0:T(8,128)S(1)}, f32[4,8,512]{2,1,0:T(8,128)S(1)}, u32[]{:S(2)}, u32[]{:S(2)}) collective-permute-start(f32[4,8,512]{2,1,0:T(8,128)S(1)} %get-tuple-element.30), channel_id=1, source_target_pairs={{0,1},{1,0},{2,3},{3,2},{4,5},{5,4},{6,7},{7,6},{8,9},{9,8},{10,11... | collective-permute-start | bytes 196616 | tf_op jit(solution)/shard_map/ppermute | solution.py:340
  5.7 2.7 %collective-permute-start.6 = (f32[4,8,512]{2,1,0:T(8,128)S(1)}, f32[4,8,512]{2,1,0:T(8,128)S(1)}, u32[]{:S(2)}, u32[]{:S(2)}) collective-permute-start(f32[4,8,512]{2,1,0:T(8,128)S(1)} %get-tuple-element.31), channel_id=1, source_target_pairs={{0,16},{1,2},{2,1},{3,19},{16,0},{17,18},{18,17},{19,3},{4,20},{5,... | collective-permute-start | bytes 196616 | tf_op jit(solution)/shard_map/ppermute | solution.py:341
  8.4 0.0 collective-permute-done.refs_1_
  8.4 0.0 collective-permute-done.1.refs_2_.even_ref
  8.4 0.0 collective-permute-done.2.refs_3_.odd_ref
  8.4 0.1 collective-permute-start.4
  8.5 0.5 %collective-permute-start.3 = (f32[4,8,128]{2,1,0:T(8,128)S(1)}, f32[4,8,128]{2,1,0:T(8,128)S(1)}, u32[]{:S(2)}, u32[]{:S(2)}) collective-permute-start(f32[4,8,128]{2,1,0:T(8,128)S(1)} %gather_blocks.1), channel_id=1, source_target_pairs={{0,16},{16,0},{1,17},{17,1},{2,18},{18,2},{3,19},{19,3},{4,20},{20... | collective-permute-start | bytes 49160 | tf_op jit(solution)/shard_map/ppermute | solution.py:365
  9.0 0.7 %scatter.2.refs_4_ = f32[2,8,8,512]{3,2,1,0:T(8,128)S(1)} custom-call(f32[1,8,128]{2,1,0:T(8,128)S(1)} %get-tuple-element.24.refs_0_, f32[1,8,128]{2,1,0:T(8,128)S(1)} %collective-permute-done.refs_1_, f32[9,8,128]{2,1,0:T(8,128)S(1)} %collective-permute-done.1.refs_2_.even_ref, f32[9,8,128]{2,1,0:T(8,128)S(1)} %collective-permute-done.2.refs_3_.odd_ref), custom_call_target="tpu_custom_call" | custom-call | tf_op jit(solution)/shard_map/scatter/pallas_call | solution.py:143
  9.6 0.0 copy-start.1
  9.6 0.0 copy-start.3
  9.6 0.1 collective-permute-done.3.refs_0_.refs_1_.refs_2_.refs_3_
  9.8 0.7 %scatter.3.src_ref = f32[2,8,8,512]{3,2,1,0:T(8,128)S(1)} custom-call(f32[4,8,128]{2,1,0:T(8,128)S(1)} %collective-permute-done.3.refs_0_.refs_1_.refs_2_.refs_3_, f32[4,8,128]{2,1,0:T(8,128)S(1)} %collective-permute-done.3.refs_0_.refs_1_.refs_2_.refs_3_, f32[4,8,128]{2,1,0:T(8,128)S(1)} %collective-permute-done.3.refs_0_.refs_1_.refs_2_.refs_3_, ...), custom_call_target="tpu_custom_call" | custom-call | tf_op jit(solution)/shard_map/scatter/pallas_call | solution.py:143
  10.5 0.0 collective-permute-done.5.refs_1_
  10.5 0.1 collective-permute-done.6.refs_2_
  10.6 0.0 copy-start.2
  10.6 0.4 %first_step.1 = (f32[8,8,512]{2,1,0:T(8,128)S(1)}, f32[8,8,256]{2,1,0:T(8,128)S(1)}, f32[8,8,256]{2,1,0:T(8,128)S(1)}) custom-call(f32[8,8,512]{2,1,0:T(8,128)S(1)} %copy-done, f32[8,8,512]{2,1,0:T(8,128)S(1)} %copy-done.3, f32[8,8,512]{2,1,0:T(8,128)S(1)} %copy-done.1, f32[2,8,8,512]{3,2,1,0:T(8,128)S(1)} %scatter.3.src_ref, ...), custom_call_target="tpu_custom_call" | custom-call | tf_op jit(solution)/shard_map/first_step/pallas_call | solution.py:305
  11.0 0.6 %collective-permute-start.7 = (f32[8,8,256]{2,1,0:T(8,128)S(1)}, f32[8,8,256]{2,1,0:T(8,128)S(1)}, u32[]{:S(2)}, u32[]{:S(2)}) collective-permute-start(f32[8,8,256]{2,1,0:T(8,128)S(1)} %get-tuple-element.33), channel_id=1, source_target_pairs={{0,4},{4,0},{8,12},{12,8},{1,5},{5,1},{9,13},{13,9},{2,6},{6,2},{1... | collective-permute-start | bytes 196616 | tf_op jit(solution)/shard_map/ppermute | solution.py:340
  11.6 2.4 %collective-permute-start.8 = (f32[8,8,256]{2,1,0:T(8,128)S(1)}, f32[8,8,256]{2,1,0:T(8,128)S(1)}, u32[]{:S(2)}, u32[]{:S(2)}) collective-permute-start(f32[8,8,256]{2,1,0:T(8,128)S(1)} %get-tuple-element.34), channel_id=1, source_target_pairs={{0,16},{4,8},{8,4},{12,28},{16,0},{20,24},{24,20},{28,12},{1,17},{... | collective-permute-start | bytes 196616 | tf_op jit(solution)/shard_map/ppermute | solution.py:341
  14.1 0.1 collective-permute-start.9
  14.2 0.1 collective-permute-start.10
  14.3 2.1 %collective-permute-start.11 = (f32[4,8,512]{2,1,0:T(8,128)S(1)}, f32[4,8,512]{2,1,0:T(8,128)S(1)}, u32[]{:S(2)}, u32[]{:S(2)}) collective-permute-start(f32[4,8,512]{2,1,0:T(8,128)S(1)} %get-tuple-element.42), channel_id=1, source_target_pairs={{0,16},{1,2},{2,1},{3,19},{16,0},{17,18},{18,17},{19,3},{4,20},{5,... | collective-permute-start | bytes 196616 | tf_op jit(solution)/shard_map/ppermute | solution.py:341
  16.3 0.0 collective-permute-done.7.even_ref
  16.4 1.3 %collective-permute-done.8.odd_ref = f32[8,8,256]{2,1,0:T(8,128)S(1)} collective-permute-done((f32[8,8,256]{2,1,0:T(8,128)S(1)}, f32[8,8,256]{2,1,0:T(8,128)S(1)}, u32[]{:S(2)}, u32[]{:S(2)}) %collective-permute-start.8) | collective-permute-done | bytes 65568 | tf_op jit(solution)/shard_map/ppermute | solution.py:341
  17.7 0.7 %second_start.1 = (f32[8,8,512]{2,1,0:T(8,128)}, f32[8,8,512]{2,1,0:T(8,128)S(1)}, f32[8,8,512]{2,1,0:T(8,128)S(1)}, f32[8,8,512]{2,1,0:T(8,128)S(1)}, f32[8,8,512]{2,1,0:T(8,128)S(1)}) custom-call(f32[8,8,512]{2,1,0:T(8,128)S(1)} %get-tuple-element.32.cur_ref, f32[8,8,512]{2,1,0:T(8,128)S(1)} %copy-done, f32[8,8,512]{2,1,0:T(8,128)S(1)} %copy-done.1, ...), custom_call_target="tpu_custom_call" | custom-call | tf_op jit(solution)/shard_map/second_start/pallas_call | solution.py:305
  18.4 0.0 collective-permute-done.9.refs_0_
  18.4 0.3 %collective-permute-done.10.refs_1_ = f32[4,8,512]{2,1,0:T(8,128)S(1)} collective-permute-done((f32[4,8,512]{2,1,0:T(8,128)S(1)}, f32[4,8,512]{2,1,0:T(8,128)S(1)}, u32[]{:S(2)}, u32[]{:S(2)}) %collective-permute-start.10) | collective-permute-done | bytes 65568 | tf_op jit(solution)/shard_map/ppermute | solution.py:340
  18.7 0.3 %collective-permute-done.11.refs_2_ = f32[4,8,512]{2,1,0:T(8,128)S(1)} collective-permute-done((f32[4,8,512]{2,1,0:T(8,128)S(1)}, f32[4,8,512]{2,1,0:T(8,128)S(1)}, u32[]{:S(2)}, u32[]{:S(2)}) %collective-permute-start.11) | collective-permute-done | bytes 65568 | tf_op jit(solution)/shard_map/ppermute | solution.py:341
  19.0 0.9 %second_end.1 = (f32[8,8,512]{2,1,0:T(8,128)}, f32[8,8,512]{2,1,0:T(8,128)}) custom-call(f32[8,8,512]{2,1,0:T(8,128)S(1)} %get-tuple-element.32.cur_ref, f32[8,8,512]{2,1,0:T(8,128)S(1)} %get-tuple-element.36.part_ref, f32[8,8,512]{2,1,0:T(8,128)S(1)} %get-tuple-element.37.speed_ref, f32[8,8,512]{2,1,0:T(8,128)S(1)} %get-tuple-element.38.sum_ref, ...), custom_call_target="tpu_custom_call" | custom-call | tf_op jit(solution)/shard_map/second_end/pallas_call | solution.py:305
  (9 shorter events, 0.1 us)
Async XLA Ops:
  0.6 4.5 %copy-start = (f32[8,8,512]{2,1,0:T(8,128)S(1)}, f32[8,8,512]{2,1,0:T(8,128)}, u32[]{:S(2)}) copy-start(f32[8,8,512]{2,1,0:T(8,128)} %prev_ref.3) | copy-start | bytes 393220
  1.6 6.8 %collective-permute-start.1 = (f32[9,8,128]{2,1,0:T(8,128)S(1)}, f32[9,8,128]{2,1,0:T(8,128)S(1)}, u32[]{:S(2)}, u32[]{:S(2)}) collective-permute-start(f32[9,8,128]{2,1,0:T(8,128)S(1)} %get-tuple-element.25), channel_id=1, source_target_pairs={{0,4},{4,0},{8,12},{12,8},{1,5},{5,1},{9,13},{13,9},{2,6},{6,2},{1... | collective-permute-start | bytes 110600 | tf_op jit(solution)/shard_map/ppermute | solution.py:356
  2.2 6.2 %collective-permute-start.2 = (f32[9,8,128]{2,1,0:T(8,128)S(1)}, f32[9,8,128]{2,1,0:T(8,128)S(1)}, u32[]{:S(2)}, u32[]{:S(2)}) collective-permute-start(f32[9,8,128]{2,1,0:T(8,128)S(1)} %get-tuple-element.26), channel_id=1, source_target_pairs={{0,12},{4,8},{8,4},{12,0},{1,13},{5,9},{9,5},{13,1},{2,14},{6,10},... | collective-permute-start | bytes 110600 | tf_op jit(solution)/shard_map/ppermute | solution.py:357
  4.6 3.8 %collective-permute-start = (f32[1,8,128]{2,1,0:T(8,128)S(1)}, f32[1,8,128]{2,1,0:T(8,128)S(1)}, u32[]{:S(2)}, u32[]{:S(2)}) collective-permute-start(f32[1,8,128]{2,1,0:T(8,128)S(1)} %get-tuple-element.24.refs_0_), channel_id=1, source_target_pairs={{0,8},{4,12},{8,0},{12,4},{1,9},{5,13},{9,1},{13,5},{2,10},{6,14},... | collective-permute-start | bytes 12296 | tf_op jit(solution)/shard_map/ppermute | solution.py:358
  5.1 5.3 %collective-permute-start.5 = (f32[4,8,512]{2,1,0:T(8,128)S(1)}, f32[4,8,512]{2,1,0:T(8,128)S(1)}, u32[]{:S(2)}, u32[]{:S(2)}) collective-permute-start(f32[4,8,512]{2,1,0:T(8,128)S(1)} %get-tuple-element.30), channel_id=1, source_target_pairs={{0,1},{1,0},{2,3},{3,2},{4,5},{5,4},{6,7},{7,6},{8,9},{9,8},{10,11... | collective-permute-start | bytes 196616 | tf_op jit(solution)/shard_map/ppermute | solution.py:340
  5.7 4.9 %collective-permute-start.6 = (f32[4,8,512]{2,1,0:T(8,128)S(1)}, f32[4,8,512]{2,1,0:T(8,128)S(1)}, u32[]{:S(2)}, u32[]{:S(2)}) collective-permute-start(f32[4,8,512]{2,1,0:T(8,128)S(1)} %get-tuple-element.31), channel_id=1, source_target_pairs={{0,16},{1,2},{2,1},{3,19},{16,0},{17,18},{18,17},{19,3},{4,20},{5,... | collective-permute-start | bytes 196616 | tf_op jit(solution)/shard_map/ppermute | solution.py:341
  8.4 2.2 %collective-permute-start.4 = (f32[4,8,512]{2,1,0:T(8,128)S(1)}, f32[4,8,512]{2,1,0:T(8,128)S(1)}, u32[]{:S(2)}, u32[]{:S(2)}) collective-permute-start(f32[4,8,512]{2,1,0:T(8,128)S(1)} %get-tuple-element.29), channel_id=1, source_target_pairs={{0,16},{16,0},{1,17},{17,1},{2,18},{18,2},{3,19},{19,3},{4,20},{20... | collective-permute-start | bytes 196616 | tf_op jit(solution)/shard_map/ppermute | solution.py:346
  8.5 1.3 %collective-permute-start.3 = (f32[4,8,128]{2,1,0:T(8,128)S(1)}, f32[4,8,128]{2,1,0:T(8,128)S(1)}, u32[]{:S(2)}, u32[]{:S(2)}) collective-permute-start(f32[4,8,128]{2,1,0:T(8,128)S(1)} %gather_blocks.1), channel_id=1, source_target_pairs={{0,16},{16,0},{1,17},{17,1},{2,18},{18,2},{3,19},{19,3},{4,20},{20... | collective-permute-start | bytes 49160 | tf_op jit(solution)/shard_map/ppermute | solution.py:365
  9.6 1.0 %copy-start.1 = (f32[8,8,512]{2,1,0:T(8,128)S(1)}, f32[8,8,512]{2,1,0:T(8,128)}, u32[]{:S(2)}) copy-start(f32[8,8,512]{2,1,0:T(8,128)} %vel_ref.3) | copy-start | bytes 393220
  9.6 1.0 %copy-start.3 = (f32[8,8,512]{2,1,0:T(8,128)S(1)}, f32[8,8,512]{2,1,0:T(8,128)}, u32[]{:S(2)}) copy-start(f32[8,8,512]{2,1,0:T(8,128)} %prev_ref.2) | copy-start | bytes 393220
  10.6 7.1 %copy-start.2 = (f32[2,8,8,512]{3,2,1,0:T(8,128)S(1)}, f32[2,8,8,512]{3,2,1,0:T(8,128)}, u32[]{:S(2)}) copy-start(f32[2,8,8,512]{3,2,1,0:T(8,128)} %accel_ref.1) | copy-start | bytes 786436
  11.0 5.3 %collective-permute-start.7 = (f32[8,8,256]{2,1,0:T(8,128)S(1)}, f32[8,8,256]{2,1,0:T(8,128)S(1)}, u32[]{:S(2)}, u32[]{:S(2)}) collective-permute-start(f32[8,8,256]{2,1,0:T(8,128)S(1)} %get-tuple-element.33), channel_id=1, source_target_pairs={{0,4},{4,0},{8,12},{12,8},{1,5},{5,1},{9,13},{13,9},{2,6},{6,2},{1... | collective-permute-start | bytes 196616 | tf_op jit(solution)/shard_map/ppermute | solution.py:340
  11.6 6.1 %collective-permute-start.8 = (f32[8,8,256]{2,1,0:T(8,128)S(1)}, f32[8,8,256]{2,1,0:T(8,128)S(1)}, u32[]{:S(2)}, u32[]{:S(2)}) collective-permute-start(f32[8,8,256]{2,1,0:T(8,128)S(1)} %get-tuple-element.34), channel_id=1, source_target_pairs={{0,16},{4,8},{8,4},{12,28},{16,0},{20,24},{24,20},{28,12},{1,17},{... | collective-permute-start | bytes 196616 | tf_op jit(solution)/shard_map/ppermute | solution.py:341
  14.1 4.3 %collective-permute-start.9 = (f32[4,8,512]{2,1,0:T(8,128)S(1)}, f32[4,8,512]{2,1,0:T(8,128)S(1)}, u32[]{:S(2)}, u32[]{:S(2)}) collective-permute-start(f32[4,8,512]{2,1,0:T(8,128)S(1)} %get-tuple-element.40), channel_id=1, source_target_pairs={{0,16},{16,0},{1,17},{17,1},{2,18},{18,2},{3,19},{19,3},{4,20},{20... | collective-permute-start | bytes 196616 | tf_op jit(solution)/shard_map/ppermute | solution.py:346
  14.2 4.5 %collective-permute-start.10 = (f32[4,8,512]{2,1,0:T(8,128)S(1)}, f32[4,8,512]{2,1,0:T(8,128)S(1)}, u32[]{:S(2)}, u32[]{:S(2)}) collective-permute-start(f32[4,8,512]{2,1,0:T(8,128)S(1)} %get-tuple-element.41), channel_id=1, source_target_pairs={{0,1},{1,0},{2,3},{3,2},{4,5},{5,4},{6,7},{7,6},{8,9},{9,8},{10,11... | collective-permute-start | bytes 196616 | tf_op jit(solution)/shard_map/ppermute | solution.py:340
  14.3 4.7 %collective-permute-start.11 = (f32[4,8,512]{2,1,0:T(8,128)S(1)}, f32[4,8,512]{2,1,0:T(8,128)S(1)}, u32[]{:S(2)}, u32[]{:S(2)}) collective-permute-start(f32[4,8,512]{2,1,0:T(8,128)S(1)} %get-tuple-element.42), channel_id=1, source_target_pairs={{0,16},{1,2},{2,1},{3,19},{16,0},{17,18},{18,17},{19,3},{4,20},{5,... | collective-permute-start | bytes 196616 | tf_op jit(solution)/shard_map/ppermute | solution.py:341

commit v5 on v4

--- a/solution.py
+++ b/solution.py
@@ -249,16 +249,18 @@
         yield where, centre, total
 
 
-def first_kernel(counts, cur_ref, prev_ref, vel_ref, src_ref, even_ref, odd_ref, *refs):
-    count_x, count_z, count_y = counts
+def first_start_kernel(counts, cur_ref, prev_ref, vel_ref, even_ref, odd_ref, part_ref):
+    for where, centre, laplacian in along_columns(counts[2], cur_ref, (even_ref, odd_ref)):
+        scaled = vel_ref[:, :, where] * courant_scale
+        part_ref[:, :, where] = 2.0 * centre - prev_ref[:, :, where] + scaled * scaled * laplacian
+
+
+def first_end_kernel(counts, cur_ref, vel_ref, src_ref, part_ref, *refs):
+    count_x, count_z, _ = counts
     x_refs, z_refs, (next_ref, even_out, odd_out) = refs[:count_x], refs[count_x : count_x + 2], refs[count_x + 2 :]
-    along = along_columns(count_y, cur_ref, (even_ref, odd_ref))
-    across = across_columns(count_z, cur_ref, x_refs, z_refs)
-    for (where, centre, total), (_, _, more) in zip(along, across):
+    for where, _, laplacian in across_columns(count_z, cur_ref, x_refs, z_refs):
         scaled = vel_ref[:, :, where] * courant_scale
-        next_ref[:, :, where] = (
-            2.0 * centre - prev_ref[:, :, where] + scaled * scaled * (total + more) + src_ref[0, :, :, where]
-        )
+        next_ref[:, :, where] = part_ref[:, :, where] + scaled * scaled * laplacian + src_ref[0, :, :, where]
     is_odd = lax.rem(lax.axis_index("gy"), 2) == 1
     width = even_out.shape[2]
     first, last = next_ref[:, :, 0:width], next_ref[:, :, next_ref.shape[2] - width :]
@@ -375,10 +377,16 @@
     counts = (messages_x, count_z, count_y)
     field, face = pltpu.VMEM(shape, F32), pltpu.VMEM(shape[:2] + (2 * LANES,), F32)
     whole = jax.ShapeDtypeStruct(shape, F32)
+    (part,) = call(
+        functools.partial(first_start_kernel, counts),
+        "first_start",
+        [current, adj_prev, velocity, even, odd],
+        [field],
+    )
     advanced, even_face, odd_face = call(
-        functools.partial(first_kernel, counts),
-        "first_step",
-        [current, adj_prev, velocity, source, even, odd, *along_x, *along_z],
+        functools.partial(first_end_kernel, counts),
+        "first_end",
+        [current, velocity, source, part, *along_x, *along_z],
         [field, face, face],
     )
     faces = faces_xz(advanced, messages_x)

time: 20.2 us -> 20 us (0.990)
  waiting for transfers between devices: 2.2 us -> 1.91 us
    ppermute x3, waiting for transfers between devices: 1.74 us -> 1.47 us  [swap_faces(): return lax.ppermute(face, ('gx', axis), full_swaps(count_x, size, offset))]
    pallas_call x5 -> x6, Pallas kernels: 2.01 us -> 2.19 us  [call(): pl.pallas_call(kernel, out_shape=tuple(outputs), in_specs=[VMEM] * len(op...]
  transfers between devices with their start and end apart: 12 -> 12, of which waited for: 5 -> 3; matrix products, arithmetic and copies ran while one was open for 0% -> 0% of each run, Pallas kernels for 10% -> 12%
where the time goes in v5:
time: 20 us; the launch traced here: 19.7 us
  starting transfers between devices  12.5 us (62%)
  Pallas kernels  4.41 us (22%)
  waiting for transfers between devices  1.91 us (10%)
  between operations  0.82 us (4%)
    ppermute x3, starting transfers between devices, swap_faces(): return lax.ppermute(face, ('gx', axis), full_swaps(count_x, size, offset))  7.11 us
    ppermute x1, starting transfers between devices, shards(): odd = lax.ppermute(odd_face, 'gy', xor_swaps(4, 3))  2.45 us
    pallas_call x6, Pallas kernels, call(): pl.pallas_call(kernel, out_shape=tuple(outputs), in_specs=[VMEM] * len(op...  2.19 us
    ppermute x3, waiting for transfers between devices, swap_faces(): return lax.ppermute(face, ('gx', axis), full_swaps(count_x, size, offset))  1.47 us
    pallas_call x2, Pallas kernels, scatter(): pl.pallas_call(functools.partial(scatter_kernel, picks, len(base)), out_s...  1.32 us
    ppermute x3, starting transfers between devices, swap_faces(): return lax.ppermute(face, axis, pair_swaps(size, offset))  1.19 us
    pallas_call x1, Pallas kernels, pack(): pl.pallas_call(pack_kernel, out_shape=(message, message, pltpu.VMEM((1, 8...  0.9 us
    ppermute x1, starting transfers between devices, shards(): even = lax.ppermute(even_face, 'gy', xor_swaps(4, 1))  0.6 us
  transfers between devices with their start and end apart: 12, of which 3 were waited for; matrix products, arithmetic and copies ran while one was open for 0% of the time, Pallas kernels for 12%

profile of v5, /device:TPU:10, one launch (start us, length us, event | category | flops | bytes accessed | tf_op | source)
XLA Modules:
  0.0 19.7 jit_solution(14127328156327758856)
XLA Ops:
  0.6 0.9 %pack.1 = (f32[9,8,128]{2,1,0:T(8,128)S(1)}, f32[9,8,128]{2,1,0:T(8,128)S(1)}, f32[1,8,128]{2,1,0:T(8,128)S(1)}) custom-call(f32[8,8,512]{2,1,0:T(8,128)} %prev_ref.3, f32[2,256]{1,0:T(2,128)} %res_ref.1, s32[2,128]{1,0:T(2,128)} %bitcast.2, s32[2,128]{1,0:T(2,128)} %bitcast.3), custom_call_target="tpu_custom_call" | custom-call | tf_op jit(solution)/shard_map/pack/pallas_call | solution.py:75
  1.6 0.6 %collective-permute-start.1 = (f32[9,8,128]{2,1,0:T(8,128)S(1)}, f32[9,8,128]{2,1,0:T(8,128)S(1)}, u32[]{:S(2)}, u32[]{:S(2)}) collective-permute-start(f32[9,8,128]{2,1,0:T(8,128)S(1)} %get-tuple-element.25), channel_id=1, source_target_pairs={{0,4},{4,0},{8,12},{12,8},{1,5},{5,1},{9,13},{13,9},{2,6},{6,2},{1... | collective-permute-start | bytes 110600 | tf_op jit(solution)/shard_map/ppermute | solution.py:358
  2.2 2.4 %collective-permute-start.2 = (f32[9,8,128]{2,1,0:T(8,128)S(1)}, f32[9,8,128]{2,1,0:T(8,128)S(1)}, u32[]{:S(2)}, u32[]{:S(2)}) collective-permute-start(f32[9,8,128]{2,1,0:T(8,128)S(1)} %get-tuple-element.26), channel_id=1, source_target_pairs={{0,12},{4,8},{8,4},{12,0},{1,13},{5,9},{9,5},{13,1},{2,14},{6,10},... | collective-permute-start | bytes 110600 | tf_op jit(solution)/shard_map/ppermute | solution.py:359
  4.6 0.5 %collective-permute-start = (f32[1,8,128]{2,1,0:T(8,128)S(1)}, f32[1,8,128]{2,1,0:T(8,128)S(1)}, u32[]{:S(2)}, u32[]{:S(2)}) collective-permute-start(f32[1,8,128]{2,1,0:T(8,128)S(1)} %get-tuple-element.24.refs_0_), channel_id=1, source_target_pairs={{0,8},{4,12},{8,0},{12,4},{1,9},{5,13},{9,1},{13,5},{2,10},{6,14},... | collective-permute-start | bytes 12296 | tf_op jit(solution)/shard_map/ppermute | solution.py:360
  5.1 0.5 %collective-permute-start.5 = (f32[4,8,512]{2,1,0:T(8,128)S(1)}, f32[4,8,512]{2,1,0:T(8,128)S(1)}, u32[]{:S(2)}, u32[]{:S(2)}) collective-permute-start(f32[4,8,512]{2,1,0:T(8,128)S(1)} %get-tuple-element.30), channel_id=1, source_target_pairs={{0,1},{1,0},{2,3},{3,2},{4,5},{5,4},{6,7},{7,6},{8,9},{9,8},{10,11... | collective-permute-start | bytes 196616 | tf_op jit(solution)/shard_map/ppermute | solution.py:342
  5.7 2.7 %collective-permute-start.6 = (f32[4,8,512]{2,1,0:T(8,128)S(1)}, f32[4,8,512]{2,1,0:T(8,128)S(1)}, u32[]{:S(2)}, u32[]{:S(2)}) collective-permute-start(f32[4,8,512]{2,1,0:T(8,128)S(1)} %get-tuple-element.31), channel_id=1, source_target_pairs={{0,16},{1,2},{2,1},{3,19},{16,0},{17,18},{18,17},{19,3},{4,20},{5,... | collective-permute-start | bytes 196616 | tf_op jit(solution)/shard_map/ppermute | solution.py:343
  8.4 0.0 collective-permute-done.refs_1_
  8.4 0.0 collective-permute-done.1.refs_2_.even_ref
  8.4 0.0 collective-permute-done.2.refs_3_.odd_ref
  8.4 0.0 copy-start.1
  8.4 0.0 copy-start.3
  8.4 0.1 collective-permute-start.4
  8.5 0.5 %collective-permute-start.3 = (f32[4,8,128]{2,1,0:T(8,128)S(1)}, f32[4,8,128]{2,1,0:T(8,128)S(1)}, u32[]{:S(2)}, u32[]{:S(2)}) collective-permute-start(f32[4,8,128]{2,1,0:T(8,128)S(1)} %gather_blocks.1), channel_id=1, source_target_pairs={{0,16},{16,0},{1,17},{17,1},{2,18},{18,2},{3,19},{19,3},{4,20},{20... | collective-permute-start | bytes 49160 | tf_op jit(solution)/shard_map/ppermute | solution.py:367
  9.0 0.7 %scatter.2.refs_4_ = f32[2,8,8,512]{3,2,1,0:T(8,128)S(1)} custom-call(f32[1,8,128]{2,1,0:T(8,128)S(1)} %get-tuple-element.24.refs_0_, f32[1,8,128]{2,1,0:T(8,128)S(1)} %collective-permute-done.refs_1_, f32[9,8,128]{2,1,0:T(8,128)S(1)} %collective-permute-done.1.refs_2_.even_ref, f32[9,8,128]{2,1,0:T(8,128)S(1)} %collective-permute-done.2.refs_3_.odd_ref), custom_call_target="tpu_custom_call" | custom-call | tf_op jit(solution)/shard_map/scatter/pallas_call | solution.py:143
  9.7 0.4 %first_start.1.part_ref = f32[8,8,512]{2,1,0:T(8,128)S(1)} custom-call(f32[8,8,512]{2,1,0:T(8,128)S(1)} %copy-done, f32[8,8,512]{2,1,0:T(8,128)S(1)} %copy-done.3, f32[8,8,512]{2,1,0:T(8,128)S(1)} %copy-done.1, f32[9,8,128]{2,1,0:T(8,128)S(1)} %collective-permute-done.1.refs_2_.even_ref, f32[9,8,128]{2,1,0:T(8,128)S(1)} %collective-permute-done.2.refs_3_.odd_ref), custom_call_target="tpu_custom_call" | custom-call | tf_op jit(solution)/shard_map/first_start/pallas_call | solution.py:307
  10.0 0.0 collective-permute-done.3.refs_0_.refs_1_.refs_2_.refs_3_
  10.0 0.7 %scatter.3.src_ref = f32[2,8,8,512]{3,2,1,0:T(8,128)S(1)} custom-call(f32[4,8,128]{2,1,0:T(8,128)S(1)} %collective-permute-done.3.refs_0_.refs_1_.refs_2_.refs_3_, f32[4,8,128]{2,1,0:T(8,128)S(1)} %collective-permute-done.3.refs_0_.refs_1_.refs_2_.refs_3_, f32[4,8,128]{2,1,0:T(8,128)S(1)} %collective-permute-done.3.refs_0_.refs_1_.refs_2_.refs_3_, ...), custom_call_target="tpu_custom_call" | custom-call | tf_op jit(solution)/shard_map/scatter/pallas_call | solution.py:143
  10.7 0.0 collective-permute-done.6.refs_2_
  10.7 0.0 collective-permute-done.4.refs_0_
  10.7 0.0 copy-start.2
  10.8 0.2 %first_end.1 = (f32[8,8,512]{2,1,0:T(8,128)S(1)}, f32[8,8,256]{2,1,0:T(8,128)S(1)}, f32[8,8,256]{2,1,0:T(8,128)S(1)}) custom-call(f32[8,8,512]{2,1,0:T(8,128)S(1)} %copy-done, f32[8,8,512]{2,1,0:T(8,128)S(1)} %copy-done.1, f32[2,8,8,512]{3,2,1,0:T(8,128)S(1)} %scatter.3.src_ref, f32[8,8,512]{2,1,0:T(8,128)S(1)} %first_start.1.part_ref, ...), custom_call_target="tpu_custom_call" | custom-call | tf_op jit(solution)/shard_map/first_end/pallas_call | solution.py:307
  11.0 0.6 %collective-permute-start.7 = (f32[8,8,256]{2,1,0:T(8,128)S(1)}, f32[8,8,256]{2,1,0:T(8,128)S(1)}, u32[]{:S(2)}, u32[]{:S(2)}) collective-permute-start(f32[8,8,256]{2,1,0:T(8,128)S(1)} %get-tuple-element.33), channel_id=1, source_target_pairs={{0,4},{4,0},{8,12},{12,8},{1,5},{5,1},{9,13},{13,9},{2,6},{6,2},{1... | collective-permute-start | bytes 196616 | tf_op jit(solution)/shard_map/ppermute | solution.py:342
  11.6 2.4 %collective-permute-start.8 = (f32[8,8,256]{2,1,0:T(8,128)S(1)}, f32[8,8,256]{2,1,0:T(8,128)S(1)}, u32[]{:S(2)}, u32[]{:S(2)}) collective-permute-start(f32[8,8,256]{2,1,0:T(8,128)S(1)} %get-tuple-element.34), channel_id=1, source_target_pairs={{0,16},{4,8},{8,4},{12,28},{16,0},{20,24},{24,20},{28,12},{1,17},{... | collective-permute-start | bytes 196616 | tf_op jit(solution)/shard_map/ppermute | solution.py:343
  14.1 0.1 collective-permute-start.9
  14.1 0.1 collective-permute-start.10
  14.2 2.0 %collective-permute-start.11 = (f32[4,8,512]{2,1,0:T(8,128)S(1)}, f32[4,8,512]{2,1,0:T(8,128)S(1)}, u32[]{:S(2)}, u32[]{:S(2)}) collective-permute-start(f32[4,8,512]{2,1,0:T(8,128)S(1)} %get-tuple-element.42), channel_id=1, source_target_pairs={{0,16},{1,2},{2,1},{3,19},{16,0},{17,18},{18,17},{19,3},{4,20},{5,... | collective-permute-start | bytes 196616 | tf_op jit(solution)/shard_map/ppermute | solution.py:343
  16.2 0.0 collective-permute-done.7.even_ref
  16.2 1.4 %collective-permute-done.8.odd_ref = f32[8,8,256]{2,1,0:T(8,128)S(1)} collective-permute-done((f32[8,8,256]{2,1,0:T(8,128)S(1)}, f32[8,8,256]{2,1,0:T(8,128)S(1)}, u32[]{:S(2)}, u32[]{:S(2)}) %collective-permute-start.8) | collective-permute-done | bytes 65568 | tf_op jit(solution)/shard_map/ppermute | solution.py:343
  17.5 0.7 %second_start.1 = (f32[8,8,512]{2,1,0:T(8,128)}, f32[8,8,512]{2,1,0:T(8,128)S(1)}, f32[8,8,512]{2,1,0:T(8,128)S(1)}, f32[8,8,512]{2,1,0:T(8,128)S(1)}, f32[8,8,512]{2,1,0:T(8,128)S(1)}) custom-call(f32[8,8,512]{2,1,0:T(8,128)S(1)} %get-tuple-element.32.cur_ref, f32[8,8,512]{2,1,0:T(8,128)S(1)} %copy-done, f32[8,8,512]{2,1,0:T(8,128)S(1)} %copy-done.1, ...), custom_call_target="tpu_custom_call" | custom-call | tf_op jit(solution)/shard_map/second_start/pallas_call | solution.py:307
  18.2 0.4 %collective-permute-done.10.refs_1_ = f32[4,8,512]{2,1,0:T(8,128)S(1)} collective-permute-done((f32[4,8,512]{2,1,0:T(8,128)S(1)}, f32[4,8,512]{2,1,0:T(8,128)S(1)}, u32[]{:S(2)}, u32[]{:S(2)}) %collective-permute-start.10) | collective-permute-done | bytes 65568 | tf_op jit(solution)/shard_map/ppermute | solution.py:342
  18.6 0.1 collective-permute-done.11.refs_2_
  18.8 0.9 %second_end.1 = (f32[8,8,512]{2,1,0:T(8,128)}, f32[8,8,512]{2,1,0:T(8,128)}) custom-call(f32[8,8,512]{2,1,0:T(8,128)S(1)} %get-tuple-element.32.cur_ref, f32[8,8,512]{2,1,0:T(8,128)S(1)} %get-tuple-element.36.part_ref, f32[8,8,512]{2,1,0:T(8,128)S(1)} %get-tuple-element.37.speed_ref, f32[8,8,512]{2,1,0:T(8,128)S(1)} %get-tuple-element.38.sum_ref, ...), custom_call_target="tpu_custom_call" | custom-call | tf_op jit(solution)/shard_map/second_end/pallas_call | solution.py:307
  (10 shorter events, 0.1 us)
Async XLA Ops:
  0.6 4.5 %copy-start = (f32[8,8,512]{2,1,0:T(8,128)S(1)}, f32[8,8,512]{2,1,0:T(8,128)}, u32[]{:S(2)}) copy-start(f32[8,8,512]{2,1,0:T(8,128)} %prev_ref.3) | copy-start | bytes 393220
  1.6 6.8 %collective-permute-start.1 = (f32[9,8,128]{2,1,0:T(8,128)S(1)}, f32[9,8,128]{2,1,0:T(8,128)S(1)}, u32[]{:S(2)}, u32[]{:S(2)}) collective-permute-start(f32[9,8,128]{2,1,0:T(8,128)S(1)} %get-tuple-element.25), channel_id=1, source_target_pairs={{0,4},{4,0},{8,12},{12,8},{1,5},{5,1},{9,13},{13,9},{2,6},{6,2},{1... | collective-permute-start | bytes 110600 | tf_op jit(solution)/shard_map/ppermute | solution.py:358
  2.2 6.2 %collective-permute-start.2 = (f32[9,8,128]{2,1,0:T(8,128)S(1)}, f32[9,8,128]{2,1,0:T(8,128)S(1)}, u32[]{:S(2)}, u32[]{:S(2)}) collective-permute-start(f32[9,8,128]{2,1,0:T(8,128)S(1)} %get-tuple-element.26), channel_id=1, source_target_pairs={{0,12},{4,8},{8,4},{12,0},{1,13},{5,9},{9,5},{13,1},{2,14},{6,10},... | collective-permute-start | bytes 110600 | tf_op jit(solution)/shard_map/ppermute | solution.py:359
  4.6 3.8 %collective-permute-start = (f32[1,8,128]{2,1,0:T(8,128)S(1)}, f32[1,8,128]{2,1,0:T(8,128)S(1)}, u32[]{:S(2)}, u32[]{:S(2)}) collective-permute-start(f32[1,8,128]{2,1,0:T(8,128)S(1)} %get-tuple-element.24.refs_0_), channel_id=1, source_target_pairs={{0,8},{4,12},{8,0},{12,4},{1,9},{5,13},{9,1},{13,5},{2,10},{6,14},... | collective-permute-start | bytes 12296 | tf_op jit(solution)/shard_map/ppermute | solution.py:360
  5.1 5.6 %collective-permute-start.5 = (f32[4,8,512]{2,1,0:T(8,128)S(1)}, f32[4,8,512]{2,1,0:T(8,128)S(1)}, u32[]{:S(2)}, u32[]{:S(2)}) collective-permute-start(f32[4,8,512]{2,1,0:T(8,128)S(1)} %get-tuple-element.30), channel_id=1, source_target_pairs={{0,1},{1,0},{2,3},{3,2},{4,5},{5,4},{6,7},{7,6},{8,9},{9,8},{10,11... | collective-permute-start | bytes 196616 | tf_op jit(solution)/shard_map/ppermute | solution.py:342
  5.7 5.1 %collective-permute-start.6 = (f32[4,8,512]{2,1,0:T(8,128)S(1)}, f32[4,8,512]{2,1,0:T(8,128)S(1)}, u32[]{:S(2)}, u32[]{:S(2)}) collective-permute-start(f32[4,8,512]{2,1,0:T(8,128)S(1)} %get-tuple-element.31), channel_id=1, source_target_pairs={{0,16},{1,2},{2,1},{3,19},{16,0},{17,18},{18,17},{19,3},{4,20},{5,... | collective-permute-start | bytes 196616 | tf_op jit(solution)/shard_map/ppermute | solution.py:343
  8.4 1.3 %copy-start.1 = (f32[8,8,512]{2,1,0:T(8,128)S(1)}, f32[8,8,512]{2,1,0:T(8,128)}, u32[]{:S(2)}) copy-start(f32[8,8,512]{2,1,0:T(8,128)} %vel_ref.5) | copy-start | bytes 393220
  8.4 1.3 %copy-start.3 = (f32[8,8,512]{2,1,0:T(8,128)S(1)}, f32[8,8,512]{2,1,0:T(8,128)}, u32[]{:S(2)}) copy-start(f32[8,8,512]{2,1,0:T(8,128)} %prev_ref.2) | copy-start | bytes 393220
  8.4 2.3 %collective-permute-start.4 = (f32[4,8,512]{2,1,0:T(8,128)S(1)}, f32[4,8,512]{2,1,0:T(8,128)S(1)}, u32[]{:S(2)}, u32[]{:S(2)}) collective-permute-start(f32[4,8,512]{2,1,0:T(8,128)S(1)} %get-tuple-element.29), channel_id=1, source_target_pairs={{0,16},{16,0},{1,17},{17,1},{2,18},{18,2},{3,19},{19,3},{4,20},{20... | collective-permute-start | bytes 196616 | tf_op jit(solution)/shard_map/ppermute | solution.py:348
  8.5 1.5 %collective-permute-start.3 = (f32[4,8,128]{2,1,0:T(8,128)S(1)}, f32[4,8,128]{2,1,0:T(8,128)S(1)}, u32[]{:S(2)}, u32[]{:S(2)}) collective-permute-start(f32[4,8,128]{2,1,0:T(8,128)S(1)} %gather_blocks.1), channel_id=1, source_target_pairs={{0,16},{16,0},{1,17},{17,1},{2,18},{18,2},{3,19},{19,3},{4,20},{20... | collective-permute-start | bytes 49160 | tf_op jit(solution)/shard_map/ppermute | solution.py:367
  10.7 6.8 %copy-start.2 = (f32[2,8,8,512]{3,2,1,0:T(8,128)S(1)}, f32[2,8,8,512]{3,2,1,0:T(8,128)}, u32[]{:S(2)}) copy-start(f32[2,8,8,512]{3,2,1,0:T(8,128)} %accel_ref.1) | copy-start | bytes 786436
  11.0 5.2 %collective-permute-start.7 = (f32[8,8,256]{2,1,0:T(8,128)S(1)}, f32[8,8,256]{2,1,0:T(8,128)S(1)}, u32[]{:S(2)}, u32[]{:S(2)}) collective-permute-start(f32[8,8,256]{2,1,0:T(8,128)S(1)} %get-tuple-element.33), channel_id=1, source_target_pairs={{0,4},{4,0},{8,12},{12,8},{1,5},{5,1},{9,13},{13,9},{2,6},{6,2},{1... | collective-permute-start | bytes 196616 | tf_op jit(solution)/shard_map/ppermute | solution.py:342
  11.6 6.0 %collective-permute-start.8 = (f32[8,8,256]{2,1,0:T(8,128)S(1)}, f32[8,8,256]{2,1,0:T(8,128)S(1)}, u32[]{:S(2)}, u32[]{:S(2)}) collective-permute-start(f32[8,8,256]{2,1,0:T(8,128)S(1)} %get-tuple-element.34), channel_id=1, source_target_pairs={{0,16},{4,8},{8,4},{12,28},{16,0},{20,24},{24,20},{28,12},{1,17},{... | collective-permute-start | bytes 196616 | tf_op jit(solution)/shard_map/ppermute | solution.py:343
  14.1 4.2 %collective-permute-start.9 = (f32[4,8,512]{2,1,0:T(8,128)S(1)}, f32[4,8,512]{2,1,0:T(8,128)S(1)}, u32[]{:S(2)}, u32[]{:S(2)}) collective-permute-start(f32[4,8,512]{2,1,0:T(8,128)S(1)} %get-tuple-element.40), channel_id=1, source_target_pairs={{0,16},{16,0},{1,17},{17,1},{2,18},{18,2},{3,19},{19,3},{4,20},{20... | collective-permute-start | bytes 196616 | tf_op jit(solution)/shard_map/ppermute | solution.py:348
  14.1 4.5 %collective-permute-start.10 = (f32[4,8,512]{2,1,0:T(8,128)S(1)}, f32[4,8,512]{2,1,0:T(8,128)S(1)}, u32[]{:S(2)}, u32[]{:S(2)}) collective-permute-start(f32[4,8,512]{2,1,0:T(8,128)S(1)} %get-tuple-element.41), channel_id=1, source_target_pairs={{0,1},{1,0},{2,3},{3,2},{4,5},{5,4},{6,7},{7,6},{8,9},{9,8},{10,11... | collective-permute-start | bytes 196616 | tf_op jit(solution)/shard_map/ppermute | solution.py:342
  14.2 4.5 %collective-permute-start.11 = (f32[4,8,512]{2,1,0:T(8,128)S(1)}, f32[4,8,512]{2,1,0:T(8,128)S(1)}, u32[]{:S(2)}, u32[]{:S(2)}) collective-permute-start(f32[4,8,512]{2,1,0:T(8,128)S(1)} %get-tuple-element.42), channel_id=1, source_target_pairs={{0,16},{1,2},{2,1},{3,19},{16,0},{17,18},{18,17},{19,3},{4,20},{5,... | collective-permute-start | bytes 196616 | tf_op jit(solution)/shard_map/ppermute | solution.py:343

commit v6 on v5

--- a/solution.py
+++ b/solution.py
@@ -269,9 +269,7 @@
 
 
 def second_start_kernel(counts, cur_ref, prev_ref, vel_ref, src_ref, accel_ref, even_ref, odd_ref, *refs):
-    out_ref, part_ref, speed_ref, sum_ref, factor_ref, sem = refs
-    copy = pltpu.make_async_copy(cur_ref, out_ref, sem)
-    copy.start()
+    part_ref, speed_ref, sum_ref, factor_ref = refs
     for where, centre, laplacian in along_columns(counts[2], cur_ref, (even_ref, odd_ref)):
         velocity = vel_ref[:, :, where]
         scaled = velocity * courant_scale
@@ -281,7 +279,6 @@
         weight = -2.0 / (velocity * velocity * velocity)
         sum_ref[:, :, where] = weight * accel_ref[0, :, :, where] * centre
         factor_ref[:, :, where] = weight * accel_ref[1, :, :, where]
-    copy.wait()
 
 
 def second_end_kernel(
@@ -289,8 +286,9 @@
 ):
     count_x, count_z, _ = counts
     x_refs, z_refs, refs = refs[:count_x], refs[count_x : count_x + 2], refs[count_x + 2 :]
-    next_out, gradient_out, next_ref, gradient_ref, sem = refs
-    copies = []
+    out_ref, next_out, gradient_out, next_ref, gradient_ref, sem = refs
+    copies = [pltpu.make_async_copy(cur_ref, out_ref, sem.at[sem.shape[0] - 1])]
+    copies[0].start()
     for place, (where, _, laplacian) in enumerate(across_columns(count_z, cur_ref, x_refs, z_refs)):
         advanced = part_ref[:, :, where] + speed_ref[:, :, where] * laplacian
         next_ref[place] = advanced
@@ -393,21 +391,20 @@
     along_x, along_z = halos_x(faces[2:]), halos_z(faces[:2])
     odd = swap_faces(odd_face, "gy", count_y, 1)
     even = swap_faces(even_face, "gy", count_y, 0)
-    first, *parts = call(
+    parts = call(
         functools.partial(second_start_kernel, counts),
         "second_start",
         [advanced, current, velocity, source, fwd_accel, even, odd],
-        [whole, field, field, field, field],
-        [pltpu.SemaphoreType.DMA],
+        [field, field, field, field],
     )
     blocks = shape[2] // LANES
     tiles = pltpu.VMEM((blocks,) + shape[:2] + (LANES,), F32)
-    latest, gradient = call(
+    first, latest, gradient = call(
         functools.partial(second_end_kernel, counts),
         "second_end",
         [advanced, *parts, *along_x, *along_z],
-        [whole, whole],
-        [tiles, tiles, pltpu.SemaphoreType.DMA((2 * blocks,))],
+        [whole, whole, whole],
+        [tiles, tiles, pltpu.SemaphoreType.DMA((2 * blocks + 1,))],
     )
     return first, latest, gradient
 

time: 20 us -> 20 us (level)
  waiting for transfers between devices: 1.91 us -> 2.23 us
  Pallas kernels: 4.41 us -> 4.1 us
    ppermute x3, waiting for transfers between devices: 0.42 us -> 0.75 us  [swap_faces(): return lax.ppermute(face, axis, pair_swaps(size, offset))]
    pallas_call x6, Pallas kernels: 2.19 us -> 1.87 us  [call(): pl.pallas_call(kernel, out_shape=tuple(outputs), in_specs=[VMEM] * len(op...]
  transfers between devices with their start and end apart: 12 -> 12, of which waited for: 3 -> 3; matrix products, arithmetic and copies ran while one was open for 0% -> 0% of each run, Pallas kernels for 12% -> 11%
where the time goes in v6:
time: 20 us; the launch traced here: 19.7 us
  starting transfers between devices  12.5 us (62%)
  Pallas kernels  4.1 us (20%)
  waiting for transfers between devices  2.23 us (11%)
  between operations  0.82 us (4%)
    ppermute x3, starting transfers between devices, swap_faces(): return lax.ppermute(face, ('gx', axis), full_swaps(count_x, size, offset))  7.11 us
    ppermute x1, starting transfers between devices, shards(): odd = lax.ppermute(odd_face, 'gy', xor_swaps(4, 3))  2.45 us
    pallas_call x6, Pallas kernels, call(): pl.pallas_call(kernel, out_shape=tuple(outputs), in_specs=[VMEM] * len(op...  1.87 us
    ppermute x3, waiting for transfers between devices, swap_faces(): return lax.ppermute(face, ('gx', axis), full_swaps(count_x, size, offset))  1.47 us
    pallas_call x2, Pallas kernels, scatter(): pl.pallas_call(functools.partial(scatter_kernel, picks, len(base)), out_s...  1.32 us
    ppermute x3, starting transfers between devices, swap_faces(): return lax.ppermute(face, axis, pair_swaps(size, offset))  1.19 us
    pallas_call x1, Pallas kernels, pack(): pl.pallas_call(pack_kernel, out_shape=(message, message, pltpu.VMEM((1, 8...  0.9 us
    ppermute x3, waiting for transfers between devices, swap_faces(): return lax.ppermute(face, axis, pair_swaps(size, offset))  0.75 us
  transfers between devices with their start and end apart: 12, of which 3 were waited for; matrix products, arithmetic and copies ran while one was open for 0% of the time, Pallas kernels for 11%

profile of v6, /device:TPU:10, one launch (start us, length us, event | category | flops | bytes accessed | tf_op | source)
XLA Modules:
  0.0 19.7 jit_solution(8402447634448251804)
XLA Ops:
  0.6 0.9 %pack.1 = (f32[9,8,128]{2,1,0:T(8,128)S(1)}, f32[9,8,128]{2,1,0:T(8,128)S(1)}, f32[1,8,128]{2,1,0:T(8,128)S(1)}) custom-call(f32[8,8,512]{2,1,0:T(8,128)} %prev_ref.3, f32[2,256]{1,0:T(2,128)} %res_ref.1, s32[2,128]{1,0:T(2,128)} %bitcast.2, s32[2,128]{1,0:T(2,128)} %bitcast.3), custom_call_target="tpu_custom_call" | custom-call | tf_op jit(solution)/shard_map/pack/pallas_call | solution.py:75
  1.6 0.6 %collective-permute-start.1 = (f32[9,8,128]{2,1,0:T(8,128)S(1)}, f32[9,8,128]{2,1,0:T(8,128)S(1)}, u32[]{:S(2)}, u32[]{:S(2)}) collective-permute-start(f32[9,8,128]{2,1,0:T(8,128)S(1)} %get-tuple-element.22), channel_id=1, source_target_pairs={{0,4},{4,0},{8,12},{12,8},{1,5},{5,1},{9,13},{13,9},{2,6},{6,2},{1... | collective-permute-start | bytes 110600 | tf_op jit(solution)/shard_map/ppermute | solution.py:356
  2.2 2.4 %collective-permute-start.2 = (f32[9,8,128]{2,1,0:T(8,128)S(1)}, f32[9,8,128]{2,1,0:T(8,128)S(1)}, u32[]{:S(2)}, u32[]{:S(2)}) collective-permute-start(f32[9,8,128]{2,1,0:T(8,128)S(1)} %get-tuple-element.23), channel_id=1, source_target_pairs={{0,12},{4,8},{8,4},{12,0},{1,13},{5,9},{9,5},{13,1},{2,14},{6,10},... | collective-permute-start | bytes 110600 | tf_op jit(solution)/shard_map/ppermute | solution.py:357
  4.6 0.5 %collective-permute-start = (f32[1,8,128]{2,1,0:T(8,128)S(1)}, f32[1,8,128]{2,1,0:T(8,128)S(1)}, u32[]{:S(2)}, u32[]{:S(2)}) collective-permute-start(f32[1,8,128]{2,1,0:T(8,128)S(1)} %get-tuple-element.21.refs_0_), channel_id=1, source_target_pairs={{0,8},{4,12},{8,0},{12,4},{1,9},{5,13},{9,1},{13,5},{2,10},{6,14},... | collective-permute-start | bytes 12296 | tf_op jit(solution)/shard_map/ppermute | solution.py:358
  5.1 0.5 %collective-permute-start.5 = (f32[4,8,512]{2,1,0:T(8,128)S(1)}, f32[4,8,512]{2,1,0:T(8,128)S(1)}, u32[]{:S(2)}, u32[]{:S(2)}) collective-permute-start(f32[4,8,512]{2,1,0:T(8,128)S(1)} %get-tuple-element.27), channel_id=1, source_target_pairs={{0,1},{1,0},{2,3},{3,2},{4,5},{5,4},{6,7},{7,6},{8,9},{9,8},{10,11... | collective-permute-start | bytes 196616 | tf_op jit(solution)/shard_map/ppermute | solution.py:340
  5.7 2.7 %collective-permute-start.6 = (f32[4,8,512]{2,1,0:T(8,128)S(1)}, f32[4,8,512]{2,1,0:T(8,128)S(1)}, u32[]{:S(2)}, u32[]{:S(2)}) collective-permute-start(f32[4,8,512]{2,1,0:T(8,128)S(1)} %get-tuple-element.28), channel_id=1, source_target_pairs={{0,16},{1,2},{2,1},{3,19},{16,0},{17,18},{18,17},{19,3},{4,20},{5,... | collective-permute-start | bytes 196616 | tf_op jit(solution)/shard_map/ppermute | solution.py:341
  8.4 0.0 collective-permute-done.refs_1_
  8.4 0.0 collective-permute-done.1.refs_2_.even_ref
  8.4 0.0 collective-permute-done.2.refs_3_.odd_ref
  8.4 0.0 copy-start.1
  8.4 0.0 copy-start.3
  8.4 0.1 collective-permute-start.4
  8.5 0.5 %collective-permute-start.3 = (f32[4,8,128]{2,1,0:T(8,128)S(1)}, f32[4,8,128]{2,1,0:T(8,128)S(1)}, u32[]{:S(2)}, u32[]{:S(2)}) collective-permute-start(f32[4,8,128]{2,1,0:T(8,128)S(1)} %gather_blocks.1), channel_id=1, source_target_pairs={{0,16},{16,0},{1,17},{17,1},{2,18},{18,2},{3,19},{19,3},{4,20},{20... | collective-permute-start | bytes 49160 | tf_op jit(solution)/shard_map/ppermute | solution.py:365
  9.0 0.7 %scatter.2.refs_4_ = f32[2,8,8,512]{3,2,1,0:T(8,128)S(1)} custom-call(f32[1,8,128]{2,1,0:T(8,128)S(1)} %get-tuple-element.21.refs_0_, f32[1,8,128]{2,1,0:T(8,128)S(1)} %collective-permute-done.refs_1_, f32[9,8,128]{2,1,0:T(8,128)S(1)} %collective-permute-done.1.refs_2_.even_ref, f32[9,8,128]{2,1,0:T(8,128)S(1)} %collective-permute-done.2.refs_3_.odd_ref), custom_call_target="tpu_custom_call" | custom-call | tf_op jit(solution)/shard_map/scatter/pallas_call | solution.py:143
  9.7 0.4 %first_start.1.part_ref = f32[8,8,512]{2,1,0:T(8,128)S(1)} custom-call(f32[8,8,512]{2,1,0:T(8,128)S(1)} %copy-done, f32[8,8,512]{2,1,0:T(8,128)S(1)} %copy-done.3, f32[8,8,512]{2,1,0:T(8,128)S(1)} %copy-done.1, f32[9,8,128]{2,1,0:T(8,128)S(1)} %collective-permute-done.1.refs_2_.even_ref, f32[9,8,128]{2,1,0:T(8,128)S(1)} %collective-permute-done.2.refs_3_.odd_ref), custom_call_target="tpu_custom_call" | custom-call | tf_op jit(solution)/shard_map/first_start/pallas_call | solution.py:305
  10.0 0.0 collective-permute-done.3.refs_0_.refs_1_.refs_2_.refs_3_
  10.0 0.7 %scatter.3.src_ref = f32[2,8,8,512]{3,2,1,0:T(8,128)S(1)} custom-call(f32[4,8,128]{2,1,0:T(8,128)S(1)} %collective-permute-done.3.refs_0_.refs_1_.refs_2_.refs_3_, f32[4,8,128]{2,1,0:T(8,128)S(1)} %collective-permute-done.3.refs_0_.refs_1_.refs_2_.refs_3_, f32[4,8,128]{2,1,0:T(8,128)S(1)} %collective-permute-done.3.refs_0_.refs_1_.refs_2_.refs_3_, ...), custom_call_target="tpu_custom_call" | custom-call | tf_op jit(solution)/shard_map/scatter/pallas_call | solution.py:143
  10.7 0.0 collective-permute-done.6.refs_2_
  10.7 0.0 collective-permute-done.4.refs_0_
  10.7 0.0 copy-start.2
  10.8 0.2 %first_end.1 = (f32[8,8,512]{2,1,0:T(8,128)S(1)}, f32[8,8,256]{2,1,0:T(8,128)S(1)}, f32[8,8,256]{2,1,0:T(8,128)S(1)}) custom-call(f32[8,8,512]{2,1,0:T(8,128)S(1)} %copy-done, f32[8,8,512]{2,1,0:T(8,128)S(1)} %copy-done.1, f32[2,8,8,512]{3,2,1,0:T(8,128)S(1)} %scatter.3.src_ref, f32[8,8,512]{2,1,0:T(8,128)S(1)} %first_start.1.part_ref, ...), custom_call_target="tpu_custom_call" | custom-call | tf_op jit(solution)/shard_map/first_end/pallas_call | solution.py:305
  11.0 0.6 %collective-permute-start.7 = (f32[8,8,256]{2,1,0:T(8,128)S(1)}, f32[8,8,256]{2,1,0:T(8,128)S(1)}, u32[]{:S(2)}, u32[]{:S(2)}) collective-permute-start(f32[8,8,256]{2,1,0:T(8,128)S(1)} %get-tuple-element.30), channel_id=1, source_target_pairs={{0,4},{4,0},{8,12},{12,8},{1,5},{5,1},{9,13},{13,9},{2,6},{6,2},{1... | collective-permute-start | bytes 196616 | tf_op jit(solution)/shard_map/ppermute | solution.py:340
  11.6 2.4 %collective-permute-start.8 = (f32[8,8,256]{2,1,0:T(8,128)S(1)}, f32[8,8,256]{2,1,0:T(8,128)S(1)}, u32[]{:S(2)}, u32[]{:S(2)}) collective-permute-start(f32[8,8,256]{2,1,0:T(8,128)S(1)} %get-tuple-element.31), channel_id=1, source_target_pairs={{0,16},{4,8},{8,4},{12,28},{16,0},{20,24},{24,20},{28,12},{1,17},{... | collective-permute-start | bytes 196616 | tf_op jit(solution)/shard_map/ppermute | solution.py:341
  14.1 0.1 collective-permute-start.9
  14.1 0.1 collective-permute-start.10
  14.2 2.0 %collective-permute-start.11 = (f32[4,8,512]{2,1,0:T(8,128)S(1)}, f32[4,8,512]{2,1,0:T(8,128)S(1)}, u32[]{:S(2)}, u32[]{:S(2)}) collective-permute-start(f32[4,8,512]{2,1,0:T(8,128)S(1)} %get-tuple-element.38), channel_id=1, source_target_pairs={{0,16},{1,2},{2,1},{3,19},{16,0},{17,18},{18,17},{19,3},{4,20},{5,... | collective-permute-start | bytes 196616 | tf_op jit(solution)/shard_map/ppermute | solution.py:341
  16.2 0.0 collective-permute-done.7.even_ref
  16.2 1.4 %collective-permute-done.8.odd_ref = f32[8,8,256]{2,1,0:T(8,128)S(1)} collective-permute-done((f32[8,8,256]{2,1,0:T(8,128)S(1)}, f32[8,8,256]{2,1,0:T(8,128)S(1)}, u32[]{:S(2)}, u32[]{:S(2)}) %collective-permute-start.8) | collective-permute-done | bytes 65568 | tf_op jit(solution)/shard_map/ppermute | solution.py:341
  17.5 0.4 %second_start.1 = (f32[8,8,512]{2,1,0:T(8,128)S(1)}, f32[8,8,512]{2,1,0:T(8,128)S(1)}, f32[8,8,512]{2,1,0:T(8,128)S(1)}, f32[8,8,512]{2,1,0:T(8,128)S(1)}) custom-call(f32[8,8,512]{2,1,0:T(8,128)S(1)} %get-tuple-element.29.cur_ref, f32[8,8,512]{2,1,0:T(8,128)S(1)} %copy-done, f32[8,8,512]{2,1,0:T(8,128)S(1)} %copy-done.1, ...), custom_call_target="tpu_custom_call" | custom-call | tf_op jit(solution)/shard_map/second_start/pallas_call | solution.py:305
  17.9 0.7 %collective-permute-done.10.refs_1_ = f32[4,8,512]{2,1,0:T(8,128)S(1)} collective-permute-done((f32[4,8,512]{2,1,0:T(8,128)S(1)}, f32[4,8,512]{2,1,0:T(8,128)S(1)}, u32[]{:S(2)}, u32[]{:S(2)}) %collective-permute-start.10) | collective-permute-done | bytes 65568 | tf_op jit(solution)/shard_map/ppermute | solution.py:340
  18.6 0.1 collective-permute-done.11.refs_2_
  18.8 0.9 %second_end.1 = (f32[8,8,512]{2,1,0:T(8,128)}, f32[8,8,512]{2,1,0:T(8,128)}, f32[8,8,512]{2,1,0:T(8,128)}) custom-call(f32[8,8,512]{2,1,0:T(8,128)S(1)} %get-tuple-element.29.cur_ref, f32[8,8,512]{2,1,0:T(8,128)S(1)} %get-tuple-element.32.part_ref, f32[8,8,512]{2,1,0:T(8,128)S(1)} %get-tuple-element.33.speed_ref, ...), custom_call_target="tpu_custom_call" | custom-call | tf_op jit(solution)/shard_map/second_end/pallas_call | solution.py:305
  (10 shorter events, 0.1 us)
Async XLA Ops:
  0.6 4.5 %copy-start = (f32[8,8,512]{2,1,0:T(8,128)S(1)}, f32[8,8,512]{2,1,0:T(8,128)}, u32[]{:S(2)}) copy-start(f32[8,8,512]{2,1,0:T(8,128)} %prev_ref.3) | copy-start | bytes 393220
  1.6 6.8 %collective-permute-start.1 = (f32[9,8,128]{2,1,0:T(8,128)S(1)}, f32[9,8,128]{2,1,0:T(8,128)S(1)}, u32[]{:S(2)}, u32[]{:S(2)}) collective-permute-start(f32[9,8,128]{2,1,0:T(8,128)S(1)} %get-tuple-element.22), channel_id=1, source_target_pairs={{0,4},{4,0},{8,12},{12,8},{1,5},{5,1},{9,13},{13,9},{2,6},{6,2},{1... | collective-permute-start | bytes 110600 | tf_op jit(solution)/shard_map/ppermute | solution.py:356
  2.2 6.2 %collective-permute-start.2 = (f32[9,8,128]{2,1,0:T(8,128)S(1)}, f32[9,8,128]{2,1,0:T(8,128)S(1)}, u32[]{:S(2)}, u32[]{:S(2)}) collective-permute-start(f32[9,8,128]{2,1,0:T(8,128)S(1)} %get-tuple-element.23), channel_id=1, source_target_pairs={{0,12},{4,8},{8,4},{12,0},{1,13},{5,9},{9,5},{13,1},{2,14},{6,10},... | collective-permute-start | bytes 110600 | tf_op jit(solution)/shard_map/ppermute | solution.py:357
  4.6 3.8 %collective-permute-start = (f32[1,8,128]{2,1,0:T(8,128)S(1)}, f32[1,8,128]{2,1,0:T(8,128)S(1)}, u32[]{:S(2)}, u32[]{:S(2)}) collective-permute-start(f32[1,8,128]{2,1,0:T(8,128)S(1)} %get-tuple-element.21.refs_0_), channel_id=1, source_target_pairs={{0,8},{4,12},{8,0},{12,4},{1,9},{5,13},{9,1},{13,5},{2,10},{6,14},... | collective-permute-start | bytes 12296 | tf_op jit(solution)/shard_map/ppermute | solution.py:358
  5.1 5.6 %collective-permute-start.5 = (f32[4,8,512]{2,1,0:T(8,128)S(1)}, f32[4,8,512]{2,1,0:T(8,128)S(1)}, u32[]{:S(2)}, u32[]{:S(2)}) collective-permute-start(f32[4,8,512]{2,1,0:T(8,128)S(1)} %get-tuple-element.27), channel_id=1, source_target_pairs={{0,1},{1,0},{2,3},{3,2},{4,5},{5,4},{6,7},{7,6},{8,9},{9,8},{10,11... | collective-permute-start | bytes 196616 | tf_op jit(solution)/shard_map/ppermute | solution.py:340
  5.7 5.1 %collective-permute-start.6 = (f32[4,8,512]{2,1,0:T(8,128)S(1)}, f32[4,8,512]{2,1,0:T(8,128)S(1)}, u32[]{:S(2)}, u32[]{:S(2)}) collective-permute-start(f32[4,8,512]{2,1,0:T(8,128)S(1)} %get-tuple-element.28), channel_id=1, source_target_pairs={{0,16},{1,2},{2,1},{3,19},{16,0},{17,18},{18,17},{19,3},{4,20},{5,... | collective-permute-start | bytes 196616 | tf_op jit(solution)/shard_map/ppermute | solution.py:341
  8.4 1.3 %copy-start.1 = (f32[8,8,512]{2,1,0:T(8,128)S(1)}, f32[8,8,512]{2,1,0:T(8,128)}, u32[]{:S(2)}) copy-start(f32[8,8,512]{2,1,0:T(8,128)} %vel_ref.5) | copy-start | bytes 393220
  8.4 1.3 %copy-start.3 = (f32[8,8,512]{2,1,0:T(8,128)S(1)}, f32[8,8,512]{2,1,0:T(8,128)}, u32[]{:S(2)}) copy-start(f32[8,8,512]{2,1,0:T(8,128)} %prev_ref.2) | copy-start | bytes 393220
  8.4 2.3 %collective-permute-start.4 = (f32[4,8,512]{2,1,0:T(8,128)S(1)}, f32[4,8,512]{2,1,0:T(8,128)S(1)}, u32[]{:S(2)}, u32[]{:S(2)}) collective-permute-start(f32[4,8,512]{2,1,0:T(8,128)S(1)} %get-tuple-element.26), channel_id=1, source_target_pairs={{0,16},{16,0},{1,17},{17,1},{2,18},{18,2},{3,19},{19,3},{4,20},{20... | collective-permute-start | bytes 196616 | tf_op jit(solution)/shard_map/ppermute | solution.py:346
  8.5 1.5 %collective-permute-start.3 = (f32[4,8,128]{2,1,0:T(8,128)S(1)}, f32[4,8,128]{2,1,0:T(8,128)S(1)}, u32[]{:S(2)}, u32[]{:S(2)}) collective-permute-start(f32[4,8,128]{2,1,0:T(8,128)S(1)} %gather_blocks.1), channel_id=1, source_target_pairs={{0,16},{16,0},{1,17},{17,1},{2,18},{18,2},{3,19},{19,3},{4,20},{20... | collective-permute-start | bytes 49160 | tf_op jit(solution)/shard_map/ppermute | solution.py:365
  10.7 6.8 %copy-start.2 = (f32[2,8,8,512]{3,2,1,0:T(8,128)S(1)}, f32[2,8,8,512]{3,2,1,0:T(8,128)}, u32[]{:S(2)}) copy-start(f32[2,8,8,512]{3,2,1,0:T(8,128)} %accel_ref.1) | copy-start | bytes 786436
  11.0 5.2 %collective-permute-start.7 = (f32[8,8,256]{2,1,0:T(8,128)S(1)}, f32[8,8,256]{2,1,0:T(8,128)S(1)}, u32[]{:S(2)}, u32[]{:S(2)}) collective-permute-start(f32[8,8,256]{2,1,0:T(8,128)S(1)} %get-tuple-element.30), channel_id=1, source_target_pairs={{0,4},{4,0},{8,12},{12,8},{1,5},{5,1},{9,13},{13,9},{2,6},{6,2},{1... | collective-permute-start | bytes 196616 | tf_op jit(solution)/shard_map/ppermute | solution.py:340
  11.6 6.0 %collective-permute-start.8 = (f32[8,8,256]{2,1,0:T(8,128)S(1)}, f32[8,8,256]{2,1,0:T(8,128)S(1)}, u32[]{:S(2)}, u32[]{:S(2)}) collective-permute-start(f32[8,8,256]{2,1,0:T(8,128)S(1)} %get-tuple-element.31), channel_id=1, source_target_pairs={{0,16},{4,8},{8,4},{12,28},{16,0},{20,24},{24,20},{28,12},{1,17},{... | collective-permute-start | bytes 196616 | tf_op jit(solution)/shard_map/ppermute | solution.py:341
  14.1 3.8 %collective-permute-start.9 = (f32[4,8,512]{2,1,0:T(8,128)S(1)}, f32[4,8,512]{2,1,0:T(8,128)S(1)}, u32[]{:S(2)}, u32[]{:S(2)}) collective-permute-start(f32[4,8,512]{2,1,0:T(8,128)S(1)} %get-tuple-element.36), channel_id=1, source_target_pairs={{0,16},{16,0},{1,17},{17,1},{2,18},{18,2},{3,19},{19,3},{4,20},{20... | collective-permute-start | bytes 196616 | tf_op jit(solution)/shard_map/ppermute | solution.py:346
  14.1 4.5 %collective-permute-start.10 = (f32[4,8,512]{2,1,0:T(8,128)S(1)}, f32[4,8,512]{2,1,0:T(8,128)S(1)}, u32[]{:S(2)}, u32[]{:S(2)}) collective-permute-start(f32[4,8,512]{2,1,0:T(8,128)S(1)} %get-tuple-element.37), channel_id=1, source_target_pairs={{0,1},{1,0},{2,3},{3,2},{4,5},{5,4},{6,7},{7,6},{8,9},{9,8},{10,11... | collective-permute-start | bytes 196616 | tf_op jit(solution)/shard_map/ppermute | solution.py:340
  14.2 4.5 %collective-permute-start.11 = (f32[4,8,512]{2,1,0:T(8,128)S(1)}, f32[4,8,512]{2,1,0:T(8,128)S(1)}, u32[]{:S(2)}, u32[]{:S(2)}) collective-permute-start(f32[4,8,512]{2,1,0:T(8,128)S(1)} %get-tuple-element.38), channel_id=1, source_target_pairs={{0,16},{1,2},{2,1},{3,19},{16,0},{17,18},{18,17},{19,3},{4,20},{5,... | collective-permute-start | bytes 196616 | tf_op jit(solution)/shard_map/ppermute | solution.py:341

commit v7 on v6

--- a/solution.py
+++ b/solution.py
@@ -356,6 +356,7 @@
         even = lax.ppermute(even_face, "gy", xor_swaps(4, 1))
         odd = lax.ppermute(odd_face, "gy", xor_swaps(4, 3))
         far = lax.ppermute(own, "gy", xor_swaps(4, 2))
+        current, own = lax.optimization_barrier((current, own))
         *faces_z, face_x = faces_xz(current, messages_x)
         along_z = halos_z(faces_z)
         same, picks = [own, far, even, odd], (0, 0, shape[0], shape[0])

time: 20 us -> 20 us (level)
  no operation moved by 1% of the time
where the time goes in v7:
time: 20 us; the launch traced here: 19.7 us
  starting transfers between devices  12.5 us (62%)
  Pallas kernels  4.1 us (20%)
  waiting for transfers between devices  2.23 us (11%)
  between operations  0.82 us (4%)
    ppermute x3, starting transfers between devices, swap_faces(): return lax.ppermute(face, ('gx', axis), full_swaps(count_x, size, offset))  7.11 us
    ppermute x1, starting transfers between devices, shards(): odd = lax.ppermute(odd_face, 'gy', xor_swaps(4, 3))  2.45 us
    pallas_call x6, Pallas kernels, call(): pl.pallas_call(kernel, out_shape=tuple(outputs), in_specs=[VMEM] * len(op...  1.87 us
    ppermute x3, waiting for transfers between devices, swap_faces(): return lax.ppermute(face, ('gx', axis), full_swaps(count_x, size, offset))  1.47 us
    pallas_call x2, Pallas kernels, scatter(): pl.pallas_call(functools.partial(scatter_kernel, picks, len(base)), out_s...  1.32 us
    ppermute x3, starting transfers between devices, swap_faces(): return lax.ppermute(face, axis, pair_swaps(size, offset))  1.19 us
    pallas_call x1, Pallas kernels, pack(): pl.pallas_call(pack_kernel, out_shape=(message, message, pltpu.VMEM((1, 8...  0.9 us
    ppermute x3, waiting for transfers between devices, swap_faces(): return lax.ppermute(face, axis, pair_swaps(size, offset))  0.75 us
  transfers between devices with their start and end apart: 12, of which 3 were waited for; matrix products, arithmetic and copies ran while one was open for 0% of the time, Pallas kernels for 11%

profile of v7, /device:TPU:10, one launch (start us, length us, event | category | flops | bytes accessed | tf_op | source)
XLA Modules:
  0.0 19.7 jit_solution(8402447634448251804)
XLA Ops:
  0.6 0.9 %pack.1 = (f32[9,8,128]{2,1,0:T(8,128)S(1)}, f32[9,8,128]{2,1,0:T(8,128)S(1)}, f32[1,8,128]{2,1,0:T(8,128)S(1)}) custom-call(f32[8,8,512]{2,1,0:T(8,128)} %prev_ref.2, f32[2,256]{1,0:T(2,128)} %res_ref.1, s32[2,128]{1,0:T(2,128)} %bitcast.2, s32[2,128]{1,0:T(2,128)} %bitcast.3), custom_call_target="tpu_custom_call" | custom-call | tf_op jit(solution)/shard_map/pack/pallas_call | solution.py:75
  1.6 0.6 %collective-permute-start.1 = (f32[9,8,128]{2,1,0:T(8,128)S(1)}, f32[9,8,128]{2,1,0:T(8,128)S(1)}, u32[]{:S(2)}, u32[]{:S(2)}) collective-permute-start(f32[9,8,128]{2,1,0:T(8,128)S(1)} %get-tuple-element.26), channel_id=1, source_target_pairs={{0,4},{4,0},{8,12},{12,8},{1,5},{5,1},{9,13},{13,9},{2,6},{6,2},{1... | collective-permute-start | bytes 110600 | tf_op jit(solution)/shard_map/ppermute | solution.py:356
  2.2 2.4 %collective-permute-start.2 = (f32[9,8,128]{2,1,0:T(8,128)S(1)}, f32[9,8,128]{2,1,0:T(8,128)S(1)}, u32[]{:S(2)}, u32[]{:S(2)}) collective-permute-start(f32[9,8,128]{2,1,0:T(8,128)S(1)} %get-tuple-element.27), channel_id=1, source_target_pairs={{0,12},{4,8},{8,4},{12,0},{1,13},{5,9},{9,5},{13,1},{2,14},{6,10},... | collective-permute-start | bytes 110600 | tf_op jit(solution)/shard_map/ppermute | solution.py:357
  4.6 0.5 %collective-permute-start = (f32[1,8,128]{2,1,0:T(8,128)S(1)}, f32[1,8,128]{2,1,0:T(8,128)S(1)}, u32[]{:S(2)}, u32[]{:S(2)}) collective-permute-start(f32[1,8,128]{2,1,0:T(8,128)S(1)} %get-tuple-element.25.refs_0_), channel_id=1, source_target_pairs={{0,8},{4,12},{8,0},{12,4},{1,9},{5,13},{9,1},{13,5},{2,10},{6,14},... | collective-permute-start | bytes 12296 | tf_op jit(solution)/shard_map/ppermute | solution.py:358
  5.1 0.5 %collective-permute-start.5 = (f32[4,8,512]{2,1,0:T(8,128)S(1)}, f32[4,8,512]{2,1,0:T(8,128)S(1)}, u32[]{:S(2)}, u32[]{:S(2)}) collective-permute-start(f32[4,8,512]{2,1,0:T(8,128)S(1)} %get-tuple-element.31), channel_id=1, source_target_pairs={{0,1},{1,0},{2,3},{3,2},{4,5},{5,4},{6,7},{7,6},{8,9},{9,8},{10,11... | collective-permute-start | bytes 196616 | tf_op jit(solution)/shard_map/ppermute | solution.py:340
  5.7 2.7 %collective-permute-start.6 = (f32[4,8,512]{2,1,0:T(8,128)S(1)}, f32[4,8,512]{2,1,0:T(8,128)S(1)}, u32[]{:S(2)}, u32[]{:S(2)}) collective-permute-start(f32[4,8,512]{2,1,0:T(8,128)S(1)} %get-tuple-element.32), channel_id=1, source_target_pairs={{0,16},{1,2},{2,1},{3,19},{16,0},{17,18},{18,17},{19,3},{4,20},{5,... | collective-permute-start | bytes 196616 | tf_op jit(solution)/shard_map/ppermute | solution.py:341
  8.4 0.0 collective-permute-done.refs_1_
  8.4 0.0 collective-permute-done.1.refs_2_.even_ref
  8.4 0.0 collective-permute-done.2.refs_3_.odd_ref
  8.4 0.0 copy-start.1
  8.4 0.0 copy-start.3
  8.4 0.1 collective-permute-start.4
  8.5 0.5 %collective-permute-start.3 = (f32[4,8,128]{2,1,0:T(8,128)S(1)}, f32[4,8,128]{2,1,0:T(8,128)S(1)}, u32[]{:S(2)}, u32[]{:S(2)}) collective-permute-start(f32[4,8,128]{2,1,0:T(8,128)S(1)} %gather_blocks.1), channel_id=1, source_target_pairs={{0,16},{16,0},{1,17},{17,1},{2,18},{18,2},{3,19},{19,3},{4,20},{20... | collective-permute-start | bytes 49160 | tf_op jit(solution)/shard_map/ppermute | solution.py:366
  9.0 0.7 %scatter.2.refs_4_ = f32[2,8,8,512]{3,2,1,0:T(8,128)S(1)} custom-call(f32[1,8,128]{2,1,0:T(8,128)S(1)} %get-tuple-element.25.refs_0_, f32[1,8,128]{2,1,0:T(8,128)S(1)} %collective-permute-done.refs_1_, f32[9,8,128]{2,1,0:T(8,128)S(1)} %collective-permute-done.1.refs_2_.even_ref, f32[9,8,128]{2,1,0:T(8,128)S(1)} %collective-permute-done.2.refs_3_.odd_ref), custom_call_target="tpu_custom_call" | custom-call | tf_op jit(solution)/shard_map/scatter/pallas_call | solution.py:143
  9.7 0.4 %first_start.1.part_ref = f32[8,8,512]{2,1,0:T(8,128)S(1)} custom-call(f32[8,8,512]{2,1,0:T(8,128)S(1)} %copy-done, f32[8,8,512]{2,1,0:T(8,128)S(1)} %copy-done.3, f32[8,8,512]{2,1,0:T(8,128)S(1)} %copy-done.1, f32[9,8,128]{2,1,0:T(8,128)S(1)} %collective-permute-done.1.refs_2_.even_ref, f32[9,8,128]{2,1,0:T(8,128)S(1)} %collective-permute-done.2.refs_3_.odd_ref), custom_call_target="tpu_custom_call" | custom-call | tf_op jit(solution)/shard_map/first_start/pallas_call | solution.py:305
  10.0 0.0 collective-permute-done.3.refs_0_.refs_1_.refs_2_.refs_3_
  10.0 0.7 %scatter.3.src_ref = f32[2,8,8,512]{3,2,1,0:T(8,128)S(1)} custom-call(f32[4,8,128]{2,1,0:T(8,128)S(1)} %collective-permute-done.3.refs_0_.refs_1_.refs_2_.refs_3_, f32[4,8,128]{2,1,0:T(8,128)S(1)} %collective-permute-done.3.refs_0_.refs_1_.refs_2_.refs_3_, f32[4,8,128]{2,1,0:T(8,128)S(1)} %collective-permute-done.3.refs_0_.refs_1_.refs_2_.refs_3_, ...), custom_call_target="tpu_custom_call" | custom-call | tf_op jit(solution)/shard_map/scatter/pallas_call | solution.py:143
  10.7 0.0 collective-permute-done.6.refs_2_
  10.7 0.0 collective-permute-done.4.refs_0_
  10.7 0.0 copy-start.2
  10.8 0.2 %first_end.1 = (f32[8,8,512]{2,1,0:T(8,128)S(1)}, f32[8,8,256]{2,1,0:T(8,128)S(1)}, f32[8,8,256]{2,1,0:T(8,128)S(1)}) custom-call(f32[8,8,512]{2,1,0:T(8,128)S(1)} %copy-done, f32[8,8,512]{2,1,0:T(8,128)S(1)} %copy-done.1, f32[2,8,8,512]{3,2,1,0:T(8,128)S(1)} %scatter.3.src_ref, f32[8,8,512]{2,1,0:T(8,128)S(1)} %first_start.1.part_ref, ...), custom_call_target="tpu_custom_call" | custom-call | tf_op jit(solution)/shard_map/first_end/pallas_call | solution.py:305
  11.0 0.6 %collective-permute-start.7 = (f32[8,8,256]{2,1,0:T(8,128)S(1)}, f32[8,8,256]{2,1,0:T(8,128)S(1)}, u32[]{:S(2)}, u32[]{:S(2)}) collective-permute-start(f32[8,8,256]{2,1,0:T(8,128)S(1)} %get-tuple-element.34), channel_id=1, source_target_pairs={{0,4},{4,0},{8,12},{12,8},{1,5},{5,1},{9,13},{13,9},{2,6},{6,2},{1... | collective-permute-start | bytes 196616 | tf_op jit(solution)/shard_map/ppermute | solution.py:340
  11.6 2.4 %collective-permute-start.8 = (f32[8,8,256]{2,1,0:T(8,128)S(1)}, f32[8,8,256]{2,1,0:T(8,128)S(1)}, u32[]{:S(2)}, u32[]{:S(2)}) collective-permute-start(f32[8,8,256]{2,1,0:T(8,128)S(1)} %get-tuple-element.35), channel_id=1, source_target_pairs={{0,16},{4,8},{8,4},{12,28},{16,0},{20,24},{24,20},{28,12},{1,17},{... | collective-permute-start | bytes 196616 | tf_op jit(solution)/shard_map/ppermute | solution.py:341
  14.1 0.1 collective-permute-start.9
  14.1 0.1 collective-permute-start.10
  14.2 2.0 %collective-permute-start.11 = (f32[4,8,512]{2,1,0:T(8,128)S(1)}, f32[4,8,512]{2,1,0:T(8,128)S(1)}, u32[]{:S(2)}, u32[]{:S(2)}) collective-permute-start(f32[4,8,512]{2,1,0:T(8,128)S(1)} %get-tuple-element.42), channel_id=1, source_target_pairs={{0,16},{1,2},{2,1},{3,19},{16,0},{17,18},{18,17},{19,3},{4,20},{5,... | collective-permute-start | bytes 196616 | tf_op jit(solution)/shard_map/ppermute | solution.py:341
  16.2 0.0 collective-permute-done.7.even_ref
  16.2 1.4 %collective-permute-done.8.odd_ref = f32[8,8,256]{2,1,0:T(8,128)S(1)} collective-permute-done((f32[8,8,256]{2,1,0:T(8,128)S(1)}, f32[8,8,256]{2,1,0:T(8,128)S(1)}, u32[]{:S(2)}, u32[]{:S(2)}) %collective-permute-start.8) | collective-permute-done | bytes 65568 | tf_op jit(solution)/shard_map/ppermute | solution.py:341
  17.5 0.4 %second_start.1 = (f32[8,8,512]{2,1,0:T(8,128)S(1)}, f32[8,8,512]{2,1,0:T(8,128)S(1)}, f32[8,8,512]{2,1,0:T(8,128)S(1)}, f32[8,8,512]{2,1,0:T(8,128)S(1)}) custom-call(f32[8,8,512]{2,1,0:T(8,128)S(1)} %get-tuple-element.33.cur_ref, f32[8,8,512]{2,1,0:T(8,128)S(1)} %copy-done, f32[8,8,512]{2,1,0:T(8,128)S(1)} %copy-done.1, ...), custom_call_target="tpu_custom_call" | custom-call | tf_op jit(solution)/shard_map/second_start/pallas_call | solution.py:305
  17.9 0.7 %collective-permute-done.10.refs_1_ = f32[4,8,512]{2,1,0:T(8,128)S(1)} collective-permute-done((f32[4,8,512]{2,1,0:T(8,128)S(1)}, f32[4,8,512]{2,1,0:T(8,128)S(1)}, u32[]{:S(2)}, u32[]{:S(2)}) %collective-permute-start.10) | collective-permute-done | bytes 65568 | tf_op jit(solution)/shard_map/ppermute | solution.py:340
  18.6 0.1 collective-permute-done.11.refs_2_
  18.8 0.9 %second_end.1 = (f32[8,8,512]{2,1,0:T(8,128)}, f32[8,8,512]{2,1,0:T(8,128)}, f32[8,8,512]{2,1,0:T(8,128)}) custom-call(f32[8,8,512]{2,1,0:T(8,128)S(1)} %get-tuple-element.33.cur_ref, f32[8,8,512]{2,1,0:T(8,128)S(1)} %get-tuple-element.36.part_ref, f32[8,8,512]{2,1,0:T(8,128)S(1)} %get-tuple-element.37.speed_ref, ...), custom_call_target="tpu_custom_call" | custom-call | tf_op jit(solution)/shard_map/second_end/pallas_call | solution.py:305
  (10 shorter events, 0.1 us)
Async XLA Ops:
  0.6 4.5 %copy-start = (f32[8,8,512]{2,1,0:T(8,128)S(1)}, f32[8,8,512]{2,1,0:T(8,128)}, u32[]{:S(2)}) copy-start(f32[8,8,512]{2,1,0:T(8,128)} %prev_ref.2) | copy-start | bytes 393220
  1.6 6.8 %collective-permute-start.1 = (f32[9,8,128]{2,1,0:T(8,128)S(1)}, f32[9,8,128]{2,1,0:T(8,128)S(1)}, u32[]{:S(2)}, u32[]{:S(2)}) collective-permute-start(f32[9,8,128]{2,1,0:T(8,128)S(1)} %get-tuple-element.26), channel_id=1, source_target_pairs={{0,4},{4,0},{8,12},{12,8},{1,5},{5,1},{9,13},{13,9},{2,6},{6,2},{1... | collective-permute-start | bytes 110600 | tf_op jit(solution)/shard_map/ppermute | solution.py:356
  2.2 6.2 %collective-permute-start.2 = (f32[9,8,128]{2,1,0:T(8,128)S(1)}, f32[9,8,128]{2,1,0:T(8,128)S(1)}, u32[]{:S(2)}, u32[]{:S(2)}) collective-permute-start(f32[9,8,128]{2,1,0:T(8,128)S(1)} %get-tuple-element.27), channel_id=1, source_target_pairs={{0,12},{4,8},{8,4},{12,0},{1,13},{5,9},{9,5},{13,1},{2,14},{6,10},... | collective-permute-start | bytes 110600 | tf_op jit(solution)/shard_map/ppermute | solution.py:357
  4.6 3.8 %collective-permute-start = (f32[1,8,128]{2,1,0:T(8,128)S(1)}, f32[1,8,128]{2,1,0:T(8,128)S(1)}, u32[]{:S(2)}, u32[]{:S(2)}) collective-permute-start(f32[1,8,128]{2,1,0:T(8,128)S(1)} %get-tuple-element.25.refs_0_), channel_id=1, source_target_pairs={{0,8},{4,12},{8,0},{12,4},{1,9},{5,13},{9,1},{13,5},{2,10},{6,14},... | collective-permute-start | bytes 12296 | tf_op jit(solution)/shard_map/ppermute | solution.py:358
  5.1 5.6 %collective-permute-start.5 = (f32[4,8,512]{2,1,0:T(8,128)S(1)}, f32[4,8,512]{2,1,0:T(8,128)S(1)}, u32[]{:S(2)}, u32[]{:S(2)}) collective-permute-start(f32[4,8,512]{2,1,0:T(8,128)S(1)} %get-tuple-element.31), channel_id=1, source_target_pairs={{0,1},{1,0},{2,3},{3,2},{4,5},{5,4},{6,7},{7,6},{8,9},{9,8},{10,11... | collective-permute-start | bytes 196616 | tf_op jit(solution)/shard_map/ppermute | solution.py:340
  5.7 5.1 %collective-permute-start.6 = (f32[4,8,512]{2,1,0:T(8,128)S(1)}, f32[4,8,512]{2,1,0:T(8,128)S(1)}, u32[]{:S(2)}, u32[]{:S(2)}) collective-permute-start(f32[4,8,512]{2,1,0:T(8,128)S(1)} %get-tuple-element.32), channel_id=1, source_target_pairs={{0,16},{1,2},{2,1},{3,19},{16,0},{17,18},{18,17},{19,3},{4,20},{5,... | collective-permute-start | bytes 196616 | tf_op jit(solution)/shard_map/ppermute | solution.py:341
  8.4 1.3 %copy-start.1 = (f32[8,8,512]{2,1,0:T(8,128)S(1)}, f32[8,8,512]{2,1,0:T(8,128)}, u32[]{:S(2)}) copy-start(f32[8,8,512]{2,1,0:T(8,128)} %vel_ref.5) | copy-start | bytes 393220
  8.4 1.3 %copy-start.3 = (f32[8,8,512]{2,1,0:T(8,128)S(1)}, f32[8,8,512]{2,1,0:T(8,128)}, u32[]{:S(2)}) copy-start(f32[8,8,512]{2,1,0:T(8,128)} %prev_ref.1) | copy-start | bytes 393220
  8.4 2.3 %collective-permute-start.4 = (f32[4,8,512]{2,1,0:T(8,128)S(1)}, f32[4,8,512]{2,1,0:T(8,128)S(1)}, u32[]{:S(2)}, u32[]{:S(2)}) collective-permute-start(f32[4,8,512]{2,1,0:T(8,128)S(1)} %get-tuple-element.30), channel_id=1, source_target_pairs={{0,16},{16,0},{1,17},{17,1},{2,18},{18,2},{3,19},{19,3},{4,20},{20... | collective-permute-start | bytes 196616 | tf_op jit(solution)/shard_map/ppermute | solution.py:346
  8.5 1.5 %collective-permute-start.3 = (f32[4,8,128]{2,1,0:T(8,128)S(1)}, f32[4,8,128]{2,1,0:T(8,128)S(1)}, u32[]{:S(2)}, u32[]{:S(2)}) collective-permute-start(f32[4,8,128]{2,1,0:T(8,128)S(1)} %gather_blocks.1), channel_id=1, source_target_pairs={{0,16},{16,0},{1,17},{17,1},{2,18},{18,2},{3,19},{19,3},{4,20},{20... | collective-permute-start | bytes 49160 | tf_op jit(solution)/shard_map/ppermute | solution.py:366
  10.7 6.8 %copy-start.2 = (f32[2,8,8,512]{3,2,1,0:T(8,128)S(1)}, f32[2,8,8,512]{3,2,1,0:T(8,128)}, u32[]{:S(2)}) copy-start(f32[2,8,8,512]{3,2,1,0:T(8,128)} %accel_ref.1) | copy-start | bytes 786436
  11.0 5.2 %collective-permute-start.7 = (f32[8,8,256]{2,1,0:T(8,128)S(1)}, f32[8,8,256]{2,1,0:T(8,128)S(1)}, u32[]{:S(2)}, u32[]{:S(2)}) collective-permute-start(f32[8,8,256]{2,1,0:T(8,128)S(1)} %get-tuple-element.34), channel_id=1, source_target_pairs={{0,4},{4,0},{8,12},{12,8},{1,5},{5,1},{9,13},{13,9},{2,6},{6,2},{1... | collective-permute-start | bytes 196616 | tf_op jit(solution)/shard_map/ppermute | solution.py:340
  11.6 6.0 %collective-permute-start.8 = (f32[8,8,256]{2,1,0:T(8,128)S(1)}, f32[8,8,256]{2,1,0:T(8,128)S(1)}, u32[]{:S(2)}, u32[]{:S(2)}) collective-permute-start(f32[8,8,256]{2,1,0:T(8,128)S(1)} %get-tuple-element.35), channel_id=1, source_target_pairs={{0,16},{4,8},{8,4},{12,28},{16,0},{20,24},{24,20},{28,12},{1,17},{... | collective-permute-start | bytes 196616 | tf_op jit(solution)/shard_map/ppermute | solution.py:341
  14.1 3.8 %collective-permute-start.9 = (f32[4,8,512]{2,1,0:T(8,128)S(1)}, f32[4,8,512]{2,1,0:T(8,128)S(1)}, u32[]{:S(2)}, u32[]{:S(2)}) collective-permute-start(f32[4,8,512]{2,1,0:T(8,128)S(1)} %get-tuple-element.40), channel_id=1, source_target_pairs={{0,16},{16,0},{1,17},{17,1},{2,18},{18,2},{3,19},{19,3},{4,20},{20... | collective-permute-start | bytes 196616 | tf_op jit(solution)/shard_map/ppermute | solution.py:346
  14.1 4.5 %collective-permute-start.10 = (f32[4,8,512]{2,1,0:T(8,128)S(1)}, f32[4,8,512]{2,1,0:T(8,128)S(1)}, u32[]{:S(2)}, u32[]{:S(2)}) collective-permute-start(f32[4,8,512]{2,1,0:T(8,128)S(1)} %get-tuple-element.41), channel_id=1, source_target_pairs={{0,1},{1,0},{2,3},{3,2},{4,5},{5,4},{6,7},{7,6},{8,9},{9,8},{10,11... | collective-permute-start | bytes 196616 | tf_op jit(solution)/shard_map/ppermute | solution.py:340
  14.2 4.5 %collective-permute-start.11 = (f32[4,8,512]{2,1,0:T(8,128)S(1)}, f32[4,8,512]{2,1,0:T(8,128)S(1)}, u32[]{:S(2)}, u32[]{:S(2)}) collective-permute-start(f32[4,8,512]{2,1,0:T(8,128)S(1)} %get-tuple-element.42), channel_id=1, source_target_pairs={{0,16},{1,2},{2,1},{3,19},{16,0},{17,18},{18,17},{19,3},{4,20},{5,... | collective-permute-start | bytes 196616 | tf_op jit(solution)/shard_map/ppermute | solution.py:341
